TPU v7x, 32 devices: a whole 2x2x4 slice. The times are simulated.
32 devices in a mesh: group: 2 (over x), expert: 16 (over z, y, core).
Axes of the slice: x: 2, y: 2, z: 4, core: 2. Of those that a mesh axis runs over, the one named last changes fastest.
Arguments:
- tokens: bfloat16 [16, 16, 2048], P('expert', 'group'), may hold values from -6 to 6
- out_grad: bfloat16 [16, 16, 2048], P('expert', 'group'), may hold values from -6 to 6
- gates: bfloat16 [16, 16, 8], P('expert', 'group'), may hold values from 0.049804688 to 0.34960938
- routes: int32 [16, 16, 8], P('expert', 'group'), may hold values from 0 to 31, as said below
- shard_of: int32 [2, 16], replicated, may hold values from 0 to 15, each once within a row
- w_gate: bfloat16 [2, 16, 768, 2048], P('group', 'expert'), may hold values from -0.125 to 0.125
- w_up: bfloat16 [2, 16, 768, 2048], P('group', 'expert'), may hold values from -0.125 to 0.125
- w_down: bfloat16 [2, 16, 768, 2048], P('group', 'expert'), may hold values from -0.21875 to 0.21875
Outputs:
- input_grad: bfloat16 [16, 16, 2048], P('expert', 'group')
- routing_grad: float32 [16, 16, 8], P('expert', 'group')
- gate_weight_grad: bfloat16 [2, 16, 768, 2048], P('group', 'expert')
- up_weight_grad: bfloat16 [2, 16, 768, 2048], P('group', 'expert')
- down_weight_grad: bfloat16 [2, 16, 768, 2048], P('group', 'expert')
Inputs may be any that keep to these rules, and one draw needn't show every extreme that they name: Each token names 8 different experts. Among the 16 tokens routes[p] of one position p, each expert is named at most 8 times, and one expert is named exactly 8 times at every position. `shard_of`: each row is a permutation of the device positions' shard numbers.
All inputs are finite; a program needn't handle non-finite values.
Results may differ from a plain program's by a relative error of at most 0.0058.
Values may be sent and summed in bfloat16 or wider, within the bound.
No kernel may reach another device: no remote copies, remote signals or barrier semaphores. Data moves between devices by JAX's collectives and lax.ppermute only.
A program may use at most 64 MiB of HBM per device.

v0:
```python
import jax
import jax.numpy as jnp
from jax import lax
from jax.sharding import PartitionSpec as P

EXP_GROUP = 16
CAP = 8


def expert_backward(rows_in, rows_grad, row_gates, gate_shard, up_shard, down_shard):
    contraction_dims = (((1,), (1,)), ((), ()))
    gate_pre = lax.dot_general(
        rows_in, gate_shard, contraction_dims, preferred_element_type=jnp.float32
    )
    up_pre = lax.dot_general(
        rows_in, up_shard, contraction_dims, preferred_element_type=jnp.float32
    )
    back_hidden = lax.dot_general(
        rows_grad, down_shard, contraction_dims, preferred_element_type=jnp.float32
    )
    sigmoid = jax.nn.sigmoid(gate_pre)
    swish_gate = gate_pre * sigmoid
    hidden = swish_gate * up_pre
    gate_part = jnp.sum(back_hidden * hidden, axis=1).astype(jnp.bfloat16)
    hidden_grad = row_gates[:, None] * back_hidden
    gate_grad = (hidden_grad * up_pre * sigmoid * (1.0 + gate_pre * (1.0 - sigmoid))).astype(
        jnp.bfloat16
    )
    up_grad = (hidden_grad * swish_gate).astype(jnp.bfloat16)
    input_part = (
        jnp.dot(gate_grad, gate_shard, preferred_element_type=jnp.float32)
        + jnp.dot(up_grad, up_shard, preferred_element_type=jnp.float32)
    ).astype(jnp.bfloat16)
    gate_weighted = (row_gates[:, None] * hidden).astype(jnp.bfloat16)
    return (input_part, gate_part, gate_grad, up_grad, gate_weighted)


def weight_grads(rows_in, rows_grad, gate_grad, up_grad, gate_weighted):
    contraction_dims = (((0,), (0,)), ((), ()))
    first = lax.dot_general(
        gate_grad, rows_in, contraction_dims, preferred_element_type=jnp.float32
    ).astype(jnp.bfloat16)
    second = lax.dot_general(
        up_grad, rows_in, contraction_dims, preferred_element_type=jnp.float32
    ).astype(jnp.bfloat16)
    third = lax.dot_general(
        gate_weighted, rows_grad, contraction_dims, preferred_element_type=jnp.float32
    ).astype(jnp.bfloat16)
    return (first, second, third)


def return_partials(input_part, gate_part, positions, width):
    return (
        lax.all_to_all(
            input_part.reshape(positions, CAP, width),
            "expert",
            split_axis=0,
            concat_axis=0,
            tiled=True,
        ),
        lax.all_to_all(
            gate_part.reshape(positions, CAP), "expert", split_axis=0, concat_axis=0, tiled=True
        ),
    )


def local(tokens, out_grad, gates, routes, shard_of, w_gate, w_up, w_down):
    positions = lax.axis_size("expert")
    group_now = lax.axis_index("group")
    shards = positions // EXP_GROUP
    all_in, all_grad, all_gates = (
        lax.all_gather(tokens, "group", axis=1, tiled=True),
        lax.all_gather(out_grad, "group", axis=1, tiled=True),
        lax.all_gather(gates, "group", axis=1, tiled=True),
    )
    all_ids = lax.all_gather(routes, "group", axis=1, tiled=True)
    width = tokens.shape[2]
    block_rows = all_in.shape[1]
    top_k = routes.shape[2]
    pair_total = block_rows * top_k
    bucket_total = EXP_GROUP * CAP
    local_ids = all_ids.reshape(pair_total) - group_now * EXP_GROUP
    onehot = (local_ids[:, None] == jnp.arange(EXP_GROUP, dtype=jnp.int32)[None, :]).astype(
        jnp.int32
    )
    slot_rank = jnp.sum((jnp.cumsum(onehot, axis=0) - 1) * onehot, axis=1)
    owned = (local_ids >= 0) & (local_ids < EXP_GROUP)
    target = jnp.where(owned, local_ids * CAP + slot_rank, bucket_total)
    pair_index = jnp.arange(pair_total, dtype=jnp.int32)
    slot_token = (
        jnp.full((bucket_total + 1,), block_rows, jnp.int32)
        .at[target]
        .set(pair_index // top_k)[:bucket_total]
    )
    slot_pair = (
        jnp.full((bucket_total + 1,), pair_total, jnp.int32)
        .at[target]
        .set(pair_index)[:bucket_total]
    )
    padded_in = jnp.concatenate([all_in[0], jnp.zeros((1, width), jnp.bfloat16)], axis=0)
    padded_grad = jnp.concatenate([all_grad[0], jnp.zeros((1, width), jnp.bfloat16)], axis=0)
    padded_gates = jnp.concatenate(
        [all_gates.reshape(pair_total), jnp.zeros((1,), jnp.bfloat16)], axis=0
    )
    holder_expert = lax.dynamic_slice_in_dim(shard_of, group_now, 1, 0)[0] // shards
    send_token = slot_token.reshape(EXP_GROUP, CAP)[holder_expert]
    send_pair = slot_pair.reshape(EXP_GROUP, CAP)[holder_expert]
    recv_in, recv_grad, recv_gates = (
        lax.all_to_all(padded_in[send_token], "expert", split_axis=0, concat_axis=0, tiled=True),
        lax.all_to_all(padded_grad[send_token], "expert", split_axis=0, concat_axis=0, tiled=True),
        lax.all_to_all(padded_gates[send_pair], "expert", split_axis=0, concat_axis=0, tiled=True),
    )
    rows_in = recv_in.reshape(positions * CAP, width)
    rows_grad = recv_grad.reshape(positions * CAP, width)
    row_gates = recv_gates.reshape(positions * CAP).astype(jnp.float32)
    input_part, gate_part, gate_grad, up_grad, gate_weighted = expert_backward(
        rows_in, rows_grad, row_gates, w_gate[0, 0], w_up[0, 0], w_down[0, 0]
    )
    grad_gate, grad_up, grad_down = weight_grads(
        rows_in, rows_grad, gate_grad, up_grad, gate_weighted
    )
    back_in, back_gates = return_partials(input_part, gate_part, positions, width)
    token_of_row = send_token.reshape(positions * CAP)
    pair_of_row = send_pair.reshape(positions * CAP)
    back_rows = back_in.reshape(positions * CAP, width).astype(jnp.float32)
    back_terms = back_gates.reshape(positions * CAP).astype(jnp.float32)
    block_input = (
        jnp.zeros((block_rows + 1, width), jnp.float32).at[token_of_row].add(back_rows)[:block_rows]
    )
    block_gates = (
        jnp.zeros((pair_total + 1,), jnp.float32).at[pair_of_row].add(back_terms)[:pair_total]
    )
    mine_input, mine_gates = (
        lax.psum_scatter(block_input[None], "group", scatter_dimension=1, tiled=True),
        lax.psum_scatter(
            block_gates.reshape(1, block_rows, top_k), "group", scatter_dimension=1, tiled=True
        ),
    )
    return (
        mine_input.astype(jnp.bfloat16),
        mine_gates,
        grad_gate[None, None],
        grad_up[None, None],
        grad_down[None, None],
    )


def solution(mesh):
    return jax.shard_map(
        local,
        mesh=mesh,
        in_specs=(
            P("expert", "group", None),
            P("expert", "group", None),
            P("expert", "group", None),
            P("expert", "group", None),
            P(),
            P("group", "expert", None, None),
            P("group", "expert", None, None),
            P("group", "expert", None, None),
        ),
        out_specs=(
            P("expert", "group", None),
            P("expert", "group", None),
            P("group", "expert", None, None),
            P("group", "expert", None, None),
            P("group", "expert", None, None),
        ),
        check_vma=False,
    )
```

profile of v0, /device:TPU:0, one launch (start us, length us, event | category | flops | bytes accessed | tf_op | source)
XLA Modules:
  0.0 130.5 jit_solution(9803275911103586546)
XLA Ops:
  7.2 5.5 %all_gather.12 = s32[1,16,8]{2,1,0:T(8,128)S(1)} all-gather(s32[1,8,8]{2,1,0:T(8,128)} %param.11), channel_id=1, replica_groups=mesh['group'=2,'expert'=16] {'group'}, dimensions={1}, use_global_device_ids=true | all-gather | bytes 768 | tf_op jit(solution)/shard_map/all_gather | solution.py:76
  12.8 0.7 fusion.37
  13.5 4.5 %all_gather.13 = bf16[1,16,8]{2,1,0:T(8,128)(2,1)S(1)} all-gather(bf16[1,8,8]{2,1,0:T(8,128)(2,1)} %param.10), channel_id=1, replica_groups=mesh['group'=2,'expert'=16] {'group'}, dimensions={1}, use_global_device_ids=true | all-gather | bytes 384 | tf_op jit(solution)/shard_map/all_gather | solution.py:74
  18.0 0.1 reshape.238
  18.1 0.1 mul.63
  18.2 0.1 and.25
  18.4 0.2 reduce_window_sum.11
  18.6 0.2 select_reduce_fusion
  18.8 1.0 scatter_custom_fusion.1
  19.9 0.6 gather_fusion.1
  20.7 1.2 gather_fusion.2
  22.0 0.7 all_to_all.25
  22.7 6.4 %all-to-all-start = ((bf16[16,1,8]{2,1,0:T(2,128)(2,1)}), bf16[16,1,8]{2,1,0:T(2,128)(2,1)S(1)}, u32[]{:S(2)}, u32[]{:S(2)}) async-start(bf16[16,1,8]{2,1,0:T(2,128)(2,1)} %all_to_all.25), calls=%async_computation | async-start | bytes 16384 | tf_op jit(solution)/shard_map/all_to_all | solution.py:111
  29.1 1.0 scatter_custom_fusion
  30.2 0.6 gather_fusion
  31.0 4.6 %all_gather.15 = bf16[1,16,2048]{2,1,0:T(8,128)(2,1)S(1)} all-gather(bf16[1,8,2048]{2,1,0:T(8,128)(2,1)S(1)} %copy-done.6), channel_id=1, replica_groups=mesh['group'=2,'expert'=16] {'group'}, dimensions={1}, use_global_device_ids=true | all-gather | bytes 98304 | tf_op jit(solution)/shard_map/all_gather | solution.py:72
  35.6 1.7 %gather_fusion.4 = bf16[128,2048]{1,0:T(8,128)(2,1)} fusion(bf16[17,2048]{1,0:T(8,128)(2,1)S(1)} %concatenate.11, s32[1024]{0:T(1024)S(1)} %pad_clamp_fusion), kind=kCustom, calls=%fused_computation.4 | custom fusion | bytes 1049088 | tf_op jit(solution)/shard_map/gather | solution.py:109
  37.4 6.1 %all-to-all-start.2 = ((bf16[16,8,2048]{2,1,0:T(8,128)(2,1)}), bf16[16,8,2048]{2,1,0:T(8,128)(2,1)}, u32[]{:S(2)}, u32[]{:S(2)}) async-start(bf16[16,8,2048]{2,1,0:T(8,128)(2,1)} %bitcast.90), calls=%async_computation.2 | async-start | bytes 1048576 | tf_op jit(solution)/shard_map/all_to_all | solution.py:109
  43.4 4.6 %all_gather.14 = bf16[1,16,2048]{2,1,0:T(8,128)(2,1)S(1)} all-gather(bf16[1,8,2048]{2,1,0:T(8,128)(2,1)S(1)} %copy-done.7), channel_id=1, replica_groups=mesh['group'=2,'expert'=16] {'group'}, dimensions={1}, use_global_device_ids=true | all-gather | bytes 98304 | tf_op jit(solution)/shard_map/all_gather | solution.py:73
  48.0 1.7 %gather_fusion.3 = bf16[128,2048]{1,0:T(8,128)(2,1)} fusion(bf16[17,2048]{1,0:T(8,128)(2,1)S(1)} %concatenate.10, s32[1024]{0:T(1024)S(1)} %pad_clamp_fusion), kind=kCustom, calls=%fused_computation.3 | custom fusion | bytes 1049088 | tf_op jit(solution)/shard_map/gather | solution.py:110
  49.8 8.2 %all-to-all-done.2 = bf16[16,8,2048]{2,1,0:T(8,128)(2,1)} async-done(((bf16[16,8,2048]{2,1,0:T(8,128)(2,1)}), bf16[16,8,2048]{2,1,0:T(8,128)(2,1)}, u32[]{:S(2)}, u32[]{:S(2)}) %all-to-all-start.2) | async-done | bytes 524320 | tf_op jit(solution)/shard_map/all_to_all | solution.py:109
  57.9 4.2 %all-to-all-start.1 = ((bf16[16,8,2048]{2,1,0:T(8,128)(2,1)}), bf16[16,8,2048]{2,1,0:T(8,128)(2,1)}, u32[]{:S(2)}, u32[]{:S(2)}) async-start(bf16[16,8,2048]{2,1,0:T(8,128)(2,1)} %bitcast.91), calls=%async_computation.1 | async-start | bytes 1048576 | tf_op jit(solution)/shard_map/all_to_all | solution.py:110
  62.2 0.6 reshape.245
  62.9 2.4 %fusion.2 = f32[128,768]{1,0:T(8,128)S(1)} fusion(bf16[1,1,768,2048]{3,2,1,0:T(8,128)(2,1)S(1)} %copy-done, bf16[16,8,2048]{2,1,0:T(8,128)(2,1)} %all-to-all-done.2), kind=kOutput, calls=%fused_computation.14 | convolution fusion | flops 402653184 | bytes 4063232 | tf_op jit(solution)/shard_map/dot_general | solution.py:12
  65.2 3.0 %fusion.6 = f32[128,768]{1,0:T(8,128)} fusion(bf16[1,1,768,2048]{3,2,1,0:T(8,128)(2,1)S(1)} %copy-done.1, bf16[16,8,2048]{2,1,0:T(8,128)(2,1)} %all-to-all-done.2), kind=kOutput, calls=%fused_computation.18 | convolution fusion | flops 402653184 | bytes 4063232 | tf_op jit(solution)/shard_map/dot_general | solution.py:15
  68.2 8.5 %all-to-all-done.1 = bf16[16,8,2048]{2,1,0:T(8,128)(2,1)} async-done(((bf16[16,8,2048]{2,1,0:T(8,128)(2,1)}), bf16[16,8,2048]{2,1,0:T(8,128)(2,1)}, u32[]{:S(2)}, u32[]{:S(2)}) %all-to-all-start.1) | async-done | bytes 524320 | tf_op jit(solution)/shard_map/all_to_all | solution.py:110
  76.7 4.0 %multiply_reduce_fusion = (bf16[128]{0:T(256)(128)(2,1)}, bf16[128,768]{1,0:T(8,128)(2,1)S(1)}, bf16[128,768]{1,0:T(8,128)(2,1)S(1)}) fusion(f32[128,768]{1,0:T(8,128)} %fusion.6, f32[128,768]{1,0:T(8,128)S(1)} %fusion.2, f32[128]{0:T(128)} %reshape.245, bf16[1,1,768,2048]{3,2,1,0:T(8,128)(2,1)} %param.15, bf16[16,8,2048]{2,1,0:T(8,128)(2,1)} %all-to-all-done.1), kind=kOutput, calls=%fused_computation.38 | convolution fusion | flops 404324224 | bytes 4850432 | tf_op jit(solution)/shard_map/dot_general | solution.py:18
  80.6 0.7 copy-done.4
  81.3 0.6 fusion
  81.9 0.7 copy-done.2
  82.7 1.4 %fusion.19 = bf16[16,8,2048]{2,1,0:T(8,128)(2,1)} fusion(f32[128,2048]{1,0:T(8,128)S(1)} %fusion, bf16[128,768]{1,0:T(8,128)(2,1)S(1)} %get-tuple-element.9, bf16[1,1,768,2048]{3,2,1,0:T(8,128)(2,1)S(1)} %copy-done.2), kind=kOutput, calls=%fused_computation.27 | convolution fusion | flops 403177472 | bytes 4915200 | tf_op jit(solution)/shard_map/dot_general | solution.py:32
  84.1 4.2 %all-to-all-start.3 = ((bf16[16,8,2048]{2,1,0:T(8,128)(2,1)}), bf16[16,8,2048]{2,1,0:T(8,128)(2,1)}, u32[]{:S(2)}, u32[]{:S(2)}) async-start(bf16[16,8,2048]{2,1,0:T(8,128)(2,1)} %fusion.19), calls=%async_computation.3 | async-start | bytes 1048576 | tf_op jit(solution)/shard_map/all_to_all | solution.py:54
  88.3 0.6 reshape.237
  89.0 1.2 dynamic-slice
  90.9 0.7 fusion.38
  91.6 1.4 %convert_element_type.83 = bf16[16,1,8]{2,1,0:T(2,128)(2,1)} reshape(bf16[128]{0:T(256)(128)(2,1)} %get-tuple-element.7) | data formatting | bytes 512 | tf_op jit(solution)/shard_map/convert_element_type | solution.py:24
  92.9 3.8 %fusion.11 = bf16[1,1,768,2048]{3,2,1,0:T(8,128)(2,1)} fusion(bf16[128,768]{1,0:T(8,128)(2,1)} %copy-done.5, bf16[16,8,2048]{2,1,0:T(8,128)(2,1)} %all-to-all-done.2), kind=kOutput, calls=%fused_computation.23 | convolution fusion | flops 404226048 | bytes 3866624 | tf_op jit(solution)/shard_map/dot_general | solution.py:43
  96.8 3.8 %fusion.12 = bf16[1,1,768,2048]{3,2,1,0:T(8,128)(2,1)} fusion(bf16[16,8,2048]{2,1,0:T(8,128)(2,1)} %all-to-all-done.1, f32[128]{0:T(128)S(1)} %copy-done.8, f32[128,768]{1,0:T(8,128)S(1)} %copy-done.3, f32[128,768]{1,0:T(8,128)S(1)} %fusion.2), kind=kOutput, calls=%fused_computation.24 | convolution fusion | flops 404914176 | bytes 4456960 | tf_op jit(solution)/shard_map/dot_general | solution.py:46
  100.6 2.2 %all-to-all-done.3 = bf16[16,8,2048]{2,1,0:T(8,128)(2,1)} async-done(((bf16[16,8,2048]{2,1,0:T(8,128)(2,1)}), bf16[16,8,2048]{2,1,0:T(8,128)(2,1)}, u32[]{:S(2)}, u32[]{:S(2)}) %all-to-all-start.3) | async-done | bytes 524320 | tf_op jit(solution)/shard_map/all_to_all | solution.py:54
  102.8 4.0 %all-to-all-start.4 = ((bf16[16,1,8]{2,1,0:T(2,128)(2,1)}), bf16[16,1,8]{2,1,0:T(2,128)(2,1)S(1)}, u32[]{:S(2)}, u32[]{:S(2)}) async-start(bf16[16,1,8]{2,1,0:T(2,128)(2,1)} %convert_element_type.83), calls=%async_computation.5 | async-start | bytes 16384 | tf_op jit(solution)/shard_map/all_to_all | solution.py:61
  106.8 2.8 %scatter_custom_fusion.2 = f32[17,2048]{1,0:T(8,128)S(1)} fusion(s32[128]{0:T(128)S(1)} %fusion.38, bf16[16,8,2048]{2,1,0:T(8,128)(2,1)} %all-to-all-done.3, f32[]{:T(128)} %constant.24.clone.1), kind=kCustom, calls=%fused_computation.28 | custom fusion | flops 524288 | bytes 663556 | tf_op jit(solution)/shard_map/scatter-add | solution.py:128
  109.6 0.7 slice_bitcast_fusion
  110.3 3.8 %fusion.10 = bf16[1,1,768,2048]{3,2,1,0:T(8,128)(2,1)} fusion(bf16[128,768]{1,0:T(8,128)(2,1)} %copy-done.4, bf16[16,8,2048]{2,1,0:T(8,128)(2,1)} %all-to-all-done.2), kind=kOutput, calls=%fused_computation.22 | convolution fusion | flops 404226048 | bytes 3866624 | tf_op jit(solution)/shard_map/dot_general | solution.py:40
  114.2 1.4 %scatter_custom_fusion.3 = f32[129]{0:T(256)S(1)} fusion(s32[128]{0:T(128)S(1)} %fusion.39, f32[128]{0:T(128)S(1)} %reshape.316, f32[]{:T(128)} %constant.24.clone.1), kind=kCustom, calls=%fused_computation.76 | custom fusion | flops 128 | bytes 520 | tf_op jit(solution)/shard_map/scatter-add | solution.py:131
  115.8 5.0 %all-reduce.2 = f32[1,16,8]{2,1,0:T(8,128)S(1)} all-reduce(f32[1,16,8]{2,1,0:T(8,128)S(1)} %reshape.244), channel_id=3, replica_groups=mesh['group'=2,'expert'=16] {'group'}, use_global_device_ids=true, to_apply=%region_8.9.clone | all-reduce | flops 128 | bytes 1024
  120.8 0.6 constant_dynamic-slice_fusion
  121.4 0.9 reduce-scatter.3.cloned.1.call-done
  122.2 1.5 %convert_element_type.71 = bf16[1,8,2048]{2,1,0:T(8,128)(2,1)} convert(f32[1,8,2048]{2,1,0:T(8,128)} %reduce-scatter.3.cloned.1.call-done) | non-fusion elementwise | flops 16384 | bytes 98304 | tf_op jit(solution)/shard_map/convert_element_type | solution.py:140
  (52 shorter events, 1.3 us)
Async XLA Ops:
  7.2 55.7 %copy-start = (bf16[1,1,768,2048]{3,2,1,0:T(8,128)(2,1)S(1)}, bf16[1,1,768,2048]{3,2,1,0:T(8,128)(2,1)}, u32[]{:S(2)}) copy-start(bf16[1,1,768,2048]{3,2,1,0:T(8,128)(2,1)} %param.13) | copy-start | bytes 9437188
  7.2 23.8 %copy-start.6 = (bf16[1,8,2048]{2,1,0:T(8,128)(2,1)S(1)}, bf16[1,8,2048]{2,1,0:T(8,128)(2,1)}, u32[]{:S(2)}) copy-start(bf16[1,8,2048]{2,1,0:T(8,128)(2,1)} %param.8) | copy-start | bytes 98308
  22.0 21.5 %copy-start.7 = (bf16[1,8,2048]{2,1,0:T(8,128)(2,1)S(1)}, bf16[1,8,2048]{2,1,0:T(8,128)(2,1)}, u32[]{:S(2)}) copy-start(bf16[1,8,2048]{2,1,0:T(8,128)(2,1)} %param.9) | copy-start | bytes 98308
  22.7 14.7 %all-to-all-start = ((bf16[16,1,8]{2,1,0:T(2,128)(2,1)}), bf16[16,1,8]{2,1,0:T(2,128)(2,1)S(1)}, u32[]{:S(2)}, u32[]{:S(2)}) async-start(bf16[16,1,8]{2,1,0:T(2,128)(2,1)} %all_to_all.25), calls=%async_computation | async-start | bytes 16384 | tf_op jit(solution)/shard_map/all_to_all | solution.py:111
  37.4 20.6 %all-to-all-start.2 = ((bf16[16,8,2048]{2,1,0:T(8,128)(2,1)}), bf16[16,8,2048]{2,1,0:T(8,128)(2,1)}, u32[]{:S(2)}, u32[]{:S(2)}) async-start(bf16[16,8,2048]{2,1,0:T(8,128)(2,1)} %bitcast.90), calls=%async_computation.2 | async-start | bytes 1048576 | tf_op jit(solution)/shard_map/all_to_all | solution.py:109
  57.9 18.7 %all-to-all-start.1 = ((bf16[16,8,2048]{2,1,0:T(8,128)(2,1)}), bf16[16,8,2048]{2,1,0:T(8,128)(2,1)}, u32[]{:S(2)}, u32[]{:S(2)}) async-start(bf16[16,8,2048]{2,1,0:T(8,128)(2,1)} %bitcast.91), calls=%async_computation.1 | async-start | bytes 1048576 | tf_op jit(solution)/shard_map/all_to_all | solution.py:110
  62.9 2.4 %copy-start.1 = (bf16[1,1,768,2048]{3,2,1,0:T(8,128)(2,1)S(1)}, bf16[1,1,768,2048]{3,2,1,0:T(8,128)(2,1)}, u32[]{:S(2)}) copy-start(bf16[1,1,768,2048]{3,2,1,0:T(8,128)(2,1)} %param.14) | copy-start | bytes 9437188
  80.6 0.7 copy-start.4
  80.6 1.3 copy-start.5
  80.6 2.0 %copy-start.2 = (bf16[1,1,768,2048]{3,2,1,0:T(8,128)(2,1)S(1)}, bf16[1,1,768,2048]{3,2,1,0:T(8,128)(2,1)}, u32[]{:S(2)}) copy-start(bf16[1,1,768,2048]{3,2,1,0:T(8,128)(2,1)} %param.14) | copy-start | bytes 9437188
  84.1 18.7 %all-to-all-start.3 = ((bf16[16,8,2048]{2,1,0:T(8,128)(2,1)}), bf16[16,8,2048]{2,1,0:T(8,128)(2,1)}, u32[]{:S(2)}, u32[]{:S(2)}) async-start(bf16[16,8,2048]{2,1,0:T(8,128)(2,1)} %fusion.19), calls=%async_computation.3 | async-start | bytes 1048576 | tf_op jit(solution)/shard_map/all_to_all | solution.py:54
  88.9 7.9 %copy-start.8 = (f32[128]{0:T(128)S(1)}, f32[128]{0:T(128)}, u32[]{:S(2)}) copy-start(f32[128]{0:T(128)} %reshape.245) | copy-start | bytes 1540
  92.9 3.9 %copy-start.3 = (f32[128,768]{1,0:T(8,128)S(1)}, f32[128,768]{1,0:T(8,128)}, u32[]{:S(2)}) copy-start(f32[128,768]{1,0:T(8,128)} %fusion.6) | copy-start | bytes 1179652
  102.8 11.4 %all-to-all-start.4 = ((bf16[16,1,8]{2,1,0:T(2,128)(2,1)}), bf16[16,1,8]{2,1,0:T(2,128)(2,1)S(1)}, u32[]{:S(2)}, u32[]{:S(2)}) async-start(bf16[16,1,8]{2,1,0:T(2,128)(2,1)} %convert_element_type.83), calls=%async_computation.5 | async-start | bytes 16384 | tf_op jit(solution)/shard_map/all_to_all | solution.py:61
  106.8 15.4 %reduce-scatter.3.cloned.1.call-start = ((), (), s32[]{:S(2)}) async-start(), calls=%async_computation.6 | async-start | bytes 196608 | tf_op jit(solution)/shard_map/reduce_scatter | solution.py:134
Sparse Core Ops, SparseCore 0:
  110.4 11.7 reduce-scatter.2
where the time goes:
time: 131 us
  starting transfers between devices  25 us (19%)
  blocking collectives  24.2 us (18%)
  matrix products  22.8 us (17%)
  waiting for transfers between devices  19.7 us (15%)
  local copies, waits for them, and re-layouts  16.3 us (12%)
  between operations  15 us (11%)
  other arithmetic  7.56 us (6%)
    all_to_all x1, waiting for transfers between devices, local(): lax.all_to_all(padded_grad[send_token], 'expert', split_axis=0, concat_ax...  8.46 us
    all_to_all x1, waiting for transfers between devices, local(): lax.all_to_all(padded_in[send_token], 'expert', split_axis=0, concat_axis...  8.18 us
    all_to_all x1, starting transfers between devices, local(): lax.all_to_all(padded_gates[send_pair], 'expert', split_axis=0, concat_ax...  6.43 us
    all_to_all x1, starting transfers between devices, local(): lax.all_to_all(padded_in[send_token], 'expert', split_axis=0, concat_axis...  6.06 us
    all_gather x1, blocking collectives, local(): all_ids = lax.all_gather(routes, 'group', axis=1, tiled=True)  5.53 us
    unnamed x1, blocking collectives  5 us
    all_gather x1, blocking collectives, local(): lax.all_gather(tokens, 'group', axis=1, tiled=True)  4.59 us
    all_gather x1, blocking collectives, local(): lax.all_gather(out_grad, 'group', axis=1, tiled=True)  4.59 us
  transfers between devices with their start and end apart: 6, of which 4 were waited for; matrix products, arithmetic and copies ran while one was open for 25% of the time, Pallas kernels for 0%

commit v1 on v0

v1 whole, which is shorter than its diff:
```python
import functools

import jax
import jax.numpy as jnp
from jax import lax
from jax.experimental import pallas as pl
from jax.experimental.pallas import tpu as pltpu
from jax.sharding import Mesh
from jax.sharding import PartitionSpec as P

EXP_GROUP = 16
CAP = 8
LANES = 128
F32 = jnp.float32
BF16 = jnp.bfloat16
VMEM_LIMIT = 56 * 1024 * 1024


def expert_backward(rows_in, rows_grad, row_gates, gate_shard, up_shard, down_shard):
    contraction_dims = (((1,), (1,)), ((), ()))
    gate_pre = lax.dot_general(rows_in, gate_shard, contraction_dims, preferred_element_type=F32)
    up_pre = lax.dot_general(rows_in, up_shard, contraction_dims, preferred_element_type=F32)
    back_hidden = lax.dot_general(
        rows_grad, down_shard, contraction_dims, preferred_element_type=F32
    )
    sigmoid = jax.nn.sigmoid(gate_pre)
    swish_gate = gate_pre * sigmoid
    hidden = swish_gate * up_pre
    gate_part = jnp.sum(back_hidden * hidden, axis=1).astype(BF16)
    hidden_grad = row_gates[:, None] * back_hidden
    gate_grad = (hidden_grad * up_pre * sigmoid * (1.0 + gate_pre * (1.0 - sigmoid))).astype(BF16)
    up_grad = (hidden_grad * swish_gate).astype(BF16)
    input_part = (
        jnp.dot(gate_grad, gate_shard, preferred_element_type=F32)
        + jnp.dot(up_grad, up_shard, preferred_element_type=F32)
    ).astype(BF16)
    gate_weighted = (row_gates[:, None] * hidden).astype(BF16)
    return (input_part, gate_part, gate_grad, up_grad, gate_weighted)


def weight_grads(rows_in, rows_grad, gate_grad, up_grad, gate_weighted):
    contraction_dims = (((0,), (0,)), ((), ()))

    def one(a, b):
        return lax.dot_general(a, b, contraction_dims, preferred_element_type=F32).astype(BF16)

    return one(gate_grad, rows_in), one(up_grad, rows_in), one(gate_weighted, rows_grad)


def exchange(x):
    return lax.all_to_all(x, "expert", split_axis=0, concat_axis=0, tiled=True)


def general_local(tokens, out_grad, gates, routes, shard_of, w_gate, w_up, w_down):
    positions = lax.axis_size("expert")
    group_now = lax.axis_index("group")
    shards = positions // EXP_GROUP
    gather = functools.partial(lax.all_gather, axis_name="group", axis=1, tiled=True)
    all_in, all_grad, all_gates, all_ids = (
        gather(tokens),
        gather(out_grad),
        gather(gates),
        gather(routes),
    )
    width = tokens.shape[2]
    block_rows = all_in.shape[1]
    top_k = routes.shape[2]
    pair_total = block_rows * top_k
    bucket_total = EXP_GROUP * CAP
    local_ids = all_ids.reshape(pair_total) - group_now * EXP_GROUP
    onehot = (local_ids[:, None] == jnp.arange(EXP_GROUP, dtype=jnp.int32)[None, :]).astype(
        jnp.int32
    )
    slot_rank = jnp.sum((jnp.cumsum(onehot, axis=0) - 1) * onehot, axis=1)
    owned = (local_ids >= 0) & (local_ids < EXP_GROUP)
    target = jnp.where(owned, local_ids * CAP + slot_rank, bucket_total)
    pair_index = jnp.arange(pair_total, dtype=jnp.int32)
    slot_token = (
        jnp.full((bucket_total + 1,), block_rows, jnp.int32)
        .at[target]
        .set(pair_index // top_k)[:bucket_total]
    )
    slot_pair = (
        jnp.full((bucket_total + 1,), pair_total, jnp.int32)
        .at[target]
        .set(pair_index)[:bucket_total]
    )
    padded_in = jnp.concatenate([all_in[0], jnp.zeros((1, width), BF16)], axis=0)
    padded_grad = jnp.concatenate([all_grad[0], jnp.zeros((1, width), BF16)], axis=0)
    padded_gates = jnp.concatenate([all_gates.reshape(pair_total), jnp.zeros((1,), BF16)], axis=0)
    holder_expert = lax.dynamic_slice_in_dim(shard_of, group_now, 1, 0)[0] // shards
    send_token = slot_token.reshape(EXP_GROUP, CAP)[holder_expert]
    send_pair = slot_pair.reshape(EXP_GROUP, CAP)[holder_expert]
    rows_in = exchange(padded_in[send_token]).reshape(positions * CAP, width)
    rows_grad = exchange(padded_grad[send_token]).reshape(positions * CAP, width)
    row_gates = exchange(padded_gates[send_pair]).reshape(positions * CAP).astype(F32)
    input_part, gate_part, gate_grad, up_grad, gate_weighted = expert_backward(
        rows_in, rows_grad, row_gates, w_gate[0, 0], w_up[0, 0], w_down[0, 0]
    )
    grad_gate, grad_up, grad_down = weight_grads(
        rows_in, rows_grad, gate_grad, up_grad, gate_weighted
    )
    back_in = exchange(input_part.reshape(positions, CAP, width))
    back_gates = exchange(gate_part.reshape(positions, CAP))
    token_of_row = send_token.reshape(positions * CAP)
    pair_of_row = send_pair.reshape(positions * CAP)
    back_rows = back_in.reshape(positions * CAP, width).astype(F32)
    back_terms = back_gates.reshape(positions * CAP).astype(F32)
    block_input = (
        jnp.zeros((block_rows + 1, width), F32).at[token_of_row].add(back_rows)[:block_rows]
    )
    block_gates = jnp.zeros((pair_total + 1,), F32).at[pair_of_row].add(back_terms)[:pair_total]
    scatter = functools.partial(
        lax.psum_scatter, axis_name="group", scatter_dimension=1, tiled=True
    )
    mine_input = scatter(block_input[None])
    mine_gates = scatter(block_gates.reshape(1, block_rows, top_k))
    return (
        mine_input.astype(BF16),
        mine_gates,
        grad_gate[None, None],
        grad_up[None, None],
        grad_down[None, None],
    )


def build_message(tok_ref, grad_ref, gates_ref, routes_ref, out_ref):
    width = tok_ref.shape[1]
    out_ref[:, :width] = tok_ref[...]
    out_ref[:, width : 2 * width] = grad_ref[...]
    rows, top_k = routes_ref.shape
    lane = lax.broadcasted_iota(jnp.int32, (rows, LANES), 1)
    routes = routes_ref[...]
    gates = gates_ref[...].astype(F32)
    dense = jnp.zeros((rows, LANES), F32)
    for k in range(top_k):
        chosen = routes[:, k : k + 1]
        dense = jnp.where(lane == chosen, gates[:, k : k + 1], dense)
        dense = jnp.where(lane == chosen + LANES // 2, 1.0, dense)
    out_ref[:, 2 * width :] = dense.astype(BF16)


def dot_tt(a, b, da, db):
    return lax.dot_general(a, b, (((da,), (db,)), ((), ())), preferred_element_type=F32)


def expert_kernel(
    which_ref, near_ref, far_ref, wg_ref, wu_ref, wd_ref,
    ret_near_ref, ret_far_ref, rin_ref, rgrad_ref, gg_ref, ug_ref, gw_ref,
):
    which = which_ref[0]
    half, full = near_ref.shape
    width = rin_ref.shape[1]
    slots = rin_ref.shape[0]
    total = 2 * half
    lane = lax.broadcasted_iota(jnp.int32, (8, LANES), 1)
    pick_gate = jnp.where(lane == which, 1.0, 0.0).astype(BF16)
    pick_mask = jnp.where(lane == which + LANES // 2, 1.0, 0.0).astype(BF16)
    extra = jnp.concatenate([near_ref[:, 2 * width :], far_ref[:, 2 * width :]], axis=0)
    gate_row = dot_tt(pick_gate, extra, 1, 1)
    mask_row = dot_tt(pick_mask, extra, 1, 1)
    before = (
        lax.broadcasted_iota(jnp.int32, (total, total), 0)
        < lax.broadcasted_iota(jnp.int32, (total, total), 1)
    )
    before = jnp.where(before, 1.0, 0.0).astype(BF16)
    rank_row = dot_tt(mask_row.astype(BF16), before, 1, 0)
    slot = lax.broadcasted_iota(jnp.int32, (slots, total), 0)
    hit = (slot == rank_row[:1].astype(jnp.int32)) & (mask_row[:1] > 0.5)
    select_f = jnp.where(hit, 1.0, 0.0)
    select = select_f.astype(BF16)
    row_gates = jnp.sum(select_f * gate_row[:1], axis=1, keepdims=True)
    s_near, s_far = select[:, :half], select[:, half:]

    def rows_of(lo):
        cols = slice(lo, lo + width)
        return (
            dot_tt(s_near, near_ref[:, cols], 1, 0) + dot_tt(s_far, far_ref[:, cols], 1, 0)
        ).astype(BF16)

    rows_in = rows_of(0)
    rin_ref[...] = rows_in
    rows_grad = rows_of(width)
    rgrad_ref[...] = rows_grad
    gate_pre = dot_tt(rows_in, wg_ref[...], 1, 1)
    up_pre = dot_tt(rows_in, wu_ref[...], 1, 1)
    back = dot_tt(rows_grad, wd_ref[...], 1, 1)
    sigmoid = jax.nn.sigmoid(gate_pre)
    swish_gate = gate_pre * sigmoid
    hidden = swish_gate * up_pre
    gate_part = jnp.sum(back * hidden, axis=1, keepdims=True)
    hidden_grad = row_gates * back
    gate_grad = (hidden_grad * up_pre * sigmoid * (1.0 + gate_pre * (1.0 - sigmoid))).astype(BF16)
    up_grad = (hidden_grad * swish_gate).astype(BF16)
    gg_ref[...] = gate_grad
    ug_ref[...] = up_grad
    gw_ref[...] = (row_gates * hidden).astype(BF16)
    input_part = (
        dot_tt(gate_grad, wg_ref[...], 1, 0) + dot_tt(up_grad, wu_ref[...], 1, 0)
    ).astype(BF16)
    gate_lane = lax.broadcasted_iota(jnp.int32, (slots, LANES), 1)
    gate_cols = jnp.where(gate_lane == which, gate_part, 0.0).astype(BF16)
    for s, ref in ((s_near, ret_near_ref), (s_far, ret_far_ref)):
        ref[:, :width] = dot_tt(s, input_part, 0, 0).astype(BF16)
        ref[:, width:] = dot_tt(s, gate_cols, 0, 0).astype(BF16)


def weight_kernel(a_ref, b_ref, out_ref):
    out_ref[...] = dot_tt(a_ref[...], b_ref[...], 0, 0).astype(BF16)


def weight_grad(a, b, tile):
    rows, hidden = a.shape
    width = b.shape[1]
    return pl.pallas_call(
        weight_kernel,
        grid=(hidden // tile,),
        in_specs=[
            pl.BlockSpec((rows, tile), lambda i: (0, i)),
            pl.BlockSpec((rows, width), lambda i: (0, 0)),
        ],
        out_specs=pl.BlockSpec((tile, width), lambda i: (i, 0)),
        out_shape=jax.ShapeDtypeStruct((hidden, width), BF16),
        name="weight_grad",
    )(a, b)


def final_kernel(a_ref, b_ref, c_ref, d_ref, routes_ref, in_ref, gate_ref):
    total = (
        a_ref[...].astype(F32) + b_ref[...].astype(F32) + c_ref[...].astype(F32)
        + d_ref[...].astype(F32)
    )
    width = in_ref.shape[1]
    in_ref[...] = total[:, :width].astype(BF16)
    dense = total[:, width:]
    rows, top_k = routes_ref.shape
    routes = routes_ref[...]
    lane = lax.broadcasted_iota(jnp.int32, dense.shape, 1)
    place = lax.broadcasted_iota(jnp.int32, (rows, top_k), 1)
    out = jnp.zeros((rows, top_k), F32)
    for k in range(top_k):
        value = jnp.sum(jnp.where(lane == routes[:, k : k + 1], dense, 0.0), axis=1, keepdims=True)
        out = jnp.where(place == k, value, out)
    gate_ref[...] = out


def whole(memory=pltpu.VMEM):
    return pl.BlockSpec(memory_space=memory)


def swap(x, axes, bits):
    sizes = 1
    for a in axes:
        sizes *= lax.axis_size(a)
    return lax.ppermute(x, axes, [(i, i ^ bits) for i in range(sizes)])


def spread(x, axes):
    count = 1
    for a in axes:
        count *= lax.axis_size(a)
    return [x] + [swap(x, axes, k) for k in range(1, count)]


def block_local(tokens, out_grad, gates, routes, shard_of, w_gate, w_up, w_down):
    group_now = lax.axis_index("x")
    width = tokens.shape[2]
    rows = tokens.shape[1]
    hidden = w_gate.shape[2]
    top_k = routes.shape[2]
    full = 2 * width + LANES
    back_width = width + LANES
    message = pl.pallas_call(
        build_message,
        in_specs=[whole()] * 4,
        out_specs=whole(),
        out_shape=jax.ShapeDtypeStruct((rows, full), BF16),
        name="build_message",
    )(tokens[0], out_grad[0], gates[0], routes[0])
    line = jnp.concatenate(spread(message, ("z",)), axis=0)
    near = jnp.concatenate(spread(line, ("x", "y")), axis=0)
    far = swap(near, ("core",), 1)
    place = (lax.axis_index("z") * 2 + lax.axis_index("y")) * 2 + lax.axis_index("core")
    which = (shard_of[group_now, place] + group_now * EXP_GROUP).astype(jnp.int32).reshape(1)
    half = near.shape[0]
    slots = lax.axis_size("z") * lax.axis_size("y") * lax.axis_size("core") * CAP
    ret_near, ret_far, rows_in, rows_grad, gate_grad, up_grad, weighted = pl.pallas_call(
        expert_kernel,
        in_specs=[whole(pltpu.SMEM)] + [whole()] * 5,
        out_specs=[whole()] * 7,
        out_shape=[
            jax.ShapeDtypeStruct((half, back_width), BF16),
            jax.ShapeDtypeStruct((half, back_width), BF16),
            jax.ShapeDtypeStruct((slots, width), BF16),
            jax.ShapeDtypeStruct((slots, width), BF16),
            jax.ShapeDtypeStruct((slots, hidden), BF16),
            jax.ShapeDtypeStruct((slots, hidden), BF16),
            jax.ShapeDtypeStruct((slots, hidden), BF16),
        ],
        compiler_params=pltpu.CompilerParams(vmem_limit_bytes=VMEM_LIMIT),
        name="expert",
    )(which, near, far, w_gate[0, 0], w_up[0, 0], w_down[0, 0])
    grad_gate = weight_grad(gate_grad, rows_in, 256)
    grad_up = weight_grad(up_grad, rows_in, 256)
    grad_down = weight_grad(weighted, rows_grad, 256)
    peer = swap(ret_far, ("core",), 1)
    summed = (ret_near.astype(F32) + peer.astype(F32)).astype(BF16)
    quarter = half // 4
    pieces = [summed[k * quarter : (k + 1) * quarter] for k in range(4)]
    got = [pieces[0]] + [swap(pieces[k], ("x", "y"), k) for k in range(1, 4)]
    summed = sum(g.astype(F32) for g in got).astype(BF16)
    pieces = [summed[k * rows : (k + 1) * rows] for k in range(4)]
    got = [pieces[0]] + [swap(pieces[k], ("z",), k) for k in range(1, 4)]
    mine_input, mine_gates = pl.pallas_call(
        final_kernel,
        in_specs=[whole()] * 5,
        out_specs=[whole()] * 2,
        out_shape=[
            jax.ShapeDtypeStruct((rows, width), BF16),
            jax.ShapeDtypeStruct((rows, top_k), F32),
        ],
        name="finish",
    )(*got, routes[0])
    return (
        mine_input[None],
        mine_gates[None],
        grad_gate[None, None],
        grad_up[None, None],
        grad_down[None, None],
    )


def mapped(local, mesh, group, expert):
    return jax.shard_map(
        local,
        mesh=mesh,
        in_specs=(
            P(expert, group, None),
            P(expert, group, None),
            P(expert, group, None),
            P(expert, group, None),
            P(),
            P(group, expert, None, None),
            P(group, expert, None, None),
            P(group, expert, None, None),
        ),
        out_specs=(
            P(expert, group, None),
            P(expert, group, None),
            P(group, expert, None, None),
            P(group, expert, None, None),
            P(group, expert, None, None),
        ),
        check_vma=False,
    )


def solution(mesh):
    if mesh.shape["group"] == 2 and mesh.shape["expert"] == 16:
        split = Mesh(mesh.devices.reshape(2, 4, 2, 2), ("x", "z", "y", "core"))
        return mapped(block_local, split, "x", ("z", "y", "core"))
    return mapped(general_local, mesh, "group", "expert")
```

time: 131 us -> 77.7 us (0.59)
  Pallas kernels: 0 us -> 26.5 us
  blocking collectives: 24.2 us -> 0 us
  matrix products: 22.8 us -> 0 us
  between operations: 15 us -> 1.4 us
  local copies, waits for them, and re-layouts: 16.3 us -> 4.03 us
  starting transfers between devices: 25 us -> 17.3 us
  waiting for transfers between devices: 19.7 us -> 25.7 us
  other arithmetic: 7.56 us -> 2.17 us
    pallas_call x0 -> x6, Pallas kernels: none -> 26.5 us  [the longest x3 11.8 us: weight_grad(): pl.pallas_call(weight_kernel, grid=(hidden // tile,), in_specs=[pl.BlockS...]
    ppermute x0 -> x14, waiting for transfers between devices: none -> 25.7 us  [swap(): return lax.ppermute(x, axes, [(i, i ^ bits) for i in range(sizes)])]
    all_to_all x5 -> x0, starting transfers between devices: 25 us -> none  [the longest x1 6.43 us: local(): lax.all_to_all(padded_gates[send_pair], 'expert', split_axis=0, concat_ax...]
    dot_general x8 -> x0, matrix products: 22.8 us -> none  [the longest x1 3.96 us: expert_backward(): lax.dot_general(rows_grad, down_shard, contraction_dims, preferred_elemen...]
    all_gather x4 -> x0, blocking collectives: 19.2 us -> none  [the longest x1 5.53 us: local(): all_ids = lax.all_gather(routes, 'group', axis=1, tiled=True)]
    all_to_all x5 -> x0, waiting for transfers between devices: 18.8 us -> none  [the longest x1 8.46 us: local(): lax.all_to_all(padded_grad[send_token], 'expert', split_axis=0, concat_ax...]
    ppermute x0 -> x14, starting transfers between devices: none -> 17.3 us  [swap(): return lax.ppermute(x, axes, [(i, i ^ bits) for i in range(sizes)])]
    gather x7 -> x0, local copies, waits for them, and re-layouts: 5.96 us -> none  [the longest x1 1.73 us: local(): padded_in[send_token]]
  transfers between devices with their start and end apart: 6 -> 14, of which waited for: 4 -> 9; matrix products, arithmetic and copies ran while one was open for 25% -> 2% of each run, Pallas kernels for 0% -> 15%
where the time goes in v1:
time: 77.7 us; the launch traced here: 77.1 us
  Pallas kernels  26.5 us (34%)
  waiting for transfers between devices  25.7 us (33%)
  starting transfers between devices  17.3 us (22%)
  local copies, waits for them, and re-layouts  4.03 us (5%)
  other arithmetic  2.17 us (3%)
  between operations  1.4 us (2%)
    ppermute x14, waiting for transfers between devices, swap(): return lax.ppermute(x, axes, [(i, i ^ bits) for i in range(sizes)])  25.7 us
    ppermute x14, starting transfers between devices, swap(): return lax.ppermute(x, axes, [(i, i ^ bits) for i in range(sizes)])  17.3 us
    pallas_call x3, Pallas kernels, weight_grad(): pl.pallas_call(weight_kernel, grid=(hidden // tile,), in_specs=[pl.BlockS...  11.8 us
    pallas_call x1, Pallas kernels, block_local(): pl.pallas_call(expert_kernel, in_specs=[whole(pltpu.SMEM)] + [whole()] *...  11.6 us
    unnamed x18, local copies, waits for them, and re-layouts  2.6 us
    pallas_call x1, Pallas kernels, block_local(): pl.pallas_call(final_kernel, in_specs=[whole()] * 5, out_specs=[whole()]...  1.57 us
  transfers between devices with their start and end apart: 14, of which 9 were waited for; matrix products, arithmetic and copies ran while one was open for 2% of the time, Pallas kernels for 15%

profile of v1, /device:TPU:0, one launch (start us, length us, event | category | flops | bytes accessed | tf_op | source)
XLA Modules:
  0.0 77.1 jit_solution(1683998925693725911)
XLA Ops:
  0.6 1.5 %build_message.1 = bf16[8,4224]{1,0:T(8,128)(2,1)} custom-call(bf16[8,2048]{1,0:T(8,128)(2,1)} %bitcast.20, bf16[8,2048]{1,0:T(8,128)(2,1)} %bitcast.21, bf16[8,8]{1,0:T(8,128)(2,1)} %bitcast.24, s32[8,8]{1,0:T(8,128)} %bitcast.22), custom_call_target="tpu_custom_call" | custom-call | tf_op jit(solution)/shard_map/build_message/pallas_call | solution.py:273
  2.1 5.0 %collective-permute-start.2 = (bf16[8,4224]{1,0:T(8,128)(2,1)}, bf16[8,4224]{1,0:T(8,128)(2,1)S(1)}, u32[]{:S(2)}, u32[]{:S(2)}) collective-permute-start(bf16[8,4224]{1,0:T(8,128)(2,1)} %build_message.1), channel_id=1, source_target_pairs={{0,12},{4,8},{8,4},{12,0},{1,13},{5,9},{9,5},{13,1},{2,14},{6,10},... | collective-permute-start | bytes 202760 | tf_op jit(solution)/shard_map/ppermute | solution.py:255
  7.2 0.0 collective-permute-start.1
  7.2 0.6 collective-permute-start
  7.8 0.9 %constant_dynamic-update-slice_fusion.6 = bf16[128,4224]{1,0:T(8,128)(2,1)S(1)} fusion(bf16[8,4224]{1,0:T(8,128)(2,1)} %build_message.1), kind=kLoop, calls=%fused_computation.9 | loop fusion | bytes 135168
  8.7 1.4 %collective-permute-done.2 = bf16[8,4224]{1,0:T(8,128)(2,1)S(1)} collective-permute-done((bf16[8,4224]{1,0:T(8,128)(2,1)}, bf16[8,4224]{1,0:T(8,128)(2,1)S(1)}, u32[]{:S(2)}, u32[]{:S(2)}) %collective-permute-start.2) | collective-permute-done | bytes 67616 | tf_op jit(solution)/shard_map/ppermute | solution.py:255
  10.1 3.1 %collective-permute-done.1 = bf16[8,4224]{1,0:T(8,128)(2,1)S(1)} collective-permute-done((bf16[8,4224]{1,0:T(8,128)(2,1)}, bf16[8,4224]{1,0:T(8,128)(2,1)S(1)}, u32[]{:S(2)}, u32[]{:S(2)}) %collective-permute-start.1) | collective-permute-done | bytes 67616 | tf_op jit(solution)/shard_map/ppermute | solution.py:255
  13.2 0.0 collective-permute-done
  13.2 0.9 %pad_maximum_fusion = bf16[32,4224]{1,0:T(8,128)(2,1)S(1)} fusion(bf16[8,4224]{1,0:T(8,128)(2,1)S(1)} %collective-permute-done.2, bf16[8,4224]{1,0:T(8,128)(2,1)S(1)} %collective-permute-done.1, bf16[8,4224]{1,0:T(8,128)(2,1)S(1)} %collective-permute-done, bf16[8,4224]{1,0:T(8,128)(2,1)} %build_message.1), kind=kLoop, calls=%fused_computation.2 | loop fusion | flops 1081344 | bytes 540672 | tf_op jit(solution)/shard_map/concatenate | solution.py:280
  14.1 0.0 copy-start.5
  14.1 2.5 %collective-permute-start.5 = (bf16[32,4224]{1,0:T(8,128)(2,1)S(1)}, bf16[32,4224]{1,0:T(8,128)(2,1)S(1)}, u32[]{:S(2)}, u32[]{:S(2)}) collective-permute-start(bf16[32,4224]{1,0:T(8,128)(2,1)S(1)} %pad_maximum_fusion), channel_id=1, source_target_pairs={{0,18},{2,16},{16,2},{18,0},{1,19},{3,17},{17,3},{19,1},{4,22},{6,... | collective-permute-start | bytes 811016 | tf_op jit(solution)/shard_map/ppermute | solution.py:255
  16.6 0.5 collective-permute-start.4
  17.1 0.5 collective-permute-start.3
  17.7 11.2 %collective-permute-done.3 = bf16[32,4224]{1,0:T(8,128)(2,1)S(1)} collective-permute-done((bf16[32,4224]{1,0:T(8,128)(2,1)S(1)}, bf16[32,4224]{1,0:T(8,128)(2,1)S(1)}, u32[]{:S(2)}, u32[]{:S(2)}) %collective-permute-start.3) | collective-permute-done | bytes 270368 | tf_op jit(solution)/shard_map/ppermute | solution.py:255
  28.9 0.3 collective-permute-done.4
  29.2 0.0 collective-permute-done.5
  29.2 0.0 copy-start
  29.3 0.1 collective-permute-start.6
  29.3 0.0 copy-done.5
  29.4 0.7 dynamic_slice.3
  30.8 1.3 %collective-permute-done.6.far_ref = bf16[128,4224]{1,0:T(8,128)(2,1)S(1)} collective-permute-done((bf16[128,4224]{1,0:T(8,128)(2,1)S(1)}, bf16[128,4224]{1,0:T(8,128)(2,1)S(1)}, u32[]{:S(2)}, u32[]{:S(2)}) %collective-permute-start.6) | collective-permute-done | bytes 1081376 | tf_op jit(solution)/shard_map/ppermute | solution.py:255
  32.0 1.0 %copy-done.1 = bf16[128,4224]{1,0:T(8,128)(2,1)} copy-done((bf16[128,4224]{1,0:T(8,128)(2,1)}, bf16[128,4224]{1,0:T(8,128)(2,1)S(1)}, u32[]{:S(2)}) %copy-start.1) | copy-done | bytes 1081368
  33.0 11.6 %expert.1 = (bf16[128,2176]{1,0:T(8,128)(2,1)}, bf16[128,2176]{1,0:T(8,128)(2,1)}, bf16[128,2048]{1,0:T(8,128)(2,1)}, bf16[128,2048]{1,0:T(8,128)(2,1)}, bf16[12...) custom-call(s32[1]{0:T(128)} %bitcast.1.which_ref, bf16[128,4224]{1,0:T(8,128)(2,1)} %copy-done, ...), custom_call_target="tpu_custom_call" | custom-call | tf_op jit(solution)/shard_map/expert/pallas_call | solution.py:287
  44.6 0.2 collective-permute-start.7
  44.8 2.0 %collective-permute-done.7 = bf16[128,2176]{1,0:T(8,128)(2,1)S(1)} collective-permute-done((bf16[128,2176]{1,0:T(8,128)(2,1)}, bf16[128,2176]{1,0:T(8,128)(2,1)S(1)}, u32[]{:S(2)}, u32[]{:S(2)}) %collective-permute-start.7) | collective-permute-done | bytes 557088 | tf_op jit(solution)/shard_map/ppermute | solution.py:255
  46.8 1.2 %add_convert_fusion = bf16[128,2176]{1,0:T(8,128)(2,1)S(1)} fusion(bf16[128,2176]{1,0:T(8,128)(2,1)S(1)} %collective-permute-done.7, bf16[128,2176]{1,0:T(8,128)(2,1)} %get-tuple-element.14), kind=kLoop, calls=%fused_computation | loop fusion | flops 1114112 | bytes 1671168 | tf_op jit(solution)/shard_map/convert_element_type | solution.py:307
  48.0 1.5 %collective-permute-start.8 = (bf16[32,2176]{1,0:T(8,128)(2,1)S(1)}, bf16[32,2176]{1,0:T(8,128)(2,1)S(1)}, u32[]{:S(2)}, u32[]{:S(2)}) collective-permute-start(bf16[32,2176]{1,0:T(8,128)(2,1)S(1)} %get-tuple-element.23), channel_id=1, source_target_pairs={{0,2},{2,0},{16,18},{18,16},{1,3},{3,1},{17,19},{19,17},{4,6},{6,4... | collective-permute-start | bytes 417800 | tf_op jit(solution)/shard_map/ppermute | solution.py:255
  49.6 1.5 %collective-permute-start.10 = (bf16[32,2176]{1,0:T(8,128)(2,1)S(1)}, bf16[32,2176]{1,0:T(8,128)(2,1)S(1)}, u32[]{:S(2)}, u32[]{:S(2)}) collective-permute-start(bf16[32,2176]{1,0:T(8,128)(2,1)S(1)} %get-tuple-element.24), channel_id=1, source_target_pairs={{0,18},{2,16},{16,2},{18,0},{1,19},{3,17},{17,3},{19,1},{4,22},{6,... | collective-permute-start | bytes 417800 | tf_op jit(solution)/shard_map/ppermute | solution.py:255
  51.1 0.5 collective-permute-start.9
  51.6 5.0 %collective-permute-done.8 = bf16[32,2176]{1,0:T(8,128)(2,1)S(1)} collective-permute-done((bf16[32,2176]{1,0:T(8,128)(2,1)S(1)}, bf16[32,2176]{1,0:T(8,128)(2,1)S(1)}, u32[]{:S(2)}, u32[]{:S(2)}) %collective-permute-start.8) | collective-permute-done | bytes 139296 | tf_op jit(solution)/shard_map/ppermute | solution.py:255
  56.6 0.4 collective-permute-done.10
  57.0 1.0 %collective-permute-done.9 = bf16[32,2176]{1,0:T(8,128)(2,1)S(1)} collective-permute-done((bf16[32,2176]{1,0:T(8,128)(2,1)S(1)}, bf16[32,2176]{1,0:T(8,128)(2,1)S(1)}, u32[]{:S(2)}, u32[]{:S(2)}) %collective-permute-start.9) | collective-permute-done | bytes 139296 | tf_op jit(solution)/shard_map/ppermute | solution.py:255
  58.0 0.1 add_convert_fusion.1
  58.1 0.6 fusion.1
  58.8 1.3 %collective-permute-start.13 = (bf16[8,2176]{1,0:T(8,128)(2,1)S(1)}, bf16[8,2176]{1,0:T(8,128)(2,1)S(1)}, u32[]{:S(2)}, u32[]{:S(2)}) collective-permute-start(bf16[8,2176]{1,0:T(8,128)(2,1)S(1)} %get-tuple-element.26), channel_id=1, source_target_pairs={{0,12},{4,8},{8,4},{12,0},{1,13},{5,9},{9,5},{13,1},{2,14},{6,10},... | collective-permute-start | bytes 104456 | tf_op jit(solution)/shard_map/ppermute | solution.py:255
  60.1 0.1 collective-permute-start.12
  60.1 3.0 %collective-permute-start.11 = (bf16[8,2176]{1,0:T(8,128)(2,1)S(1)}, bf16[8,2176]{1,0:T(8,128)(2,1)S(1)}, u32[]{:S(2)}, u32[]{:S(2)}) collective-permute-start(bf16[8,2176]{1,0:T(8,128)(2,1)S(1)} %get-tuple-element.28), channel_id=1, source_target_pairs={{0,4},{4,0},{8,12},{12,8},{1,5},{5,1},{9,13},{13,9},{2,6},{6,2},{1... | collective-permute-start | bytes 104456 | tf_op jit(solution)/shard_map/ppermute | solution.py:255
  63.1 3.9 %weight_grad.3 = bf16[768,2048]{1,0:T(8,128)(2,1)} custom-call(bf16[128,768]{1,0:T(8,128)(2,1)} %get-tuple-element.18.a_ref, bf16[128,2048]{1,0:T(8,128)(2,1)} %get-tuple-element.19.b_ref), custom_call_target="tpu_custom_call" | custom-call | tf_op jit(solution)/shard_map/weight_grad/pallas_call | solution.py:215
  67.1 3.9 %weight_grad.4 = bf16[768,2048]{1,0:T(8,128)(2,1)} custom-call(bf16[128,768]{1,0:T(8,128)(2,1)} %get-tuple-element.20.a_ref, bf16[128,2048]{1,0:T(8,128)(2,1)} %get-tuple-element.19.b_ref), custom_call_target="tpu_custom_call" | custom-call | tf_op jit(solution)/shard_map/weight_grad/pallas_call | solution.py:215
  71.0 3.9 %weight_grad.5 = bf16[768,2048]{1,0:T(8,128)(2,1)} custom-call(bf16[128,768]{1,0:T(8,128)(2,1)} %get-tuple-element.21.a_ref, bf16[128,2048]{1,0:T(8,128)(2,1)} %get-tuple-element.22.b_ref), custom_call_target="tpu_custom_call" | custom-call | tf_op jit(solution)/shard_map/weight_grad/pallas_call | solution.py:215
  74.9 0.0 collective-permute-done.13.d_ref
  74.9 0.0 collective-permute-done.12.c_ref
  74.9 0.0 copy-start.3
  75.0 0.0 collective-permute-done.11.b_ref
  75.0 0.6 copy-done.2
  75.5 0.0 copy-done.3
  75.6 0.0 copy-done.4
  75.6 1.6 %finish.1 = (bf16[8,2048]{1,0:T(8,128)(2,1)}, f32[8,8]{1,0:T(8,128)}) custom-call(bf16[8,2176]{1,0:T(8,128)(2,1)} %get-tuple-element.29.a_ref, bf16[8,2176]{1,0:T(8,128)(2,1)} %copy-done.4, bf16[8,2176]{1,0:T(8,128)(2,1)} %copy-done.3, bf16[8,2176]{1,0:T(8,128)(2,1)} %copy-done.2, s32[8,8]{1,0:T(8,128)} %bitcast.23), custom_call_target="tpu_custom_call" | custom-call | tf_op jit(solution)/shard_map/finish/pallas_call | solution.py:314
  (11 shorter events, 0.2 us)
Async XLA Ops:
  2.1 7.9 %collective-permute-start.2 = (bf16[8,4224]{1,0:T(8,128)(2,1)}, bf16[8,4224]{1,0:T(8,128)(2,1)S(1)}, u32[]{:S(2)}, u32[]{:S(2)}) collective-permute-start(bf16[8,4224]{1,0:T(8,128)(2,1)} %build_message.1), channel_id=1, source_target_pairs={{0,12},{4,8},{8,4},{12,0},{1,13},{5,9},{9,5},{13,1},{2,14},{6,10},... | collective-permute-start | bytes 202760 | tf_op jit(solution)/shard_map/ppermute | solution.py:255
  7.2 6.0 %collective-permute-start.1 = (bf16[8,4224]{1,0:T(8,128)(2,1)}, bf16[8,4224]{1,0:T(8,128)(2,1)S(1)}, u32[]{:S(2)}, u32[]{:S(2)}) collective-permute-start(bf16[8,4224]{1,0:T(8,128)(2,1)} %build_message.1), channel_id=1, source_target_pairs={{0,8},{4,12},{8,0},{12,4},{1,9},{5,13},{9,1},{13,5},{2,10},{6,14},... | collective-permute-start | bytes 202760 | tf_op jit(solution)/shard_map/ppermute | solution.py:255
  7.2 6.0 %collective-permute-start = (bf16[8,4224]{1,0:T(8,128)(2,1)}, bf16[8,4224]{1,0:T(8,128)(2,1)S(1)}, u32[]{:S(2)}, u32[]{:S(2)}) collective-permute-start(bf16[8,4224]{1,0:T(8,128)(2,1)} %build_message.1), channel_id=1, source_target_pairs={{0,4},{4,0},{8,12},{12,8},{1,5},{5,1},{9,13},{13,9},{2,6},{6,2},{1... | collective-permute-start | bytes 202760 | tf_op jit(solution)/shard_map/ppermute | solution.py:255
  14.1 15.3 %copy-start.5 = (s32[2,16]{1,0:T(2,128)S(1)}, s32[2,16]{1,0:T(2,128)}, u32[]{:S(2)}) copy-start(s32[2,16]{1,0:T(2,128)} %param.12) | copy-start | bytes 388
  14.1 15.1 %collective-permute-start.5 = (bf16[32,4224]{1,0:T(8,128)(2,1)S(1)}, bf16[32,4224]{1,0:T(8,128)(2,1)S(1)}, u32[]{:S(2)}, u32[]{:S(2)}) collective-permute-start(bf16[32,4224]{1,0:T(8,128)(2,1)S(1)} %pad_maximum_fusion), channel_id=1, source_target_pairs={{0,18},{2,16},{16,2},{18,0},{1,19},{3,17},{17,3},{19,1},{4,22},{6,... | collective-permute-start | bytes 811016 | tf_op jit(solution)/shard_map/ppermute | solution.py:255
  16.6 12.6 %collective-permute-start.4 = (bf16[32,4224]{1,0:T(8,128)(2,1)S(1)}, bf16[32,4224]{1,0:T(8,128)(2,1)S(1)}, u32[]{:S(2)}, u32[]{:S(2)}) collective-permute-start(bf16[32,4224]{1,0:T(8,128)(2,1)S(1)} %pad_maximum_fusion), channel_id=1, source_target_pairs={{0,16},{2,18},{16,0},{18,2},{1,17},{3,19},{17,1},{19,3},{4,20},{6,... | collective-permute-start | bytes 811016 | tf_op jit(solution)/shard_map/ppermute | solution.py:255
  17.1 11.8 %collective-permute-start.3 = (bf16[32,4224]{1,0:T(8,128)(2,1)S(1)}, bf16[32,4224]{1,0:T(8,128)(2,1)S(1)}, u32[]{:S(2)}, u32[]{:S(2)}) collective-permute-start(bf16[32,4224]{1,0:T(8,128)(2,1)S(1)} %pad_maximum_fusion), channel_id=1, source_target_pairs={{0,2},{2,0},{16,18},{18,16},{1,3},{3,1},{17,19},{19,17},{4,6},{6,4... | collective-permute-start | bytes 811016 | tf_op jit(solution)/shard_map/ppermute | solution.py:255
  29.2 2.8 %copy-start = (bf16[128,4224]{1,0:T(8,128)(2,1)}, bf16[128,4224]{1,0:T(8,128)(2,1)S(1)}, u32[]{:S(2)}) copy-start(bf16[128,4224]{1,0:T(8,128)(2,1)S(1)} %constant_dynamic-update-slice_fusion.near_ref) | copy-start | bytes 3244036
  29.3 2.8 %collective-permute-start.6 = (bf16[128,4224]{1,0:T(8,128)(2,1)S(1)}, bf16[128,4224]{1,0:T(8,128)(2,1)S(1)}, u32[]{:S(2)}, u32[]{:S(2)}) collective-permute-start(bf16[128,4224]{1,0:T(8,128)(2,1)S(1)} %constant_dynamic-update-slice_fusion.near_ref), channel_id=1, source_target_pairs={{0,1},{1,0},{2,3},{3,2},{4,5},{5,4},{6,7},{7,6},{8,9},{9,8},{10,11... | collective-permute-start | bytes 3244040 | tf_op jit(solution)/shard_map/ppermute | solution.py:255
  32.0 1.0 %copy-start.1 = (bf16[128,4224]{1,0:T(8,128)(2,1)}, bf16[128,4224]{1,0:T(8,128)(2,1)S(1)}, u32[]{:S(2)}) copy-start(bf16[128,4224]{1,0:T(8,128)(2,1)S(1)} %collective-permute-done.6.far_ref) | copy-start | bytes 3244036
  44.6 2.2 %collective-permute-start.7 = (bf16[128,2176]{1,0:T(8,128)(2,1)}, bf16[128,2176]{1,0:T(8,128)(2,1)S(1)}, u32[]{:S(2)}, u32[]{:S(2)}) collective-permute-start(bf16[128,2176]{1,0:T(8,128)(2,1)} %get-tuple-element.15), channel_id=1, source_target_pairs={{0,1},{1,0},{2,3},{3,2},{4,5},{5,4},{6,7},{7,6},{8,9},{9,8},{10,11... | collective-permute-start | bytes 1671176 | tf_op jit(solution)/shard_map/ppermute | solution.py:255
  48.0 8.6 %collective-permute-start.8 = (bf16[32,2176]{1,0:T(8,128)(2,1)S(1)}, bf16[32,2176]{1,0:T(8,128)(2,1)S(1)}, u32[]{:S(2)}, u32[]{:S(2)}) collective-permute-start(bf16[32,2176]{1,0:T(8,128)(2,1)S(1)} %get-tuple-element.23), channel_id=1, source_target_pairs={{0,2},{2,0},{16,18},{18,16},{1,3},{3,1},{17,19},{19,17},{4,6},{6,4... | collective-permute-start | bytes 417800 | tf_op jit(solution)/shard_map/ppermute | solution.py:255
  49.6 7.5 %collective-permute-start.10 = (bf16[32,2176]{1,0:T(8,128)(2,1)S(1)}, bf16[32,2176]{1,0:T(8,128)(2,1)S(1)}, u32[]{:S(2)}, u32[]{:S(2)}) collective-permute-start(bf16[32,2176]{1,0:T(8,128)(2,1)S(1)} %get-tuple-element.24), channel_id=1, source_target_pairs={{0,18},{2,16},{16,2},{18,0},{1,19},{3,17},{17,3},{19,1},{4,22},{6,... | collective-permute-start | bytes 417800 | tf_op jit(solution)/shard_map/ppermute | solution.py:255
  51.1 7.0 %collective-permute-start.9 = (bf16[32,2176]{1,0:T(8,128)(2,1)S(1)}, bf16[32,2176]{1,0:T(8,128)(2,1)S(1)}, u32[]{:S(2)}, u32[]{:S(2)}) collective-permute-start(bf16[32,2176]{1,0:T(8,128)(2,1)S(1)} %get-tuple-element.25), channel_id=1, source_target_pairs={{0,16},{2,18},{16,0},{18,2},{1,17},{3,19},{17,1},{19,3},{4,20},{6,... | collective-permute-start | bytes 417800 | tf_op jit(solution)/shard_map/ppermute | solution.py:255
  58.8 16.2 %collective-permute-start.13 = (bf16[8,2176]{1,0:T(8,128)(2,1)S(1)}, bf16[8,2176]{1,0:T(8,128)(2,1)S(1)}, u32[]{:S(2)}, u32[]{:S(2)}) collective-permute-start(bf16[8,2176]{1,0:T(8,128)(2,1)S(1)} %get-tuple-element.26), channel_id=1, source_target_pairs={{0,12},{4,8},{8,4},{12,0},{1,13},{5,9},{9,5},{13,1},{2,14},{6,10},... | collective-permute-start | bytes 104456 | tf_op jit(solution)/shard_map/ppermute | solution.py:255
  60.1 14.9 %collective-permute-start.12 = (bf16[8,2176]{1,0:T(8,128)(2,1)S(1)}, bf16[8,2176]{1,0:T(8,128)(2,1)S(1)}, u32[]{:S(2)}, u32[]{:S(2)}) collective-permute-start(bf16[8,2176]{1,0:T(8,128)(2,1)S(1)} %get-tuple-element.27), channel_id=1, source_target_pairs={{0,8},{4,12},{8,0},{12,4},{1,9},{5,13},{9,1},{13,5},{2,10},{6,14},... | collective-permute-start | bytes 104456 | tf_op jit(solution)/shard_map/ppermute | solution.py:255
  60.1 14.8 %collective-permute-start.11 = (bf16[8,2176]{1,0:T(8,128)(2,1)S(1)}, bf16[8,2176]{1,0:T(8,128)(2,1)S(1)}, u32[]{:S(2)}, u32[]{:S(2)}) collective-permute-start(bf16[8,2176]{1,0:T(8,128)(2,1)S(1)} %get-tuple-element.28), channel_id=1, source_target_pairs={{0,4},{4,0},{8,12},{12,8},{1,5},{5,1},{9,13},{13,9},{2,6},{6,2},{1... | collective-permute-start | bytes 104456 | tf_op jit(solution)/shard_map/ppermute | solution.py:255
  74.9 0.6 copy-start.2
  74.9 0.6 copy-start.3
  75.0 0.6 copy-start.4

commit v2 on v1

--- a/solution.py
+++ b/solution.py
@@ -13,7 +13,6 @@
 LANES = 128
 F32 = jnp.float32
 BF16 = jnp.bfloat16
-VMEM_LIMIT = 56 * 1024 * 1024
 
 
 def expert_backward(rows_in, rows_grad, row_gates, gate_shard, up_shard, down_shard):
@@ -124,10 +123,14 @@
     )
 
 
+def dot_on(a, b, da, db):
+    return lax.dot_general(a, b, (((da,), (db,)), ((), ())), preferred_element_type=F32)
+
+
 def build_message(tok_ref, grad_ref, gates_ref, routes_ref, out_ref):
     width = tok_ref.shape[1]
     out_ref[:, :width] = tok_ref[...]
-    out_ref[:, width : 2 * width] = grad_ref[...]
+    out_ref[:, width + LANES :] = grad_ref[...]
     rows, top_k = routes_ref.shape
     lane = lax.broadcasted_iota(jnp.int32, (rows, LANES), 1)
     routes = routes_ref[...]
@@ -137,92 +140,153 @@
         chosen = routes[:, k : k + 1]
         dense = jnp.where(lane == chosen, gates[:, k : k + 1], dense)
         dense = jnp.where(lane == chosen + LANES // 2, 1.0, dense)
-    out_ref[:, 2 * width :] = dense.astype(BF16)
-
-
-def dot_tt(a, b, da, db):
-    return lax.dot_general(a, b, (((da,), (db,)), ((), ())), preferred_element_type=F32)
-
-
-def expert_kernel(
-    which_ref, near_ref, far_ref, wg_ref, wu_ref, wd_ref,
-    ret_near_ref, ret_far_ref, rin_ref, rgrad_ref, gg_ref, ug_ref, gw_ref,
+    out_ref[:, width : width + LANES] = dense.astype(BF16)
+
+
+def my_expert(shard_ref):
+    group = lax.axis_index("x")
+    place = (lax.axis_index("z") * 2 + lax.axis_index("y")) * 2 + lax.axis_index("core")
+    return shard_ref[group, place] + group * EXP_GROUP
+
+
+def load(src_ref, dst_ref, sems, parts=4):
+    step = src_ref.shape[0] // parts
+    copies = []
+    for i in range(parts):
+        part = slice(i * step, (i + 1) * step)
+        copies.append(pltpu.make_async_copy(src_ref.at[part], dst_ref.at[part], sems.at[i]))
+        copies[-1].start()
+    return copies
+
+
+def forward_kernel(
+    shard_ref, near_ref, far_ref, wg_hbm, wu_hbm, wd_hbm,
+    rin_ref, hidden_ref, gfac_ref, ufac_ref, gw_ref, snear_ref, sfar_ref, wg_ref, wu_ref, wd_ref,
+    sems,
 ):
-    which = which_ref[0]
-    half, full = near_ref.shape
-    width = rin_ref.shape[1]
-    slots = rin_ref.shape[0]
+    loads = [
+        load(src, dst, sems.at[n])
+        for n, (src, dst) in enumerate(((wg_hbm, wg_ref), (wu_hbm, wu_ref), (wd_hbm, wd_ref)))
+    ]
+    which = my_expert(shard_ref)
+    core = lax.axis_index("core")
+    half = near_ref.shape[0]
+    slots, width = rin_ref.shape
     total = 2 * half
     lane = lax.broadcasted_iota(jnp.int32, (8, LANES), 1)
     pick_gate = jnp.where(lane == which, 1.0, 0.0).astype(BF16)
     pick_mask = jnp.where(lane == which + LANES // 2, 1.0, 0.0).astype(BF16)
-    extra = jnp.concatenate([near_ref[:, 2 * width :], far_ref[:, 2 * width :]], axis=0)
-    gate_row = dot_tt(pick_gate, extra, 1, 1)
-    mask_row = dot_tt(pick_mask, extra, 1, 1)
+    extra = jnp.concatenate([near_ref[:, width:], far_ref[:, width:]], axis=0)
+    gate_row = dot_on(pick_gate, extra, 1, 1)
+    mask_row = dot_on(pick_mask, extra, 1, 1)
     before = (
         lax.broadcasted_iota(jnp.int32, (total, total), 0)
         < lax.broadcasted_iota(jnp.int32, (total, total), 1)
     )
     before = jnp.where(before, 1.0, 0.0).astype(BF16)
-    rank_row = dot_tt(mask_row.astype(BF16), before, 1, 0)
+    rank_row = dot_on(mask_row.astype(BF16), before, 1, 0)
     slot = lax.broadcasted_iota(jnp.int32, (slots, total), 0)
     hit = (slot == rank_row[:1].astype(jnp.int32)) & (mask_row[:1] > 0.5)
     select_f = jnp.where(hit, 1.0, 0.0)
     select = select_f.astype(BF16)
     row_gates = jnp.sum(select_f * gate_row[:1], axis=1, keepdims=True)
     s_near, s_far = select[:, :half], select[:, half:]
-
-    def rows_of(lo):
-        cols = slice(lo, lo + width)
-        return (
-            dot_tt(s_near, near_ref[:, cols], 1, 0) + dot_tt(s_far, far_ref[:, cols], 1, 0)
-        ).astype(BF16)
-
-    rows_in = rows_of(0)
+    rows_in = (
+        dot_on(s_near, near_ref[:, :width], 1, 0) + dot_on(s_far, far_ref[:, :width], 1, 0)
+    ).astype(BF16)
     rin_ref[...] = rows_in
-    rows_grad = rows_of(width)
-    rgrad_ref[...] = rows_grad
-    gate_pre = dot_tt(rows_in, wg_ref[...], 1, 1)
-    up_pre = dot_tt(rows_in, wu_ref[...], 1, 1)
-    back = dot_tt(rows_grad, wd_ref[...], 1, 1)
+    row = lax.broadcasted_iota(jnp.int32, (half, half), 0)
+    col = lax.broadcasted_iota(jnp.int32, (half, half), 1)
+    turned = (col % 8) + 8 * ((col // 32) + 4 * ((col // 8) % 4))
+    turn = jnp.where(row == turned, 1.0, 0.0).astype(BF16)
+    for part, ref, turn_it in ((s_near, snear_ref, core > 0), (s_far, sfar_ref, core == 0)):
+        ref[...] = jnp.where(turn_it & (MIXED != MIXED_T), dot_on(part, turn, 1, 0), part.astype(F32)).astype(BF16)
+    for copy in loads[0]:
+        copy.wait()
+    gate_pre = dot_on(rows_in, wg_ref[...], 1, 1)
+    for copy in loads[1]:
+        copy.wait()
+    up_pre = dot_on(rows_in, wu_ref[...], 1, 1)
     sigmoid = jax.nn.sigmoid(gate_pre)
     swish_gate = gate_pre * sigmoid
     hidden = swish_gate * up_pre
-    gate_part = jnp.sum(back * hidden, axis=1, keepdims=True)
-    hidden_grad = row_gates * back
-    gate_grad = (hidden_grad * up_pre * sigmoid * (1.0 + gate_pre * (1.0 - sigmoid))).astype(BF16)
-    up_grad = (hidden_grad * swish_gate).astype(BF16)
+    hidden_ref[...] = hidden
+    gw_ref[...] = (row_gates * hidden).astype(BF16)
+    ufac_ref[...] = row_gates * swish_gate
+    gfac_ref[...] = row_gates * (up_pre * sigmoid * (1.0 + gate_pre * (1.0 - sigmoid)))
+    for copy in loads[2]:
+        copy.wait()
+
+
+def backward_kernel(
+    shard_ref, near_ref, far_ref, snear_ref, sfar_ref, hidden_ref, gfac_ref, ufac_ref,
+    wg_ref, wu_ref, wd_ref,
+    ret_near_ref, ret_far_ref, rgrad_ref, gg_ref, ug_ref,
+):
+    which = my_expert(shard_ref)
+    slots, width = rgrad_ref.shape
+    s_near, s_far = snear_ref[...], sfar_ref[...]
+    rows_grad = (dot_on(s_near, near_ref[...], 1, 0) + dot_on(s_far, far_ref[...], 1, 0)).astype(
+        BF16
+    )
+    rgrad_ref[...] = rows_grad
+    back = dot_on(rows_grad, wd_ref[...], 1, 1)
+    gate_grad = (back * gfac_ref[...]).astype(BF16)
+    up_grad = (back * ufac_ref[...]).astype(BF16)
     gg_ref[...] = gate_grad
     ug_ref[...] = up_grad
-    gw_ref[...] = (row_gates * hidden).astype(BF16)
+    gate_part = jnp.sum(back * hidden_ref[...], axis=1, keepdims=True)
     input_part = (
-        dot_tt(gate_grad, wg_ref[...], 1, 0) + dot_tt(up_grad, wu_ref[...], 1, 0)
+        dot_on(gate_grad, wg_ref[...], 1, 0) + dot_on(up_grad, wu_ref[...], 1, 0)
     ).astype(BF16)
     gate_lane = lax.broadcasted_iota(jnp.int32, (slots, LANES), 1)
     gate_cols = jnp.where(gate_lane == which, gate_part, 0.0).astype(BF16)
     for s, ref in ((s_near, ret_near_ref), (s_far, ret_far_ref)):
-        ref[:, :width] = dot_tt(s, input_part, 0, 0).astype(BF16)
-        ref[:, width:] = dot_tt(s, gate_cols, 0, 0).astype(BF16)
-
-
-def weight_kernel(a_ref, b_ref, out_ref):
-    out_ref[...] = dot_tt(a_ref[...], b_ref[...], 0, 0).astype(BF16)
-
-
-def weight_grad(a, b, tile):
-    rows, hidden = a.shape
-    width = b.shape[1]
+        ref[:, :width] = dot_on(s, input_part, 0, 0).astype(BF16)
+        ref[:, width:] = dot_on(s, gate_cols, 0, 0).astype(BF16)
+
+
+def weight_kernel(tile, count, *refs):
+    pairs = [(refs[2 * n], refs[2 * n + 1]) for n in range(count)]
+    outs = refs[2 * count : 3 * count]
+    held, sems = refs[3 * count :]
+    steps = outs[0].shape[0] // tile
+    copies = []
+    for n, ((a_ref, b_ref), out) in enumerate(zip(pairs, outs)):
+        for i in range(steps):
+            part = slice(i * tile, (i + 1) * tile)
+            held[n, part, :] = dot_on(a_ref[:, part], b_ref[...], 0, 0).astype(BF16)
+            copy = pltpu.make_async_copy(held.at[n, part, :], out.at[part, :], sems.at[n, i])
+            copy.start()
+            copies.append(copy)
+    for copy in copies:
+        copy.wait()
+
+
+def weight_grads_of(*pairs, tile=256):
+    count = len(pairs)
+    hidden = pairs[0][0].shape[1]
+    width = pairs[0][1].shape[1]
+    flat = [in_vmem(v) for pair in pairs for v in pair]
     return pl.pallas_call(
-        weight_kernel,
-        grid=(hidden // tile,),
-        in_specs=[
-            pl.BlockSpec((rows, tile), lambda i: (0, i)),
-            pl.BlockSpec((rows, width), lambda i: (0, 0)),
+        functools.partial(weight_kernel, tile, count),
+        in_specs=[whole()] * len(flat),
+        out_specs=[whole(pl.ANY)] * count,
+        out_shape=[jax.ShapeDtypeStruct((hidden, width), BF16)] * count,
+        scratch_shapes=[
+            pltpu.VMEM((count, hidden, width), BF16),
+            pltpu.SemaphoreType.DMA((count, hidden // tile)),
         ],
-        out_specs=pl.BlockSpec((tile, width), lambda i: (i, 0)),
-        out_shape=jax.ShapeDtypeStruct((hidden, width), BF16),
-        name="weight_grad",
-    )(a, b)
+        compiler_params=pltpu.CompilerParams(vmem_limit_bytes=20 * 1024 * 1024),
+        name="weight_grads",
+    )(*flat)
+
+
+def sum_kernel(a_ref, b_ref, c_ref, d_ref, out_ref):
+    out_ref[...] = (
+        a_ref[...].astype(F32) + b_ref[...].astype(F32) + c_ref[...].astype(F32)
+        + d_ref[...].astype(F32)
+    ).astype(BF16)
 
 
 def final_kernel(a_ref, b_ref, c_ref, d_ref, routes_ref, in_ref, gate_ref):
@@ -244,73 +308,112 @@
     gate_ref[...] = out
 
 
+MIXED = True
+MIXED_T = MIXED
+AXES = ("x", "z", "y", "core")
+
+
 def whole(memory=pltpu.VMEM):
     return pl.BlockSpec(memory_space=memory)
 
 
-def swap(x, axes, bits):
-    sizes = 1
-    for a in axes:
-        sizes *= lax.axis_size(a)
-    return lax.ppermute(x, axes, [(i, i ^ bits) for i in range(sizes)])
-
-
-def spread(x, axes):
-    count = 1
-    for a in axes:
-        count *= lax.axis_size(a)
-    return [x] + [swap(x, axes, k) for k in range(1, count)]
+def in_vmem(x):
+    return pltpu.with_memory_space_constraint(x, pltpu.VMEM)
+
+
+def in_hbm(x):
+    return pltpu.with_memory_space_constraint(x, pltpu.HBM)
+
+
+def partner(device, plane, k):
+    x, z, y, core = device // 16, device // 4 % 4, device // 2 % 2, device % 2
+    if plane:
+        x, y = x ^ (k & 1), y ^ (k >> 1)
+    else:
+        z = z ^ k
+    return ((x * 4 + z) * 2 + y) * 2 + core
+
+
+def swap(value, late, mixed, k):
+    pairs = []
+    for device in range(32):
+        plane = late != (mixed and device % 2 == 1)
+        pairs.append((device, partner(device, plane, k)))
+    return lax.ppermute(value, AXES, pairs)
+
+
+def swap_core(value):
+    return lax.ppermute(value, AXES, [(d, d ^ 1) for d in range(32)])
+
+
+def spread(value, late, mixed):
+    return [value] + [swap(value, late, mixed, k) for k in (1, 2, 3)]
+
+
+def join(pieces):
+    return jnp.concatenate(pieces, axis=0)
+
+
+def fold(value, late, mixed):
+    part = value.shape[0] // 4
+    pieces = [value[k * part : (k + 1) * part] for k in range(4)]
+    return [pieces[0]] + [swap(pieces[k], late, mixed, k) for k in (1, 2, 3)]
 
 
 def block_local(tokens, out_grad, gates, routes, shard_of, w_gate, w_up, w_down):
-    group_now = lax.axis_index("x")
     width = tokens.shape[2]
     rows = tokens.shape[1]
     hidden = w_gate.shape[2]
     top_k = routes.shape[2]
-    full = 2 * width + LANES
     back_width = width + LANES
     message = pl.pallas_call(
         build_message,
         in_specs=[whole()] * 4,
         out_specs=whole(),
-        out_shape=jax.ShapeDtypeStruct((rows, full), BF16),
+        out_shape=pltpu.VMEM((rows, back_width + width), BF16),
         name="build_message",
     )(tokens[0], out_grad[0], gates[0], routes[0])
-    line = jnp.concatenate(spread(message, ("z",)), axis=0)
-    near = jnp.concatenate(spread(line, ("x", "y")), axis=0)
-    far = swap(near, ("core",), 1)
-    place = (lax.axis_index("z") * 2 + lax.axis_index("y")) * 2 + lax.axis_index("core")
-    which = (shard_of[group_now, place] + group_now * EXP_GROUP).astype(jnp.int32).reshape(1)
-    half = near.shape[0]
-    slots = lax.axis_size("z") * lax.axis_size("y") * lax.axis_size("core") * CAP
-    ret_near, ret_far, rows_in, rows_grad, gate_grad, up_grad, weighted = pl.pallas_call(
-        expert_kernel,
-        in_specs=[whole(pltpu.SMEM)] + [whole()] * 5,
-        out_specs=[whole()] * 7,
-        out_shape=[
-            jax.ShapeDtypeStruct((half, back_width), BF16),
-            jax.ShapeDtypeStruct((half, back_width), BF16),
-            jax.ShapeDtypeStruct((slots, width), BF16),
-            jax.ShapeDtypeStruct((slots, width), BF16),
-            jax.ShapeDtypeStruct((slots, hidden), BF16),
-            jax.ShapeDtypeStruct((slots, hidden), BF16),
-            jax.ShapeDtypeStruct((slots, hidden), BF16),
-        ],
-        compiler_params=pltpu.CompilerParams(vmem_limit_bytes=VMEM_LIMIT),
-        name="expert",
-    )(which, near, far, w_gate[0, 0], w_up[0, 0], w_down[0, 0])
-    grad_gate = weight_grad(gate_grad, rows_in, 256)
-    grad_up = weight_grad(up_grad, rows_in, 256)
-    grad_down = weight_grad(weighted, rows_grad, 256)
-    peer = swap(ret_far, ("core",), 1)
+    first = spread(message, False, MIXED)
+    t_near = join(spread(join([v[:, :back_width] for v in first]), True, MIXED))
+    g_parts = spread(join([v[:, back_width:] for v in first]), True, MIXED)
+    t_far = swap_core(t_near)
+    half = t_near.shape[0]
+    slots = 16 * CAP
+    rows_in, act, gate_fac, up_fac, weighted, s_near, s_far, wg, wu, wd = pl.pallas_call(
+        forward_kernel,
+        in_specs=[whole(pltpu.SMEM)] + [whole()] * 2 + [whole(pltpu.HBM)] * 3,
+        out_specs=[whole()] * 10,
+        out_shape=[pltpu.VMEM((slots, width), BF16)]
+        + [pltpu.VMEM((slots, hidden), F32)] * 3
+        + [pltpu.VMEM((slots, hidden), BF16)]
+        + [pltpu.VMEM((slots, half), BF16)] * 2
+        + [pltpu.VMEM((hidden, width), BF16)] * 3,
+        scratch_shapes=[pltpu.SemaphoreType.DMA((3, 4))],
+        compiler_params=pltpu.CompilerParams(vmem_limit_bytes=16 * 1024 * 1024),
+        name="forward",
+    )(shard_of, in_vmem(t_near), in_vmem(t_far), *(in_hbm(w[0, 0]) for w in (w_gate, w_up, w_down)))
+    g_parts, s_near = lax.optimization_barrier((g_parts, s_near))
+    g_near = join(g_parts)
+    g_far = swap_core(g_near)
+    ret_near, ret_far, rows_grad, gate_grad, up_grad = pl.pallas_call(
+        backward_kernel,
+        in_specs=[whole(pltpu.SMEM)] + [whole()] * 10,
+        out_specs=[whole()] * 5,
+        out_shape=[pltpu.VMEM((half, back_width), BF16)] * 2
+        + [pltpu.VMEM((slots, width), BF16)]
+        + [pltpu.VMEM((slots, hidden), BF16)] * 2,
+        compiler_params=pltpu.CompilerParams(vmem_limit_bytes=16 * 1024 * 1024),
+        name="backward",
+    )(shard_of, in_vmem(g_near), in_vmem(g_far), s_near, s_far, act, gate_fac, up_fac, wg, wu, wd)
+    peer = swap_core(ret_far)
     summed = (ret_near.astype(F32) + peer.astype(F32)).astype(BF16)
-    quarter = half // 4
-    pieces = [summed[k * quarter : (k + 1) * quarter] for k in range(4)]
-    got = [pieces[0]] + [swap(pieces[k], ("x", "y"), k) for k in range(1, 4)]
+    got = fold(summed, True, MIXED)
+    grad_gate, grad_up = weight_grads_of((gate_grad, rows_in), (up_grad, rows_in))
+    got, grad_gate, grad_up = lax.optimization_barrier((got, grad_gate, grad_up))
     summed = sum(g.astype(F32) for g in got).astype(BF16)
-    pieces = [summed[k * rows : (k + 1) * rows] for k in range(4)]
-    got = [pieces[0]] + [swap(pieces[k], ("z",), k) for k in range(1, 4)]
+    got = fold(summed, False, MIXED)
+    (grad_down,) = weight_grads_of((weighted, rows_grad))
+    got, grad_down = lax.optimization_barrier((got, grad_down))
     mine_input, mine_gates = pl.pallas_call(
         final_kernel,
         in_specs=[whole()] * 5,
@@ -320,7 +423,7 @@
             jax.ShapeDtypeStruct((rows, top_k), F32),
         ],
         name="finish",
-    )(*got, routes[0])
+    )(*[in_vmem(g) for g in got], routes[0])
     return (
         mine_input[None],
         mine_gates[None],

time: 77.7 us -> 56.6 us (0.73)
  waiting for transfers between devices: 25.7 us -> 15 us
  Pallas kernels: 26.5 us -> 17.4 us
  starting transfers between devices: 17.3 us -> 22 us
  local copies, waits for them, and re-layouts: 4.03 us -> 0.89 us
  other arithmetic: 2.17 us -> 0.24 us
    ppermute x14 -> x18, waiting for transfers between devices: 25.7 us -> 15 us  [the longest x15 11.9 us: swap(): return lax.ppermute(value, AXES, pairs)]
    pallas_call x4, Pallas kernels: 23.4 us -> 15 us  [the longest x1 5.58 us: block_local(): pl.pallas_call(forward_kernel, in_specs=[whole(pltpu.SMEM)] + [whole()] *...]
    ppermute x14 -> x18, starting transfers between devices: 17.3 us -> 22 us  [the longest x15 20.9 us: swap(): return lax.ppermute(value, AXES, pairs)]
    unnamed x18 -> x7, local copies, waits for them, and re-layouts: 2.6 us -> 0.75 us
    convert_element_type x1, other arithmetic: 1.18 us -> 0.13 us  [block_local(): summed = (ret_near.astype(F32) + peer.astype(F32)).astype(BF16)]
    concatenate x1 -> x2, other arithmetic: 0.9 us -> 0.03 us  [join(): return jnp.concatenate(pieces, axis=0)]
  transfers between devices with their start and end apart: 14 -> 18, of which waited for: 9 -> 8; matrix products, arithmetic and copies ran while one was open for 2% -> 0% of each run, Pallas kernels for 15% -> 19%
where the time goes in v2:
time: 56.6 us; the launch traced here: 56.4 us
  starting transfers between devices  22 us (39%)
  Pallas kernels  17.4 us (31%)
  waiting for transfers between devices  15 us (27%)
  local copies, waits for them, and re-layouts  0.89 us (2%)
  between operations  0.86 us (2%)
    ppermute x15, starting transfers between devices, swap(): return lax.ppermute(value, AXES, pairs)  20.9 us
    ppermute x15, waiting for transfers between devices, swap(): return lax.ppermute(value, AXES, pairs)  11.9 us
    pallas_call x1, Pallas kernels, block_local(): pl.pallas_call(forward_kernel, in_specs=[whole(pltpu.SMEM)] + [whole()] *...  5.58 us
    pallas_call x2, Pallas kernels, weight_grads_of(): pl.pallas_call(functools.partial(weight_kernel, tile, count), in_specs=[w...  5.32 us
    pallas_call x1, Pallas kernels, block_local(): pl.pallas_call(backward_kernel, in_specs=[whole(pltpu.SMEM)] + [whole()]...  4.15 us
    ppermute x3, waiting for transfers between devices, swap_core(): return lax.ppermute(value, AXES, [(d, d ^ 1) for d in range(32)])  3.12 us
    pallas_call x1, Pallas kernels, block_local(): pl.pallas_call(final_kernel, in_specs=[whole()] * 5, out_specs=[whole()]...  1.44 us
  transfers between devices with their start and end apart: 18, of which 8 were waited for; matrix products, arithmetic and copies ran while one was open for 0% of the time, Pallas kernels for 19%

profile of v2, /device:TPU:0, one launch (start us, length us, event | category | flops | bytes accessed | tf_op | source)
XLA Modules:
  0.0 56.4 jit_solution(11266854492898838491)
XLA Ops:
  0.6 0.9 %build_message.1 = bf16[8,4224]{1,0:T(8,128)(2,1)S(1)} custom-call(bf16[8,2048]{1,0:T(8,128)(2,1)} %bitcast.16, bf16[8,2048]{1,0:T(8,128)(2,1)} %bitcast.17, bf16[8,8]{1,0:T(8,128)(2,1)} %bitcast.20, s32[8,8]{1,0:T(8,128)} %bitcast.18), custom_call_target="tpu_custom_call" | custom-call | tf_op jit(solution)/shard_map/build_message/pallas_call | solution.py:369
  1.5 5.1 %collective-permute-start.2 = (bf16[8,4224]{1,0:T(8,128)(2,1)S(1)}, bf16[8,4224]{1,0:T(8,128)(2,1)S(1)}, u32[]{:S(2)}, u32[]{:S(2)}) collective-permute-start(bf16[8,4224]{1,0:T(8,128)(2,1)S(1)} %build_message.1), channel_id=1, source_target_pairs={{0,12},{1,19},{2,14},{3,17},{4,8},{5,23},{6,10},{7,21},{8,4},{9,27... | collective-permute-start | bytes 202760 | tf_op jit(solution)/shard_map/ppermute | solution.py:342
  6.6 0.0 collective-permute-start.1
  6.6 0.6 %collective-permute-start = (bf16[8,4224]{1,0:T(8,128)(2,1)S(1)}, bf16[8,4224]{1,0:T(8,128)(2,1)S(1)}, u32[]{:S(2)}, u32[]{:S(2)}) collective-permute-start(bf16[8,4224]{1,0:T(8,128)(2,1)S(1)} %build_message.1), channel_id=1, source_target_pairs={{0,4},{1,17},{2,6},{3,19},{4,0},{5,21},{6,2},{7,23},{8,12},{9,25},... | collective-permute-start | bytes 202760 | tf_op jit(solution)/shard_map/ppermute | solution.py:342
  7.3 3.6 %collective-permute-done = bf16[8,4224]{1,0:T(8,128)(2,1)S(1)} collective-permute-done((bf16[8,4224]{1,0:T(8,128)(2,1)S(1)}, bf16[8,4224]{1,0:T(8,128)(2,1)S(1)}, u32[]{:S(2)}, u32[]{:S(2)}) %collective-permute-start) | collective-permute-done | bytes 67616 | tf_op jit(solution)/shard_map/ppermute | solution.py:342
  10.9 0.9 %collective-permute-done.1 = bf16[8,4224]{1,0:T(8,128)(2,1)S(1)} collective-permute-done((bf16[8,4224]{1,0:T(8,128)(2,1)S(1)}, bf16[8,4224]{1,0:T(8,128)(2,1)S(1)}, u32[]{:S(2)}, u32[]{:S(2)}) %collective-permute-start.1) | collective-permute-done | bytes 67616 | tf_op jit(solution)/shard_map/ppermute | solution.py:342
  11.9 0.0 collective-permute-done.2
  11.9 1.9 %collective-permute-start.6 = (bf16[32,2176]{1,0:T(8,128)(2,1)S(1)}, bf16[32,2176]{1,0:T(8,128)(2,1)S(1)}, u32[]{:S(2)}, u32[]{:S(2)}) collective-permute-start(bf16[32,2176]{1,0:T(8,128)(2,1)S(1)} %pad_maximum_fusion), channel_id=1, source_target_pairs={{0,16},{1,5},{2,18},{3,7},{4,20},{5,1},{6,22},{7,3},{8,24},{9,13},... | collective-permute-start | bytes 417800 | tf_op jit(solution)/shard_map/ppermute | solution.py:342
  13.8 1.3 %collective-permute-start.8 = (bf16[32,2176]{1,0:T(8,128)(2,1)S(1)}, bf16[32,2176]{1,0:T(8,128)(2,1)S(1)}, u32[]{:S(2)}, u32[]{:S(2)}) collective-permute-start(bf16[32,2176]{1,0:T(8,128)(2,1)S(1)} %pad_maximum_fusion), channel_id=1, source_target_pairs={{0,18},{1,13},{2,16},{3,15},{4,22},{5,9},{6,20},{7,11},{8,26},{9,5... | collective-permute-start | bytes 417800 | tf_op jit(solution)/shard_map/ppermute | solution.py:342
  15.0 0.5 collective-permute-start.7
  15.5 1.5 %collective-permute-done.6 = bf16[32,2176]{1,0:T(8,128)(2,1)S(1)} collective-permute-done((bf16[32,2176]{1,0:T(8,128)(2,1)S(1)}, bf16[32,2176]{1,0:T(8,128)(2,1)S(1)}, u32[]{:S(2)}, u32[]{:S(2)}) %collective-permute-start.6) | collective-permute-done | bytes 139296 | tf_op jit(solution)/shard_map/ppermute | solution.py:342
  17.0 4.2 %collective-permute-done.7 = bf16[32,2176]{1,0:T(8,128)(2,1)S(1)} collective-permute-done((bf16[32,2176]{1,0:T(8,128)(2,1)S(1)}, bf16[32,2176]{1,0:T(8,128)(2,1)S(1)}, u32[]{:S(2)}, u32[]{:S(2)}) %collective-permute-start.7) | collective-permute-done | bytes 139296 | tf_op jit(solution)/shard_map/ppermute | solution.py:342
  21.2 0.0 collective-permute-done.8
  21.3 0.1 collective-permute-start.9
  21.4 1.6 %collective-permute-start.5 = (bf16[32,2048]{1,0:T(8,128)(2,1)S(1)}, bf16[32,2048]{1,0:T(8,128)(2,1)S(1)}, u32[]{:S(2)}, u32[]{:S(2)}) collective-permute-start(bf16[32,2048]{1,0:T(8,128)(2,1)S(1)} %pad_maximum_fusion.1), channel_id=1, source_target_pairs={{0,18},{1,13},{2,16},{3,15},{4,22},{5,9},{6,20},{7,11},{8,26},{9,5... | collective-permute-start | bytes 393224 | tf_op jit(solution)/shard_map/ppermute | solution.py:342
  23.0 1.7 %collective-permute-start.4 = (bf16[32,2048]{1,0:T(8,128)(2,1)S(1)}, bf16[32,2048]{1,0:T(8,128)(2,1)S(1)}, u32[]{:S(2)}, u32[]{:S(2)}) collective-permute-start(bf16[32,2048]{1,0:T(8,128)(2,1)S(1)} %pad_maximum_fusion.1), channel_id=1, source_target_pairs={{0,2},{1,9},{2,0},{3,11},{4,6},{5,13},{6,4},{7,15},{8,10},{9,1},{1... | collective-permute-start | bytes 393224 | tf_op jit(solution)/shard_map/ppermute | solution.py:342
  24.7 0.3 collective-permute-start.3
  25.0 0.0 collective-permute-done.9.far_ref
  25.0 0.0 copy-start
  25.0 0.7 %copy-done = s32[2,16]{1,0:T(2,128)S(1)} copy-done((s32[2,16]{1,0:T(2,128)S(1)}, s32[2,16]{1,0:T(2,128)}, u32[]{:S(2)}) %copy-start) | copy-done | bytes 152
  25.7 5.6 %forward.1 = (bf16[128,2048]{1,0:T(8,128)(2,1)S(1)}, f32[128,768]{1,0:T(8,128)S(1)}, f32[128,768]{1,0:T(8,128)S(1)}, f32[128,768]{1,0:T(8,128)S(1)}, bf16[128,76...) custom-call(s32[2,16]{1,0:T(2,128)S(1)} %copy-done, ...), custom_call_target="tpu_custom_call" | custom-call | tf_op jit(solution)/shard_map/forward/pallas_call | solution.py:382
  31.3 0.0 collective-permute-done.5
  31.3 0.0 collective-permute-done.4
  31.3 0.0 collective-permute-done.3
  31.4 0.6 %collective-permute-start.10 = (bf16[128,2048]{1,0:T(8,128)(2,1)S(1)}, bf16[128,2048]{1,0:T(8,128)(2,1)S(1)}, u32[]{:S(2)}, u32[]{:S(2)}) collective-permute-start(bf16[128,2048]{1,0:T(8,128)(2,1)S(1)} %constant_dynamic-update-slice_fusion.7.near_ref), channel_id=1, source_target_pairs={{0,1},{1,0},{2,3},{3,2},{4,5},{5,4},{6,7},{7,6},{8,9},{9,8},{10,11... | collective-permute-start | bytes 1572872 | tf_op jit(solution)/shard_map/ppermute | solution.py:346
  32.0 1.5 %collective-permute-done.10.far_ref = bf16[128,2048]{1,0:T(8,128)(2,1)S(1)} collective-permute-done((bf16[128,2048]{1,0:T(8,128)(2,1)S(1)}, bf16[128,2048]{1,0:T(8,128)(2,1)S(1)}, u32[]{:S(2)}, u32[]{:S(2)}) %collective-permute-start.10) | collective-permute-done | bytes 524320 | tf_op jit(solution)/shard_map/ppermute | solution.py:346
  33.5 4.1 %backward.1 = (bf16[128,2176]{1,0:T(8,128)(2,1)S(1)}, bf16[128,2176]{1,0:T(8,128)(2,1)S(1)}, bf16[128,2048]{1,0:T(8,128)(2,1)S(1)}, bf16[128,768]{1,0:T(8,128)(2,1)S(1)}, bf16[128,768]{1,0:T(8,128)(2,1)S(1)}) custom-call(s32[2,16]{1,0:T(2,128)S(1)} %copy-done, bf16[128,2048]{1,0:T(8,128)(2,1)S(1)} %constant_dynamic-update-slice_fusion.7.near_ref, ...), custom_call_target="tpu_custom_call" | custom-call | tf_op jit(solution)/shard_map/backward/pallas_call | solution.py:398
  37.7 0.4 collective-permute-start.11
  38.1 1.6 %collective-permute-done.11 = bf16[128,2176]{1,0:T(8,128)(2,1)S(1)} collective-permute-done((bf16[128,2176]{1,0:T(8,128)(2,1)S(1)}, bf16[128,2176]{1,0:T(8,128)(2,1)S(1)}, u32[]{:S(2)}, u32[]{:S(2)}) %collective-permute-start.11) | collective-permute-done | bytes 557088 | tf_op jit(solution)/shard_map/ppermute | solution.py:346
  39.7 0.1 add_convert_fusion
  39.9 1.6 %collective-permute-start.14 = (bf16[32,2176]{1,0:T(8,128)(2,1)S(1)}, bf16[32,2176]{1,0:T(8,128)(2,1)S(1)}, u32[]{:S(2)}, u32[]{:S(2)}) collective-permute-start(bf16[32,2176]{1,0:T(8,128)(2,1)S(1)} %get-tuple-element.75), channel_id=1, source_target_pairs={{0,18},{1,13},{2,16},{3,15},{4,22},{5,9},{6,20},{7,11},{8,26},{9,5... | collective-permute-start | bytes 417800 | tf_op jit(solution)/shard_map/ppermute | solution.py:342
  41.4 1.7 %collective-permute-start.13 = (bf16[32,2176]{1,0:T(8,128)(2,1)S(1)}, bf16[32,2176]{1,0:T(8,128)(2,1)S(1)}, u32[]{:S(2)}, u32[]{:S(2)}) collective-permute-start(bf16[32,2176]{1,0:T(8,128)(2,1)S(1)} %get-tuple-element.76), channel_id=1, source_target_pairs={{0,2},{1,9},{2,0},{3,11},{4,6},{5,13},{6,4},{7,15},{8,10},{9,1},{1... | collective-permute-start | bytes 417800 | tf_op jit(solution)/shard_map/ppermute | solution.py:342
  43.2 0.3 collective-permute-start.12
  43.4 3.2 %weight_grads.2 = (bf16[768,2048]{1,0:T(8,128)(2,1)}, bf16[768,2048]{1,0:T(8,128)(2,1)}) custom-call(bf16[128,768]{1,0:T(8,128)(2,1)S(1)} %get-tuple-element.55.refs_0_, bf16[128,2048]{1,0:T(8,128)(2,1)S(1)} %get-tuple-element.56.refs_1_.refs_3_, bf16[128,768]{1,0:T(8,128)(2,1)S(1)} %get-tuple-element.57.refs_2_, ...), custom_call_target="tpu_custom_call" | custom-call | tf_op jit(solution)/shard_map/weight_grads/pallas_call | solution.py:271
  46.6 0.0 collective-permute-done.14
  46.6 0.8 %collective-permute-done.13 = bf16[32,2176]{1,0:T(8,128)(2,1)S(1)} collective-permute-done((bf16[32,2176]{1,0:T(8,128)(2,1)S(1)}, bf16[32,2176]{1,0:T(8,128)(2,1)S(1)}, u32[]{:S(2)}, u32[]{:S(2)}) %collective-permute-start.13) | collective-permute-done | bytes 139296 | tf_op jit(solution)/shard_map/ppermute | solution.py:342
  47.4 0.8 %collective-permute-done.12 = bf16[32,2176]{1,0:T(8,128)(2,1)S(1)} collective-permute-done((bf16[32,2176]{1,0:T(8,128)(2,1)S(1)}, bf16[32,2176]{1,0:T(8,128)(2,1)S(1)}, u32[]{:S(2)}, u32[]{:S(2)}) %collective-permute-start.12) | collective-permute-done | bytes 139296 | tf_op jit(solution)/shard_map/ppermute | solution.py:342
  48.2 0.1 add_convert_fusion.1
  48.3 1.2 %collective-permute-start.17 = (bf16[8,2176]{1,0:T(8,128)(2,1)S(1)}, bf16[8,2176]{1,0:T(8,128)(2,1)S(1)}, u32[]{:S(2)}, u32[]{:S(2)}) collective-permute-start(bf16[8,2176]{1,0:T(8,128)(2,1)S(1)} %get-tuple-element.79), channel_id=1, source_target_pairs={{0,12},{1,19},{2,14},{3,17},{4,8},{5,23},{6,10},{7,21},{8,4},{9,27... | collective-permute-start | bytes 104456 | tf_op jit(solution)/shard_map/ppermute | solution.py:342
  49.5 0.9 %collective-permute-start.16 = (bf16[8,2176]{1,0:T(8,128)(2,1)S(1)}, bf16[8,2176]{1,0:T(8,128)(2,1)S(1)}, u32[]{:S(2)}, u32[]{:S(2)}) collective-permute-start(bf16[8,2176]{1,0:T(8,128)(2,1)S(1)} %get-tuple-element.80), channel_id=1, source_target_pairs={{0,8},{1,3},{2,10},{3,1},{4,12},{5,7},{6,14},{7,5},{8,0},{9,11},{1... | collective-permute-start | bytes 104456 | tf_op jit(solution)/shard_map/ppermute | solution.py:342
  50.4 2.4 %collective-permute-start.15 = (bf16[8,2176]{1,0:T(8,128)(2,1)S(1)}, bf16[8,2176]{1,0:T(8,128)(2,1)S(1)}, u32[]{:S(2)}, u32[]{:S(2)}) collective-permute-start(bf16[8,2176]{1,0:T(8,128)(2,1)S(1)} %get-tuple-element.81), channel_id=1, source_target_pairs={{0,4},{1,17},{2,6},{3,19},{4,0},{5,21},{6,2},{7,23},{8,12},{9,25},... | collective-permute-start | bytes 104456 | tf_op jit(solution)/shard_map/ppermute | solution.py:342
  52.8 2.1 %weight_grads.3 = bf16[768,2048]{1,0:T(8,128)(2,1)} custom-call(bf16[128,768]{1,0:T(8,128)(2,1)S(1)} %get-tuple-element.64.refs_0_, bf16[128,2048]{1,0:T(8,128)(2,1)S(1)} %get-tuple-element.65.refs_1_), custom_call_target="tpu_custom_call" | custom-call | tf_op jit(solution)/shard_map/weight_grads/pallas_call | solution.py:271
  54.9 0.0 collective-permute-done.17.d_ref
  54.9 0.0 collective-permute-done.16.c_ref
  54.9 0.0 collective-permute-done.15.b_ref
  55.0 1.4 %finish.1 = (bf16[8,2048]{1,0:T(8,128)(2,1)}, f32[8,8]{1,0:T(8,128)}) custom-call(bf16[8,2176]{1,0:T(8,128)(2,1)S(1)} %get-tuple-element.66.a_ref, bf16[8,2176]{1,0:T(8,128)(2,1)S(1)} %collective-permute-done.15.b_ref, bf16[8,2176]{1,0:T(8,128)(2,1)S(1)} %collective-permute-done.16.c_ref, bf16[8,2176]{1,0:T(8,128)(2,1)S(1)} %collective-permute-done.17.d_ref, ...), custom_call_target="tpu_custom_call" | custom-call | tf_op jit(solution)/shard_map/finish/pallas_call | solution.py:417
  (19 shorter events, 0.2 us)
Async XLA Ops:
  1.5 10.4 %collective-permute-start.2 = (bf16[8,4224]{1,0:T(8,128)(2,1)S(1)}, bf16[8,4224]{1,0:T(8,128)(2,1)S(1)}, u32[]{:S(2)}, u32[]{:S(2)}) collective-permute-start(bf16[8,4224]{1,0:T(8,128)(2,1)S(1)} %build_message.1), channel_id=1, source_target_pairs={{0,12},{1,19},{2,14},{3,17},{4,8},{5,23},{6,10},{7,21},{8,4},{9,27... | collective-permute-start | bytes 202760 | tf_op jit(solution)/shard_map/ppermute | solution.py:342
  6.6 5.2 %collective-permute-start.1 = (bf16[8,4224]{1,0:T(8,128)(2,1)S(1)}, bf16[8,4224]{1,0:T(8,128)(2,1)S(1)}, u32[]{:S(2)}, u32[]{:S(2)}) collective-permute-start(bf16[8,4224]{1,0:T(8,128)(2,1)S(1)} %build_message.1), channel_id=1, source_target_pairs={{0,8},{1,3},{2,10},{3,1},{4,12},{5,7},{6,14},{7,5},{8,0},{9,11},{1... | collective-permute-start | bytes 202760 | tf_op jit(solution)/shard_map/ppermute | solution.py:342
  6.6 4.3 %collective-permute-start = (bf16[8,4224]{1,0:T(8,128)(2,1)S(1)}, bf16[8,4224]{1,0:T(8,128)(2,1)S(1)}, u32[]{:S(2)}, u32[]{:S(2)}) collective-permute-start(bf16[8,4224]{1,0:T(8,128)(2,1)S(1)} %build_message.1), channel_id=1, source_target_pairs={{0,4},{1,17},{2,6},{3,19},{4,0},{5,21},{6,2},{7,23},{8,12},{9,25},... | collective-permute-start | bytes 202760 | tf_op jit(solution)/shard_map/ppermute | solution.py:342
  11.9 5.1 %collective-permute-start.6 = (bf16[32,2176]{1,0:T(8,128)(2,1)S(1)}, bf16[32,2176]{1,0:T(8,128)(2,1)S(1)}, u32[]{:S(2)}, u32[]{:S(2)}) collective-permute-start(bf16[32,2176]{1,0:T(8,128)(2,1)S(1)} %pad_maximum_fusion), channel_id=1, source_target_pairs={{0,16},{1,5},{2,18},{3,7},{4,20},{5,1},{6,22},{7,3},{8,24},{9,13},... | collective-permute-start | bytes 417800 | tf_op jit(solution)/shard_map/ppermute | solution.py:342
  13.8 7.5 %collective-permute-start.8 = (bf16[32,2176]{1,0:T(8,128)(2,1)S(1)}, bf16[32,2176]{1,0:T(8,128)(2,1)S(1)}, u32[]{:S(2)}, u32[]{:S(2)}) collective-permute-start(bf16[32,2176]{1,0:T(8,128)(2,1)S(1)} %pad_maximum_fusion), channel_id=1, source_target_pairs={{0,18},{1,13},{2,16},{3,15},{4,22},{5,9},{6,20},{7,11},{8,26},{9,5... | collective-permute-start | bytes 417800 | tf_op jit(solution)/shard_map/ppermute | solution.py:342
  15.0 6.2 %collective-permute-start.7 = (bf16[32,2176]{1,0:T(8,128)(2,1)S(1)}, bf16[32,2176]{1,0:T(8,128)(2,1)S(1)}, u32[]{:S(2)}, u32[]{:S(2)}) collective-permute-start(bf16[32,2176]{1,0:T(8,128)(2,1)S(1)} %pad_maximum_fusion), channel_id=1, source_target_pairs={{0,2},{1,9},{2,0},{3,11},{4,6},{5,13},{6,4},{7,15},{8,10},{9,1},{1... | collective-permute-start | bytes 417800 | tf_op jit(solution)/shard_map/ppermute | solution.py:342
  21.3 3.7 %collective-permute-start.9 = (bf16[128,2176]{1,0:T(8,128)(2,1)S(1)}, bf16[128,2176]{1,0:T(8,128)(2,1)S(1)}, u32[]{:S(2)}, u32[]{:S(2)}) collective-permute-start(bf16[128,2176]{1,0:T(8,128)(2,1)S(1)} %constant_dynamic-update-slice_fusion.near_ref), channel_id=1, source_target_pairs={{0,1},{1,0},{2,3},{3,2},{4,5},{5,4},{6,7},{7,6},{8,9},{9,8},{10,11... | collective-permute-start | bytes 1671176 | tf_op jit(solution)/shard_map/ppermute | solution.py:346
  21.4 9.8 %collective-permute-start.5 = (bf16[32,2048]{1,0:T(8,128)(2,1)S(1)}, bf16[32,2048]{1,0:T(8,128)(2,1)S(1)}, u32[]{:S(2)}, u32[]{:S(2)}) collective-permute-start(bf16[32,2048]{1,0:T(8,128)(2,1)S(1)} %pad_maximum_fusion.1), channel_id=1, source_target_pairs={{0,18},{1,13},{2,16},{3,15},{4,22},{5,9},{6,20},{7,11},{8,26},{9,5... | collective-permute-start | bytes 393224 | tf_op jit(solution)/shard_map/ppermute | solution.py:342
  23.0 8.3 %collective-permute-start.4 = (bf16[32,2048]{1,0:T(8,128)(2,1)S(1)}, bf16[32,2048]{1,0:T(8,128)(2,1)S(1)}, u32[]{:S(2)}, u32[]{:S(2)}) collective-permute-start(bf16[32,2048]{1,0:T(8,128)(2,1)S(1)} %pad_maximum_fusion.1), channel_id=1, source_target_pairs={{0,2},{1,9},{2,0},{3,11},{4,6},{5,13},{6,4},{7,15},{8,10},{9,1},{1... | collective-permute-start | bytes 393224 | tf_op jit(solution)/shard_map/ppermute | solution.py:342
  24.7 6.6 %collective-permute-start.3 = (bf16[32,2048]{1,0:T(8,128)(2,1)S(1)}, bf16[32,2048]{1,0:T(8,128)(2,1)S(1)}, u32[]{:S(2)}, u32[]{:S(2)}) collective-permute-start(bf16[32,2048]{1,0:T(8,128)(2,1)S(1)} %pad_maximum_fusion.1), channel_id=1, source_target_pairs={{0,16},{1,5},{2,18},{3,7},{4,20},{5,1},{6,22},{7,3},{8,24},{9,13},... | collective-permute-start | bytes 393224 | tf_op jit(solution)/shard_map/ppermute | solution.py:342
  25.0 0.7 %copy-start = (s32[2,16]{1,0:T(2,128)S(1)}, s32[2,16]{1,0:T(2,128)}, u32[]{:S(2)}) copy-start(s32[2,16]{1,0:T(2,128)} %shard_ref.3) | copy-start | bytes 388
  31.4 2.1 %collective-permute-start.10 = (bf16[128,2048]{1,0:T(8,128)(2,1)S(1)}, bf16[128,2048]{1,0:T(8,128)(2,1)S(1)}, u32[]{:S(2)}, u32[]{:S(2)}) collective-permute-start(bf16[128,2048]{1,0:T(8,128)(2,1)S(1)} %constant_dynamic-update-slice_fusion.7.near_ref), channel_id=1, source_target_pairs={{0,1},{1,0},{2,3},{3,2},{4,5},{5,4},{6,7},{7,6},{8,9},{9,8},{10,11... | collective-permute-start | bytes 1572872 | tf_op jit(solution)/shard_map/ppermute | solution.py:346
  37.7 2.0 %collective-permute-start.11 = (bf16[128,2176]{1,0:T(8,128)(2,1)S(1)}, bf16[128,2176]{1,0:T(8,128)(2,1)S(1)}, u32[]{:S(2)}, u32[]{:S(2)}) collective-permute-start(bf16[128,2176]{1,0:T(8,128)(2,1)S(1)} %get-tuple-element.54), channel_id=1, source_target_pairs={{0,1},{1,0},{2,3},{3,2},{4,5},{5,4},{6,7},{7,6},{8,9},{9,8},{10,11... | collective-permute-start | bytes 1671176 | tf_op jit(solution)/shard_map/ppermute | solution.py:346
  39.9 6.7 %collective-permute-start.14 = (bf16[32,2176]{1,0:T(8,128)(2,1)S(1)}, bf16[32,2176]{1,0:T(8,128)(2,1)S(1)}, u32[]{:S(2)}, u32[]{:S(2)}) collective-permute-start(bf16[32,2176]{1,0:T(8,128)(2,1)S(1)} %get-tuple-element.75), channel_id=1, source_target_pairs={{0,18},{1,13},{2,16},{3,15},{4,22},{5,9},{6,20},{7,11},{8,26},{9,5... | collective-permute-start | bytes 417800 | tf_op jit(solution)/shard_map/ppermute | solution.py:342
  41.4 6.0 %collective-permute-start.13 = (bf16[32,2176]{1,0:T(8,128)(2,1)S(1)}, bf16[32,2176]{1,0:T(8,128)(2,1)S(1)}, u32[]{:S(2)}, u32[]{:S(2)}) collective-permute-start(bf16[32,2176]{1,0:T(8,128)(2,1)S(1)} %get-tuple-element.76), channel_id=1, source_target_pairs={{0,2},{1,9},{2,0},{3,11},{4,6},{5,13},{6,4},{7,15},{8,10},{9,1},{1... | collective-permute-start | bytes 417800 | tf_op jit(solution)/shard_map/ppermute | solution.py:342
  43.2 5.1 %collective-permute-start.12 = (bf16[32,2176]{1,0:T(8,128)(2,1)S(1)}, bf16[32,2176]{1,0:T(8,128)(2,1)S(1)}, u32[]{:S(2)}, u32[]{:S(2)}) collective-permute-start(bf16[32,2176]{1,0:T(8,128)(2,1)S(1)} %get-tuple-element.77), channel_id=1, source_target_pairs={{0,16},{1,5},{2,18},{3,7},{4,20},{5,1},{6,22},{7,3},{8,24},{9,13},... | collective-permute-start | bytes 417800 | tf_op jit(solution)/shard_map/ppermute | solution.py:342
  48.3 6.6 %collective-permute-start.17 = (bf16[8,2176]{1,0:T(8,128)(2,1)S(1)}, bf16[8,2176]{1,0:T(8,128)(2,1)S(1)}, u32[]{:S(2)}, u32[]{:S(2)}) collective-permute-start(bf16[8,2176]{1,0:T(8,128)(2,1)S(1)} %get-tuple-element.79), channel_id=1, source_target_pairs={{0,12},{1,19},{2,14},{3,17},{4,8},{5,23},{6,10},{7,21},{8,4},{9,27... | collective-permute-start | bytes 104456 | tf_op jit(solution)/shard_map/ppermute | solution.py:342
  49.5 5.4 %collective-permute-start.16 = (bf16[8,2176]{1,0:T(8,128)(2,1)S(1)}, bf16[8,2176]{1,0:T(8,128)(2,1)S(1)}, u32[]{:S(2)}, u32[]{:S(2)}) collective-permute-start(bf16[8,2176]{1,0:T(8,128)(2,1)S(1)} %get-tuple-element.80), channel_id=1, source_target_pairs={{0,8},{1,3},{2,10},{3,1},{4,12},{5,7},{6,14},{7,5},{8,0},{9,11},{1... | collective-permute-start | bytes 104456 | tf_op jit(solution)/shard_map/ppermute | solution.py:342
  50.4 4.5 %collective-permute-start.15 = (bf16[8,2176]{1,0:T(8,128)(2,1)S(1)}, bf16[8,2176]{1,0:T(8,128)(2,1)S(1)}, u32[]{:S(2)}, u32[]{:S(2)}) collective-permute-start(bf16[8,2176]{1,0:T(8,128)(2,1)S(1)} %get-tuple-element.81), channel_id=1, source_target_pairs={{0,4},{1,17},{2,6},{3,19},{4,0},{5,21},{6,2},{7,23},{8,12},{9,25},... | collective-permute-start | bytes 104456 | tf_op jit(solution)/shard_map/ppermute | solution.py:342

commit v3 on v2

--- a/solution.py
+++ b/solution.py
@@ -127,8 +127,18 @@
     return lax.dot_general(a, b, (((da,), (db,)), ((), ())), preferred_element_type=F32)
 
 
-def build_message(tok_ref, grad_ref, gates_ref, routes_ref, out_ref):
+def build_message(
+    tok_hbm, grad_hbm, gates_hbm, routes_hbm, out_ref, tok_ref, grad_ref, gates_ref, routes_ref, sems
+):
     width = tok_ref.shape[1]
+    arrivals = (
+        (gates_hbm, gates_ref), (routes_hbm, routes_ref), (tok_hbm, tok_ref), (grad_hbm, grad_ref),
+    )
+    copies = [pltpu.make_async_copy(*pair, sems.at[n]) for n, pair in enumerate(arrivals)]
+    for copy in copies:
+        copy.start()
+    for copy in copies:
+        copy.wait()
     out_ref[:, :width] = tok_ref[...]
     out_ref[:, width + LANES :] = grad_ref[...]
     rows, top_k = routes_ref.shape
@@ -159,15 +169,32 @@
     return copies
 
 
+def prefetch_kernel(*refs):
+    count = (len(refs) - 1) // 2
+    sems = refs[-1]
+    copies = []
+    for n in range(count):
+        copies += load(refs[n], refs[count + n], sems.at[n])
+    for copy in copies:
+        copy.wait()
+
+
+def prefetch(*weights):
+    return pl.pallas_call(
+        prefetch_kernel,
+        in_specs=[whole(pltpu.HBM)] * len(weights),
+        out_specs=[whole()] * len(weights),
+        out_shape=[pltpu.VMEM(w.shape, w.dtype) for w in weights],
+        scratch_shapes=[pltpu.SemaphoreType.DMA((len(weights), 4))],
+        compiler_params=limit(2),
+        name="prefetch",
+    )(*(in_hbm(w) for w in weights))
+
+
 def forward_kernel(
-    shard_ref, near_ref, far_ref, wg_hbm, wu_hbm, wd_hbm,
-    rin_ref, hidden_ref, gfac_ref, ufac_ref, gw_ref, snear_ref, sfar_ref, wg_ref, wu_ref, wd_ref,
-    sems,
+    shard_ref, near_ref, far_ref, wg_ref, wu_ref,
+    rin_ref, hidden_ref, gfac_ref, ufac_ref, gw_ref, snear_ref, sfar_ref,
 ):
-    loads = [
-        load(src, dst, sems.at[n])
-        for n, (src, dst) in enumerate(((wg_hbm, wg_ref), (wu_hbm, wu_ref), (wd_hbm, wd_ref)))
-    ]
     which = my_expert(shard_ref)
     core = lax.axis_index("core")
     half = near_ref.shape[0]
@@ -201,11 +228,7 @@
     turn = jnp.where(row == turned, 1.0, 0.0).astype(BF16)
     for part, ref, turn_it in ((s_near, snear_ref, core > 0), (s_far, sfar_ref, core == 0)):
         ref[...] = jnp.where(turn_it & (MIXED != MIXED_T), dot_on(part, turn, 1, 0), part.astype(F32)).astype(BF16)
-    for copy in loads[0]:
-        copy.wait()
     gate_pre = dot_on(rows_in, wg_ref[...], 1, 1)
-    for copy in loads[1]:
-        copy.wait()
     up_pre = dot_on(rows_in, wu_ref[...], 1, 1)
     sigmoid = jax.nn.sigmoid(gate_pre)
     swish_gate = gate_pre * sigmoid
@@ -214,8 +237,6 @@
     gw_ref[...] = (row_gates * hidden).astype(BF16)
     ufac_ref[...] = row_gates * swish_gate
     gfac_ref[...] = row_gates * (up_pre * sigmoid * (1.0 + gate_pre * (1.0 - sigmoid)))
-    for copy in loads[2]:
-        copy.wait()
 
 
 def backward_kernel(
@@ -277,7 +298,7 @@
             pltpu.VMEM((count, hidden, width), BF16),
             pltpu.SemaphoreType.DMA((count, hidden // tile)),
         ],
-        compiler_params=pltpu.CompilerParams(vmem_limit_bytes=20 * 1024 * 1024),
+        compiler_params=limit(20),
         name="weight_grads",
     )(*flat)
 
@@ -313,6 +334,10 @@
 AXES = ("x", "z", "y", "core")
 
 
+def limit(mebibytes):
+    return pltpu.CompilerParams(vmem_limit_bytes=mebibytes * 1024 * 1024)
+
+
 def whole(memory=pltpu.VMEM):
     return pl.BlockSpec(memory_space=memory)
 
@@ -368,33 +393,43 @@
     back_width = width + LANES
     message = pl.pallas_call(
         build_message,
-        in_specs=[whole()] * 4,
+        in_specs=[whole(pltpu.HBM)] * 4,
         out_specs=whole(),
+        scratch_shapes=[
+            pltpu.VMEM(v.shape[1:], v.dtype) for v in (tokens, out_grad, gates, routes)
+        ]
+        + [pltpu.SemaphoreType.DMA((4,))],
         out_shape=pltpu.VMEM((rows, back_width + width), BF16),
+        compiler_params=limit(4),
         name="build_message",
-    )(tokens[0], out_grad[0], gates[0], routes[0])
+    )(*(in_hbm(v[0]) for v in (tokens, out_grad, gates, routes)))
     first = spread(message, False, MIXED)
-    t_near = join(spread(join([v[:, :back_width] for v in first]), True, MIXED))
-    g_parts = spread(join([v[:, back_width:] for v in first]), True, MIXED)
-    t_far = swap_core(t_near)
+    wg, wu, wd = prefetch(w_gate[0, 0], w_up[0, 0], w_down[0, 0])
+    first, wg, wu, wd = lax.optimization_barrier((first, wg, wu, wd))
+    line = join(first)
+    pieces = [line, swap(line, True, MIXED, 1), swap(line, True, MIXED, 2)]
+    t_last = swap(line[:, :back_width], True, MIXED, 3)
+    g_last = swap(line[:, back_width:], True, MIXED, 3)
+    far_pieces = [swap_core(v) for v in pieces]
+    t_near = join([v[:, :back_width] for v in pieces] + [t_last])
+    t_far = join([v[:, :back_width] for v in far_pieces] + [swap_core(t_last)])
     half = t_near.shape[0]
     slots = 16 * CAP
-    rows_in, act, gate_fac, up_fac, weighted, s_near, s_far, wg, wu, wd = pl.pallas_call(
+    rows_in, act, gate_fac, up_fac, weighted, s_near, s_far = pl.pallas_call(
         forward_kernel,
-        in_specs=[whole(pltpu.SMEM)] + [whole()] * 2 + [whole(pltpu.HBM)] * 3,
-        out_specs=[whole()] * 10,
+        in_specs=[whole(pltpu.SMEM)] + [whole()] * 4,
+        out_specs=[whole()] * 7,
         out_shape=[pltpu.VMEM((slots, width), BF16)]
         + [pltpu.VMEM((slots, hidden), F32)] * 3
         + [pltpu.VMEM((slots, hidden), BF16)]
-        + [pltpu.VMEM((slots, half), BF16)] * 2
-        + [pltpu.VMEM((hidden, width), BF16)] * 3,
-        scratch_shapes=[pltpu.SemaphoreType.DMA((3, 4))],
-        compiler_params=pltpu.CompilerParams(vmem_limit_bytes=16 * 1024 * 1024),
+        + [pltpu.VMEM((slots, half), BF16)] * 2,
+        compiler_params=limit(16),
+        cost_estimate=pl.CostEstimate(flops=1, transcendentals=0, bytes_accessed=1),
         name="forward",
-    )(shard_of, in_vmem(t_near), in_vmem(t_far), *(in_hbm(w[0, 0]) for w in (w_gate, w_up, w_down)))
-    g_parts, s_near = lax.optimization_barrier((g_parts, s_near))
-    g_near = join(g_parts)
-    g_far = swap_core(g_near)
+    )(shard_of, in_vmem(t_near), in_vmem(t_far), wg, wu)
+    g_last, _ = lax.optimization_barrier((g_last, s_near))
+    g_near = join([v[:, back_width:] for v in pieces] + [g_last])
+    g_far = join([v[:, back_width:] for v in far_pieces] + [swap_core(g_last)])
     ret_near, ret_far, rows_grad, gate_grad, up_grad = pl.pallas_call(
         backward_kernel,
         in_specs=[whole(pltpu.SMEM)] + [whole()] * 10,
@@ -402,7 +437,7 @@
         out_shape=[pltpu.VMEM((half, back_width), BF16)] * 2
         + [pltpu.VMEM((slots, width), BF16)]
         + [pltpu.VMEM((slots, hidden), BF16)] * 2,
-        compiler_params=pltpu.CompilerParams(vmem_limit_bytes=16 * 1024 * 1024),
+        compiler_params=limit(16),
         name="backward",
     )(shard_of, in_vmem(g_near), in_vmem(g_far), s_near, s_far, act, gate_fac, up_fac, wg, wu, wd)
     peer = swap_core(ret_far)
@@ -422,6 +457,7 @@
             jax.ShapeDtypeStruct((rows, width), BF16),
             jax.ShapeDtypeStruct((rows, top_k), F32),
         ],
+        compiler_params=limit(4),
         name="finish",
     )(*[in_vmem(g) for g in got], routes[0])
     return (

time: 56.6 us -> 52 us (0.919)
  waiting for transfers between devices: 15 us -> 10.9 us
  local copies, waits for them, and re-layouts: 0.89 us -> 0.23 us
    ppermute x15 -> x13, waiting for transfers between devices: 11.9 us -> 6.85 us  [swap(): return lax.ppermute(value, AXES, pairs)]
    pallas_call x1 -> x2, Pallas kernels: 0.88 us -> 4.74 us  [the longest x1 3.79 us: prefetch(): pl.pallas_call(prefetch_kernel, in_specs=[whole(pltpu.HBM)] * len(weights...]
    pallas_call x1, Pallas kernels: 5.58 us -> 2.9 us  [block_local(): pl.pallas_call(forward_kernel, in_specs=[whole(pltpu.SMEM)] + [whole()] *...]
    ppermute x3 -> x6, waiting for transfers between devices: 3.12 us -> 4.02 us  [swap_core(): return lax.ppermute(value, AXES, [(d, d ^ 1) for d in range(32)])]
    ppermute x15 -> x13, starting transfers between devices: 20.9 us -> 20.1 us  [swap(): return lax.ppermute(value, AXES, pairs)]
    unnamed x7 -> x13, local copies, waits for them, and re-layouts: 0.75 us -> 0.06 us
    pallas_call x1, Pallas kernels: 1.44 us -> 0.75 us  [block_local(): pl.pallas_call(final_kernel, in_specs=[whole()] * 5, out_specs=[whole()]...]
    ppermute x3 -> x6, starting transfers between devices: 1.11 us -> 1.47 us  [swap_core(): return lax.ppermute(value, AXES, [(d, d ^ 1) for d in range(32)])]
  transfers between devices with their start and end apart: 18 -> 19, of which waited for: 8 -> 10; matrix products, arithmetic and copies ran while one was open for 0% -> 0% of each run, Pallas kernels for 19% -> 23%
where the time goes in v3:
time: 52 us; the launch traced here: 51.8 us
  starting transfers between devices  21.5 us (41%)
  Pallas kernels  17.9 us (34%)
  waiting for transfers between devices  10.9 us (21%)
  between operations  0.91 us (2%)
    ppermute x13, starting transfers between devices, swap(): return lax.ppermute(value, AXES, pairs)  20.1 us
    ppermute x13, waiting for transfers between devices, swap(): return lax.ppermute(value, AXES, pairs)  6.85 us
    pallas_call x2, Pallas kernels, weight_grads_of(): pl.pallas_call(functools.partial(weight_kernel, tile, count), in_specs=[w...  5.31 us
    pallas_call x1, Pallas kernels, block_local(): pl.pallas_call(backward_kernel, in_specs=[whole(pltpu.SMEM)] + [whole()]...  4.16 us
    ppermute x6, waiting for transfers between devices, swap_core(): return lax.ppermute(value, AXES, [(d, d ^ 1) for d in range(32)])  4.02 us
    pallas_call x1, Pallas kernels, prefetch(): pl.pallas_call(prefetch_kernel, in_specs=[whole(pltpu.HBM)] * len(weights...  3.79 us
    pallas_call x1, Pallas kernels, block_local(): pl.pallas_call(forward_kernel, in_specs=[whole(pltpu.SMEM)] + [whole()] *...  2.9 us
    ppermute x6, starting transfers between devices, swap_core(): return lax.ppermute(value, AXES, [(d, d ^ 1) for d in range(32)])  1.47 us
  transfers between devices with their start and end apart: 19, of which 10 were waited for; matrix products, arithmetic and copies ran while one was open for 0% of the time, Pallas kernels for 23%

profile of v3, /device:TPU:0, one launch (start us, length us, event | category | flops | bytes accessed | tf_op | source)
XLA Modules:
  0.0 51.8 jit_solution(11826571211327055879)
XLA Ops:
  0.6 0.9 %build_message.1 = bf16[8,4224]{1,0:T(8,128)(2,1)S(1)} custom-call(bf16[8,2048]{1,0:T(8,128)(2,1)} %bitcast.18, bf16[8,2048]{1,0:T(8,128)(2,1)} %bitcast.19, bf16[8,8]{1,0:T(8,128)(2,1)} %bitcast.20, s32[8,8]{1,0:T(8,128)} %bitcast.12), custom_call_target="tpu_custom_call" | custom-call | tf_op jit(solution)/shard_map/build_message/pallas_call | solution.py:394
  1.6 5.1 %collective-permute-start.2 = (bf16[8,4224]{1,0:T(8,128)(2,1)S(1)}, bf16[8,4224]{1,0:T(8,128)(2,1)S(1)}, u32[]{:S(2)}, u32[]{:S(2)}) collective-permute-start(bf16[8,4224]{1,0:T(8,128)(2,1)S(1)} %build_message.1), channel_id=1, source_target_pairs={{0,12},{1,19},{2,14},{3,17},{4,8},{5,23},{6,10},{7,21},{8,4},{9,27... | collective-permute-start | bytes 202760 | tf_op jit(solution)/shard_map/ppermute | solution.py:367
  6.7 0.0 collective-permute-start.1
  6.7 0.6 %collective-permute-start = (bf16[8,4224]{1,0:T(8,128)(2,1)S(1)}, bf16[8,4224]{1,0:T(8,128)(2,1)S(1)}, u32[]{:S(2)}, u32[]{:S(2)}) collective-permute-start(bf16[8,4224]{1,0:T(8,128)(2,1)S(1)} %build_message.1), channel_id=1, source_target_pairs={{0,4},{1,17},{2,6},{3,19},{4,0},{5,21},{6,2},{7,23},{8,12},{9,25},... | collective-permute-start | bytes 202760 | tf_op jit(solution)/shard_map/ppermute | solution.py:367
  7.3 3.8 %prefetch.1 = (bf16[768,2048]{1,0:T(8,128)(2,1)S(1)}, bf16[768,2048]{1,0:T(8,128)(2,1)S(1)}, bf16[768,2048]{1,0:T(8,128)(2,1)S(1)}) custom-call(bf16[768,2048]{1,0:T(8,128)(2,1)} %bitcast.14, bf16[768,2048]{1,0:T(8,128)(2,1)} %bitcast.15, bf16[768,2048]{1,0:T(8,128)(2,1)} %bitcast.16), custom_call_target="tpu_custom_call" | custom-call | tf_op jit(solution)/shard_map/prefetch/pallas_call | solution.py:183
  11.1 0.0 collective-permute-done.2
  11.2 0.7 %collective-permute-done.1 = bf16[8,4224]{1,0:T(8,128)(2,1)S(1)} collective-permute-done((bf16[8,4224]{1,0:T(8,128)(2,1)S(1)}, bf16[8,4224]{1,0:T(8,128)(2,1)S(1)}, u32[]{:S(2)}, u32[]{:S(2)}) %collective-permute-start.1) | collective-permute-done | bytes 67616 | tf_op jit(solution)/shard_map/ppermute | solution.py:367
  11.9 0.0 collective-permute-done
  12.0 1.6 %collective-permute-start.4 = (bf16[32,4224]{1,0:T(8,128)(2,1)S(1)}, bf16[32,4224]{1,0:T(8,128)(2,1)S(1)}, u32[]{:S(2)}, u32[]{:S(2)}) collective-permute-start(bf16[32,4224]{1,0:T(8,128)(2,1)S(1)} %constant_dynamic-update-slice_fusion), channel_id=1, source_target_pairs={{0,2},{1,9},{2,0},{3,11},{4,6},{5,13},{6,4},{7,15},{8,10},{9,1},{1... | collective-permute-start | bytes 811016 | tf_op jit(solution)/shard_map/ppermute | solution.py:367
  13.5 1.5 %collective-permute-start.3 = (bf16[32,4224]{1,0:T(8,128)(2,1)S(1)}, bf16[32,4224]{1,0:T(8,128)(2,1)S(1)}, u32[]{:S(2)}, u32[]{:S(2)}) collective-permute-start(bf16[32,4224]{1,0:T(8,128)(2,1)S(1)} %constant_dynamic-update-slice_fusion), channel_id=1, source_target_pairs={{0,16},{1,5},{2,18},{3,7},{4,20},{5,1},{6,22},{7,3},{8,24},{9,13},... | collective-permute-start | bytes 811016 | tf_op jit(solution)/shard_map/ppermute | solution.py:367
  15.0 0.5 %collective-permute-start.6 = (bf16[32,2176]{1,0:T(8,128)(2,1)S(1)}, bf16[32,2176]{1,0:T(8,128)(2,1)S(1)}, u32[]{:S(2)}, u32[]{:S(2)}) collective-permute-start(bf16[32,2176]{1,0:T(8,128)(2,1)S(1)} %slice.85), channel_id=1, source_target_pairs={{0,18},{1,13},{2,16},{3,15},{4,22},{5,9},{6,20},{7,11},{8,26},{9,5... | collective-permute-start | bytes 417800 | tf_op jit(solution)/shard_map/ppermute | solution.py:367
  15.6 0.1 collective-permute-start.7
  15.7 2.5 %collective-permute-start.5 = (bf16[32,2048]{1,0:T(8,128)(2,1)S(1)}, bf16[32,2048]{1,0:T(8,128)(2,1)S(1)}, u32[]{:S(2)}, u32[]{:S(2)}) collective-permute-start(bf16[32,2048]{1,0:T(8,128)(2,1)S(1)} %slice.82), channel_id=1, source_target_pairs={{0,18},{1,13},{2,16},{3,15},{4,22},{5,9},{6,20},{7,11},{8,26},{9,5... | collective-permute-start | bytes 393224 | tf_op jit(solution)/shard_map/ppermute | solution.py:367
  18.2 3.2 %collective-permute-done.6 = bf16[32,2176]{1,0:T(8,128)(2,1)S(1)} collective-permute-done((bf16[32,2176]{1,0:T(8,128)(2,1)S(1)}, bf16[32,2176]{1,0:T(8,128)(2,1)S(1)}, u32[]{:S(2)}, u32[]{:S(2)}) %collective-permute-start.6) | collective-permute-done | bytes 139296 | tf_op jit(solution)/shard_map/ppermute | solution.py:367
  21.4 0.0 collective-permute-start.10
  21.4 0.0 collective-permute-done.4
  21.5 0.6 %collective-permute-start.9 = (bf16[32,4224]{1,0:T(8,128)(2,1)S(1)}, bf16[32,4224]{1,0:T(8,128)(2,1)S(1)}, u32[]{:S(2)}, u32[]{:S(2)}) collective-permute-start(bf16[32,4224]{1,0:T(8,128)(2,1)S(1)} %collective-permute-done.4), channel_id=1, source_target_pairs={{0,1},{1,0},{2,3},{3,2},{4,5},{5,4},{6,7},{7,6},{8,9},{9,8},{10,11... | collective-permute-start | bytes 811016 | tf_op jit(solution)/shard_map/ppermute | solution.py:371
  22.0 0.0 collective-permute-done.3
  22.0 0.1 collective-permute-start.8
  22.2 0.0 collective-permute-done.7
  22.2 0.0 copy-start.2
  22.2 0.0 copy-start.1
  22.3 0.9 %collective-permute-done.9 = bf16[32,4224]{1,0:T(8,128)(2,1)S(1)} collective-permute-done((bf16[32,4224]{1,0:T(8,128)(2,1)S(1)}, bf16[32,4224]{1,0:T(8,128)(2,1)S(1)}, u32[]{:S(2)}, u32[]{:S(2)}) %collective-permute-start.9) | collective-permute-done | bytes 270368 | tf_op jit(solution)/shard_map/ppermute | solution.py:371
  23.2 0.4 collective-permute-done.8
  23.7 0.0 collective-permute-done.10
  23.8 2.9 %forward.1 = (bf16[128,2048]{1,0:T(8,128)(2,1)S(1)}, f32[128,768]{1,0:T(8,128)S(1)}, f32[128,768]{1,0:T(8,128)S(1)}, f32[128,768]{1,0:T(8,128)S(1)}, bf16[128,76...) custom-call(s32[2,16]{1,0:T(2,128)S(1)} %copy-done.1, ...), custom_call_target="tpu_custom_call" | custom-call | flops 1 | bytes 1 | tf_op jit(solution)/shard_map/forward/pallas_call | solution.py:418
  26.7 0.0 slice-start
  26.7 0.0 collective-permute-done.5
  26.7 0.4 collective-permute-start.11
  27.1 1.0 %collective-permute-done.11 = bf16[32,2048]{1,0:T(8,128)(2,1)S(1)} collective-permute-done((bf16[32,2048]{1,0:T(8,128)(2,1)S(1)}, bf16[32,2048]{1,0:T(8,128)(2,1)S(1)}, u32[]{:S(2)}, u32[]{:S(2)}) %collective-permute-start.11) | collective-permute-done | bytes 131104 | tf_op jit(solution)/shard_map/ppermute | solution.py:371
  28.2 4.2 %backward.1 = (bf16[128,2176]{1,0:T(8,128)(2,1)S(1)}, bf16[128,2176]{1,0:T(8,128)(2,1)S(1)}, bf16[128,2048]{1,0:T(8,128)(2,1)S(1)}, bf16[128,768]{1,0:T(8,128)(2,1)S(1)}, bf16[128,768]{1,0:T(8,128)(2,1)S(1)}) custom-call(s32[2,16]{1,0:T(2,128)S(1)} %copy-done.1, bf16[128,2048]{1,0:T(8,128)(2,1)S(1)} %pad_maximum_fusion.2.near_ref, ...), custom_call_target="tpu_custom_call" | custom-call | tf_op jit(solution)/shard_map/backward/pallas_call | solution.py:433
  32.3 0.4 collective-permute-start.12
  32.7 1.7 %collective-permute-done.12 = bf16[128,2176]{1,0:T(8,128)(2,1)S(1)} collective-permute-done((bf16[128,2176]{1,0:T(8,128)(2,1)S(1)}, bf16[128,2176]{1,0:T(8,128)(2,1)S(1)}, u32[]{:S(2)}, u32[]{:S(2)}) %collective-permute-start.12) | collective-permute-done | bytes 557088 | tf_op jit(solution)/shard_map/ppermute | solution.py:371
  34.3 0.1 add_convert_fusion
  34.5 2.5 %collective-permute-start.15 = (bf16[32,2176]{1,0:T(8,128)(2,1)S(1)}, bf16[32,2176]{1,0:T(8,128)(2,1)S(1)}, u32[]{:S(2)}, u32[]{:S(2)}) collective-permute-start(bf16[32,2176]{1,0:T(8,128)(2,1)S(1)} %get-tuple-element.81), channel_id=1, source_target_pairs={{0,18},{1,13},{2,16},{3,15},{4,22},{5,9},{6,20},{7,11},{8,26},{9,5... | collective-permute-start | bytes 417800 | tf_op jit(solution)/shard_map/ppermute | solution.py:367
  37.0 0.5 collective-permute-start.14
  37.5 0.5 %collective-permute-start.13 = (bf16[32,2176]{1,0:T(8,128)(2,1)S(1)}, bf16[32,2176]{1,0:T(8,128)(2,1)S(1)}, u32[]{:S(2)}, u32[]{:S(2)}) collective-permute-start(bf16[32,2176]{1,0:T(8,128)(2,1)S(1)} %get-tuple-element.83), channel_id=1, source_target_pairs={{0,16},{1,5},{2,18},{3,7},{4,20},{5,1},{6,22},{7,3},{8,24},{9,13},... | collective-permute-start | bytes 417800 | tf_op jit(solution)/shard_map/ppermute | solution.py:367
  38.1 3.2 %weight_grads.2 = (bf16[768,2048]{1,0:T(8,128)(2,1)}, bf16[768,2048]{1,0:T(8,128)(2,1)}) custom-call(bf16[128,768]{1,0:T(8,128)(2,1)S(1)} %get-tuple-element.61.refs_0_, bf16[128,2048]{1,0:T(8,128)(2,1)S(1)} %get-tuple-element.62.refs_1_.refs_3_, bf16[128,768]{1,0:T(8,128)(2,1)S(1)} %get-tuple-element.63.refs_2_, ...), custom_call_target="tpu_custom_call" | custom-call | tf_op jit(solution)/shard_map/weight_grads/pallas_call | solution.py:292
  41.3 0.8 %collective-permute-done.14 = bf16[32,2176]{1,0:T(8,128)(2,1)S(1)} collective-permute-done((bf16[32,2176]{1,0:T(8,128)(2,1)S(1)}, bf16[32,2176]{1,0:T(8,128)(2,1)S(1)}, u32[]{:S(2)}, u32[]{:S(2)}) %collective-permute-start.14) | collective-permute-done | bytes 139296 | tf_op jit(solution)/shard_map/ppermute | solution.py:367
  42.1 0.5 collective-permute-done.13
  42.6 0.1 add_convert_fusion.1
  42.7 3.1 %collective-permute-start.18 = (bf16[8,2176]{1,0:T(8,128)(2,1)S(1)}, bf16[8,2176]{1,0:T(8,128)(2,1)S(1)}, u32[]{:S(2)}, u32[]{:S(2)}) collective-permute-start(bf16[8,2176]{1,0:T(8,128)(2,1)S(1)} %get-tuple-element.85), channel_id=1, source_target_pairs={{0,12},{1,19},{2,14},{3,17},{4,8},{5,23},{6,10},{7,21},{8,4},{9,27... | collective-permute-start | bytes 104456 | tf_op jit(solution)/shard_map/ppermute | solution.py:367
  45.8 1.0 %collective-permute-start.17 = (bf16[8,2176]{1,0:T(8,128)(2,1)S(1)}, bf16[8,2176]{1,0:T(8,128)(2,1)S(1)}, u32[]{:S(2)}, u32[]{:S(2)}) collective-permute-start(bf16[8,2176]{1,0:T(8,128)(2,1)S(1)} %get-tuple-element.86), channel_id=1, source_target_pairs={{0,8},{1,3},{2,10},{3,1},{4,12},{5,7},{6,14},{7,5},{8,0},{9,11},{1... | collective-permute-start | bytes 104456 | tf_op jit(solution)/shard_map/ppermute | solution.py:367
  46.8 0.5 collective-permute-start.16
  47.3 2.1 %weight_grads.3 = bf16[768,2048]{1,0:T(8,128)(2,1)} custom-call(bf16[128,768]{1,0:T(8,128)(2,1)S(1)} %get-tuple-element.70.refs_0_, bf16[128,2048]{1,0:T(8,128)(2,1)S(1)} %get-tuple-element.71.refs_1_), custom_call_target="tpu_custom_call" | custom-call | tf_op jit(solution)/shard_map/weight_grads/pallas_call | solution.py:292
  49.5 1.2 %collective-permute-done.17.c_ref = bf16[8,2176]{1,0:T(8,128)(2,1)S(1)} collective-permute-done((bf16[8,2176]{1,0:T(8,128)(2,1)S(1)}, bf16[8,2176]{1,0:T(8,128)(2,1)S(1)}, u32[]{:S(2)}, u32[]{:S(2)}) %collective-permute-start.17) | collective-permute-done | bytes 34848 | tf_op jit(solution)/shard_map/ppermute | solution.py:367
  50.7 0.4 collective-permute-done.16.b_ref
  51.0 0.8 %finish.1 = (bf16[8,2048]{1,0:T(8,128)(2,1)}, f32[8,8]{1,0:T(8,128)}) custom-call(bf16[8,2176]{1,0:T(8,128)(2,1)S(1)} %get-tuple-element.72.a_ref, bf16[8,2176]{1,0:T(8,128)(2,1)S(1)} %collective-permute-done.16.b_ref, bf16[8,2176]{1,0:T(8,128)(2,1)S(1)} %collective-permute-done.17.c_ref, bf16[8,2176]{1,0:T(8,128)(2,1)S(1)} %collective-permute-done.18.d_ref, ...), custom_call_target="tpu_custom_call" | custom-call | tf_op jit(solution)/shard_map/finish/pallas_call | solution.py:452
  (34 shorter events, 0.4 us)
Async XLA Ops:
  1.6 9.6 %collective-permute-start.2 = (bf16[8,4224]{1,0:T(8,128)(2,1)S(1)}, bf16[8,4224]{1,0:T(8,128)(2,1)S(1)}, u32[]{:S(2)}, u32[]{:S(2)}) collective-permute-start(bf16[8,4224]{1,0:T(8,128)(2,1)S(1)} %build_message.1), channel_id=1, source_target_pairs={{0,12},{1,19},{2,14},{3,17},{4,8},{5,23},{6,10},{7,21},{8,4},{9,27... | collective-permute-start | bytes 202760 | tf_op jit(solution)/shard_map/ppermute | solution.py:367
  6.7 5.2 %collective-permute-start.1 = (bf16[8,4224]{1,0:T(8,128)(2,1)S(1)}, bf16[8,4224]{1,0:T(8,128)(2,1)S(1)}, u32[]{:S(2)}, u32[]{:S(2)}) collective-permute-start(bf16[8,4224]{1,0:T(8,128)(2,1)S(1)} %build_message.1), channel_id=1, source_target_pairs={{0,8},{1,3},{2,10},{3,1},{4,12},{5,7},{6,14},{7,5},{8,0},{9,11},{1... | collective-permute-start | bytes 202760 | tf_op jit(solution)/shard_map/ppermute | solution.py:367
  6.7 5.2 %collective-permute-start = (bf16[8,4224]{1,0:T(8,128)(2,1)S(1)}, bf16[8,4224]{1,0:T(8,128)(2,1)S(1)}, u32[]{:S(2)}, u32[]{:S(2)}) collective-permute-start(bf16[8,4224]{1,0:T(8,128)(2,1)S(1)} %build_message.1), channel_id=1, source_target_pairs={{0,4},{1,17},{2,6},{3,19},{4,0},{5,21},{6,2},{7,23},{8,12},{9,25},... | collective-permute-start | bytes 202760 | tf_op jit(solution)/shard_map/ppermute | solution.py:367
  12.0 9.5 %collective-permute-start.4 = (bf16[32,4224]{1,0:T(8,128)(2,1)S(1)}, bf16[32,4224]{1,0:T(8,128)(2,1)S(1)}, u32[]{:S(2)}, u32[]{:S(2)}) collective-permute-start(bf16[32,4224]{1,0:T(8,128)(2,1)S(1)} %constant_dynamic-update-slice_fusion), channel_id=1, source_target_pairs={{0,2},{1,9},{2,0},{3,11},{4,6},{5,13},{6,4},{7,15},{8,10},{9,1},{1... | collective-permute-start | bytes 811016 | tf_op jit(solution)/shard_map/ppermute | solution.py:367
  13.5 8.5 %collective-permute-start.3 = (bf16[32,4224]{1,0:T(8,128)(2,1)S(1)}, bf16[32,4224]{1,0:T(8,128)(2,1)S(1)}, u32[]{:S(2)}, u32[]{:S(2)}) collective-permute-start(bf16[32,4224]{1,0:T(8,128)(2,1)S(1)} %constant_dynamic-update-slice_fusion), channel_id=1, source_target_pairs={{0,16},{1,5},{2,18},{3,7},{4,20},{5,1},{6,22},{7,3},{8,24},{9,13},... | collective-permute-start | bytes 811016 | tf_op jit(solution)/shard_map/ppermute | solution.py:367
  15.0 6.4 %collective-permute-start.6 = (bf16[32,2176]{1,0:T(8,128)(2,1)S(1)}, bf16[32,2176]{1,0:T(8,128)(2,1)S(1)}, u32[]{:S(2)}, u32[]{:S(2)}) collective-permute-start(bf16[32,2176]{1,0:T(8,128)(2,1)S(1)} %slice.85), channel_id=1, source_target_pairs={{0,18},{1,13},{2,16},{3,15},{4,22},{5,9},{6,20},{7,11},{8,26},{9,5... | collective-permute-start | bytes 417800 | tf_op jit(solution)/shard_map/ppermute | solution.py:367
  15.6 6.6 %collective-permute-start.7 = (bf16[32,4224]{1,0:T(8,128)(2,1)S(1)}, bf16[32,4224]{1,0:T(8,128)(2,1)S(1)}, u32[]{:S(2)}, u32[]{:S(2)}) collective-permute-start(bf16[32,4224]{1,0:T(8,128)(2,1)S(1)} %constant_dynamic-update-slice_fusion), channel_id=1, source_target_pairs={{0,1},{1,0},{2,3},{3,2},{4,5},{5,4},{6,7},{7,6},{8,9},{9,8},{10,11... | collective-permute-start | bytes 811016 | tf_op jit(solution)/shard_map/ppermute | solution.py:371
  15.7 11.0 %collective-permute-start.5 = (bf16[32,2048]{1,0:T(8,128)(2,1)S(1)}, bf16[32,2048]{1,0:T(8,128)(2,1)S(1)}, u32[]{:S(2)}, u32[]{:S(2)}) collective-permute-start(bf16[32,2048]{1,0:T(8,128)(2,1)S(1)} %slice.82), channel_id=1, source_target_pairs={{0,18},{1,13},{2,16},{3,15},{4,22},{5,9},{6,20},{7,11},{8,26},{9,5... | collective-permute-start | bytes 393224 | tf_op jit(solution)/shard_map/ppermute | solution.py:367
  21.4 2.2 %collective-permute-start.10 = (bf16[32,2176]{1,0:T(8,128)(2,1)S(1)}, bf16[32,2176]{1,0:T(8,128)(2,1)S(1)}, u32[]{:S(2)}, u32[]{:S(2)}) collective-permute-start(bf16[32,2176]{1,0:T(8,128)(2,1)S(1)} %collective-permute-done.6), channel_id=1, source_target_pairs={{0,1},{1,0},{2,3},{3,2},{4,5},{5,4},{6,7},{7,6},{8,9},{9,8},{10,11... | collective-permute-start | bytes 417800 | tf_op jit(solution)/shard_map/ppermute | solution.py:371
  21.5 1.7 %collective-permute-start.9 = (bf16[32,4224]{1,0:T(8,128)(2,1)S(1)}, bf16[32,4224]{1,0:T(8,128)(2,1)S(1)}, u32[]{:S(2)}, u32[]{:S(2)}) collective-permute-start(bf16[32,4224]{1,0:T(8,128)(2,1)S(1)} %collective-permute-done.4), channel_id=1, source_target_pairs={{0,1},{1,0},{2,3},{3,2},{4,5},{5,4},{6,7},{7,6},{8,9},{9,8},{10,11... | collective-permute-start | bytes 811016 | tf_op jit(solution)/shard_map/ppermute | solution.py:371
  22.0 1.6 %collective-permute-start.8 = (bf16[32,4224]{1,0:T(8,128)(2,1)S(1)}, bf16[32,4224]{1,0:T(8,128)(2,1)S(1)}, u32[]{:S(2)}, u32[]{:S(2)}) collective-permute-start(bf16[32,4224]{1,0:T(8,128)(2,1)S(1)} %collective-permute-done.3), channel_id=1, source_target_pairs={{0,1},{1,0},{2,3},{3,2},{4,5},{5,4},{6,7},{7,6},{8,9},{9,8},{10,11... | collective-permute-start | bytes 811016 | tf_op jit(solution)/shard_map/ppermute | solution.py:371
  22.2 1.5 %copy-start.2 = (bf16[32,4224]{1,0:T(8,128)(2,1)}, bf16[32,4224]{1,0:T(8,128)(2,1)S(1)}, u32[]{:S(2)}) copy-start(bf16[32,4224]{1,0:T(8,128)(2,1)S(1)} %collective-permute-done.7) | copy-start | bytes 811012
  22.2 1.5 %copy-start.1 = (s32[2,16]{1,0:T(2,128)S(1)}, s32[2,16]{1,0:T(2,128)}, u32[]{:S(2)}) copy-start(s32[2,16]{1,0:T(2,128)} %shard_ref.3) | copy-start | bytes 388
  23.2 3.9 %copy-start.3 = (bf16[32,4224]{1,0:T(8,128)(2,1)}, bf16[32,4224]{1,0:T(8,128)(2,1)S(1)}, u32[]{:S(2)}) copy-start(bf16[32,4224]{1,0:T(8,128)(2,1)S(1)} %collective-permute-done.9) | copy-start | bytes 811012
  23.7 3.4 %copy-start.4 = (bf16[32,4224]{1,0:T(8,128)(2,1)}, bf16[32,4224]{1,0:T(8,128)(2,1)S(1)}, u32[]{:S(2)}) copy-start(bf16[32,4224]{1,0:T(8,128)(2,1)S(1)} %collective-permute-done.8) | copy-start | bytes 811012
  26.7 1.4 %slice-start = ((bf16[32,4224]{1,0:T(8,128)(2,1)}), bf16[32,2048]{1,0:T(8,128)(2,1)S(1)}, s32[]{:S(2)}) async-start(bf16[32,4224]{1,0:T(8,128)(2,1)} %copy-done.2), calls=%async_computation | async-start | bytes 262144 | tf_op jit(solution)/shard_map/slice | solution.py:432
  26.7 1.4 %collective-permute-start.11 = (bf16[32,2048]{1,0:T(8,128)(2,1)S(1)}, bf16[32,2048]{1,0:T(8,128)(2,1)S(1)}, u32[]{:S(2)}, u32[]{:S(2)}) collective-permute-start(bf16[32,2048]{1,0:T(8,128)(2,1)S(1)} %collective-permute-done.5), channel_id=1, source_target_pairs={{0,1},{1,0},{2,3},{3,2},{4,5},{5,4},{6,7},{7,6},{8,9},{9,8},{10,11... | collective-permute-start | bytes 393224 | tf_op jit(solution)/shard_map/ppermute | solution.py:371
  27.1 1.0 %slice-start.1 = ((bf16[32,4224]{1,0:T(8,128)(2,1)}), bf16[32,2048]{1,0:T(8,128)(2,1)S(1)}, s32[]{:S(2)}) async-start(bf16[32,4224]{1,0:T(8,128)(2,1)} %copy-done.3), calls=%async_computation.1 | async-start | bytes 262144 | tf_op jit(solution)/shard_map/slice | solution.py:432
  27.1 1.0 %slice-start.2 = ((bf16[32,4224]{1,0:T(8,128)(2,1)}), bf16[32,2048]{1,0:T(8,128)(2,1)S(1)}, s32[]{:S(2)}) async-start(bf16[32,4224]{1,0:T(8,128)(2,1)} %copy-done.4), calls=%async_computation.2 | async-start | bytes 262144 | tf_op jit(solution)/shard_map/slice | solution.py:432
  32.3 2.0 %collective-permute-start.12 = (bf16[128,2176]{1,0:T(8,128)(2,1)S(1)}, bf16[128,2176]{1,0:T(8,128)(2,1)S(1)}, u32[]{:S(2)}, u32[]{:S(2)}) collective-permute-start(bf16[128,2176]{1,0:T(8,128)(2,1)S(1)} %get-tuple-element.60), channel_id=1, source_target_pairs={{0,1},{1,0},{2,3},{3,2},{4,5},{5,4},{6,7},{7,6},{8,9},{9,8},{10,11... | collective-permute-start | bytes 1671176 | tf_op jit(solution)/shard_map/ppermute | solution.py:371
  34.5 6.7 %collective-permute-start.15 = (bf16[32,2176]{1,0:T(8,128)(2,1)S(1)}, bf16[32,2176]{1,0:T(8,128)(2,1)S(1)}, u32[]{:S(2)}, u32[]{:S(2)}) collective-permute-start(bf16[32,2176]{1,0:T(8,128)(2,1)S(1)} %get-tuple-element.81), channel_id=1, source_target_pairs={{0,18},{1,13},{2,16},{3,15},{4,22},{5,9},{6,20},{7,11},{8,26},{9,5... | collective-permute-start | bytes 417800 | tf_op jit(solution)/shard_map/ppermute | solution.py:367
  37.0 5.1 %collective-permute-start.14 = (bf16[32,2176]{1,0:T(8,128)(2,1)S(1)}, bf16[32,2176]{1,0:T(8,128)(2,1)S(1)}, u32[]{:S(2)}, u32[]{:S(2)}) collective-permute-start(bf16[32,2176]{1,0:T(8,128)(2,1)S(1)} %get-tuple-element.82), channel_id=1, source_target_pairs={{0,2},{1,9},{2,0},{3,11},{4,6},{5,13},{6,4},{7,15},{8,10},{9,1},{1... | collective-permute-start | bytes 417800 | tf_op jit(solution)/shard_map/ppermute | solution.py:367
  37.5 5.1 %collective-permute-start.13 = (bf16[32,2176]{1,0:T(8,128)(2,1)S(1)}, bf16[32,2176]{1,0:T(8,128)(2,1)S(1)}, u32[]{:S(2)}, u32[]{:S(2)}) collective-permute-start(bf16[32,2176]{1,0:T(8,128)(2,1)S(1)} %get-tuple-element.83), channel_id=1, source_target_pairs={{0,16},{1,5},{2,18},{3,7},{4,20},{5,1},{6,22},{7,3},{8,24},{9,13},... | collective-permute-start | bytes 417800 | tf_op jit(solution)/shard_map/ppermute | solution.py:367
  42.7 6.8 %collective-permute-start.18 = (bf16[8,2176]{1,0:T(8,128)(2,1)S(1)}, bf16[8,2176]{1,0:T(8,128)(2,1)S(1)}, u32[]{:S(2)}, u32[]{:S(2)}) collective-permute-start(bf16[8,2176]{1,0:T(8,128)(2,1)S(1)} %get-tuple-element.85), channel_id=1, source_target_pairs={{0,12},{1,19},{2,14},{3,17},{4,8},{5,23},{6,10},{7,21},{8,4},{9,27... | collective-permute-start | bytes 104456 | tf_op jit(solution)/shard_map/ppermute | solution.py:367
  45.8 4.9 %collective-permute-start.17 = (bf16[8,2176]{1,0:T(8,128)(2,1)S(1)}, bf16[8,2176]{1,0:T(8,128)(2,1)S(1)}, u32[]{:S(2)}, u32[]{:S(2)}) collective-permute-start(bf16[8,2176]{1,0:T(8,128)(2,1)S(1)} %get-tuple-element.86), channel_id=1, source_target_pairs={{0,8},{1,3},{2,10},{3,1},{4,12},{5,7},{6,14},{7,5},{8,0},{9,11},{1... | collective-permute-start | bytes 104456 | tf_op jit(solution)/shard_map/ppermute | solution.py:367
  46.8 4.2 %collective-permute-start.16 = (bf16[8,2176]{1,0:T(8,128)(2,1)S(1)}, bf16[8,2176]{1,0:T(8,128)(2,1)S(1)}, u32[]{:S(2)}, u32[]{:S(2)}) collective-permute-start(bf16[8,2176]{1,0:T(8,128)(2,1)S(1)} %get-tuple-element.87), channel_id=1, source_target_pairs={{0,4},{1,17},{2,6},{3,19},{4,0},{5,21},{6,2},{7,23},{8,12},{9,25},... | collective-permute-start | bytes 104456 | tf_op jit(solution)/shard_map/ppermute | solution.py:367
  47.3 3.7 %copy-start = (s32[1,8,8]{2,1,0:T(8,128)S(1)}, s32[1,8,8]{2,1,0:T(8,128)}, u32[]{:S(2)}) copy-start(s32[1,8,8]{2,1,0:T(8,128)} %param.11) | copy-start | bytes 772

commit v4 on v3

--- a/solution.py
+++ b/solution.py
@@ -193,10 +193,9 @@
 
 def forward_kernel(
     shard_ref, near_ref, far_ref, wg_ref, wu_ref,
-    rin_ref, hidden_ref, gfac_ref, ufac_ref, gw_ref, snear_ref, sfar_ref,
+    rin_ref, hidden_ref, gfac_ref, ufac_ref, gw_ref, select_ref,
 ):
     which = my_expert(shard_ref)
-    core = lax.axis_index("core")
     half = near_ref.shape[0]
     slots, width = rin_ref.shape
     total = 2 * half
@@ -217,17 +216,10 @@
     select_f = jnp.where(hit, 1.0, 0.0)
     select = select_f.astype(BF16)
     row_gates = jnp.sum(select_f * gate_row[:1], axis=1, keepdims=True)
-    s_near, s_far = select[:, :half], select[:, half:]
-    rows_in = (
-        dot_on(s_near, near_ref[:, :width], 1, 0) + dot_on(s_far, far_ref[:, :width], 1, 0)
-    ).astype(BF16)
+    both = jnp.concatenate([near_ref[:, :width], far_ref[:, :width]], axis=0)
+    rows_in = dot_on(select, both, 1, 0).astype(BF16)
     rin_ref[...] = rows_in
-    row = lax.broadcasted_iota(jnp.int32, (half, half), 0)
-    col = lax.broadcasted_iota(jnp.int32, (half, half), 1)
-    turned = (col % 8) + 8 * ((col // 32) + 4 * ((col // 8) % 4))
-    turn = jnp.where(row == turned, 1.0, 0.0).astype(BF16)
-    for part, ref, turn_it in ((s_near, snear_ref, core > 0), (s_far, sfar_ref, core == 0)):
-        ref[...] = jnp.where(turn_it & (MIXED != MIXED_T), dot_on(part, turn, 1, 0), part.astype(F32)).astype(BF16)
+    select_ref[...] = select
     gate_pre = dot_on(rows_in, wg_ref[...], 1, 1)
     up_pre = dot_on(rows_in, wu_ref[...], 1, 1)
     sigmoid = jax.nn.sigmoid(gate_pre)
@@ -240,16 +232,16 @@
 
 
 def backward_kernel(
-    shard_ref, near_ref, far_ref, snear_ref, sfar_ref, hidden_ref, gfac_ref, ufac_ref,
+    shard_ref, near_ref, far_ref, last_ref, select_ref, hidden_ref, gfac_ref, ufac_ref,
     wg_ref, wu_ref, wd_ref,
     ret_near_ref, ret_far_ref, rgrad_ref, gg_ref, ug_ref,
 ):
     which = my_expert(shard_ref)
     slots, width = rgrad_ref.shape
-    s_near, s_far = snear_ref[...], sfar_ref[...]
-    rows_grad = (dot_on(s_near, near_ref[...], 1, 0) + dot_on(s_far, far_ref[...], 1, 0)).astype(
-        BF16
-    )
+    select = select_ref[...]
+    half = near_ref.shape[0]
+    both = jnp.concatenate([near_ref[...], far_ref[...], last_ref[...]], axis=0)
+    rows_grad = dot_on(select, both, 1, 0).astype(BF16)
     rgrad_ref[...] = rows_grad
     back = dot_on(rows_grad, wd_ref[...], 1, 1)
     gate_grad = (back * gfac_ref[...]).astype(BF16)
@@ -262,9 +254,9 @@
     ).astype(BF16)
     gate_lane = lax.broadcasted_iota(jnp.int32, (slots, LANES), 1)
     gate_cols = jnp.where(gate_lane == which, gate_part, 0.0).astype(BF16)
-    for s, ref in ((s_near, ret_near_ref), (s_far, ret_far_ref)):
-        ref[:, :width] = dot_on(s, input_part, 0, 0).astype(BF16)
-        ref[:, width:] = dot_on(s, gate_cols, 0, 0).astype(BF16)
+    terms = jnp.concatenate([input_part, gate_cols], axis=1)
+    ret_far_ref[...] = dot_on(select[:, half:], terms, 0, 0).astype(BF16)
+    ret_near_ref[...] = dot_on(select[:, :half], terms, 0, 0).astype(BF16)
 
 
 def weight_kernel(tile, count, *refs):
@@ -298,7 +290,7 @@
             pltpu.VMEM((count, hidden, width), BF16),
             pltpu.SemaphoreType.DMA((count, hidden // tile)),
         ],
-        compiler_params=limit(20),
+        compiler_params=limit(3 + 4 * count),
         name="weight_grads",
     )(*flat)
 
@@ -330,7 +322,6 @@
 
 
 MIXED = True
-MIXED_T = MIXED
 AXES = ("x", "z", "y", "core")
 
 
@@ -413,23 +404,24 @@
     far_pieces = [swap_core(v) for v in pieces]
     t_near = join([v[:, :back_width] for v in pieces] + [t_last])
     t_far = join([v[:, :back_width] for v in far_pieces] + [swap_core(t_last)])
+    g_far = join([v[:, back_width:] for v in far_pieces])
+    g_last, g_far, _ = lax.optimization_barrier((g_last, g_far, t_far))
+    g_near = join([v[:, back_width:] for v in pieces] + [g_last])
+    g_far_last = swap_core(g_last)
     half = t_near.shape[0]
     slots = 16 * CAP
-    rows_in, act, gate_fac, up_fac, weighted, s_near, s_far = pl.pallas_call(
+    rows_in, act, gate_fac, up_fac, weighted, select = pl.pallas_call(
         forward_kernel,
         in_specs=[whole(pltpu.SMEM)] + [whole()] * 4,
-        out_specs=[whole()] * 7,
+        out_specs=[whole()] * 6,
         out_shape=[pltpu.VMEM((slots, width), BF16)]
         + [pltpu.VMEM((slots, hidden), F32)] * 3
         + [pltpu.VMEM((slots, hidden), BF16)]
-        + [pltpu.VMEM((slots, half), BF16)] * 2,
-        compiler_params=limit(16),
+        + [pltpu.VMEM((slots, 2 * half), BF16)],
+        compiler_params=limit(8),
         cost_estimate=pl.CostEstimate(flops=1, transcendentals=0, bytes_accessed=1),
         name="forward",
     )(shard_of, in_vmem(t_near), in_vmem(t_far), wg, wu)
-    g_last, _ = lax.optimization_barrier((g_last, s_near))
-    g_near = join([v[:, back_width:] for v in pieces] + [g_last])
-    g_far = join([v[:, back_width:] for v in far_pieces] + [swap_core(g_last)])
     ret_near, ret_far, rows_grad, gate_grad, up_grad = pl.pallas_call(
         backward_kernel,
         in_specs=[whole(pltpu.SMEM)] + [whole()] * 10,
@@ -437,9 +429,9 @@
         out_shape=[pltpu.VMEM((half, back_width), BF16)] * 2
         + [pltpu.VMEM((slots, width), BF16)]
         + [pltpu.VMEM((slots, hidden), BF16)] * 2,
-        compiler_params=limit(16),
+        compiler_params=limit(8),
         name="backward",
-    )(shard_of, in_vmem(g_near), in_vmem(g_far), s_near, s_far, act, gate_fac, up_fac, wg, wu, wd)
+    )(shard_of, in_vmem(g_near), in_vmem(g_far), in_vmem(g_far_last), select, act, gate_fac, up_fac, wg, wu, wd)
     peer = swap_core(ret_far)
     summed = (ret_near.astype(F32) + peer.astype(F32)).astype(BF16)
     got = fold(summed, True, MIXED)

time: 52 us -> 51.3 us (0.987)
  waiting for transfers between devices: 10.9 us -> 9.87 us
    ppermute x6, waiting for transfers between devices: 4.02 us -> 3.02 us  [swap_core(): return lax.ppermute(value, AXES, [(d, d ^ 1) for d in range(32)])]
  transfers between devices with their start and end apart: 19 -> 19, of which waited for: 10 -> 9; matrix products, arithmetic and copies ran while one was open for 0% -> 1% of each run, Pallas kernels for 23% -> 24%
where the time goes in v4:
time: 51.3 us; the launch traced here: 51.1 us
  starting transfers between devices  21.5 us (42%)
  Pallas kernels  18.1 us (35%)
  waiting for transfers between devices  9.87 us (19%)
  between operations  0.9 us (2%)
    ppermute x13, starting transfers between devices, swap(): return lax.ppermute(value, AXES, pairs)  20.1 us
    ppermute x13, waiting for transfers between devices, swap(): return lax.ppermute(value, AXES, pairs)  6.86 us
    pallas_call x2, Pallas kernels, weight_grads_of(): pl.pallas_call(functools.partial(weight_kernel, tile, count), in_specs=[w...  5.31 us
    pallas_call x1, Pallas kernels, block_local(): pl.pallas_call(backward_kernel, in_specs=[whole(pltpu.SMEM)] + [whole()]...  4.08 us
    pallas_call x1, Pallas kernels, prefetch(): pl.pallas_call(prefetch_kernel, in_specs=[whole(pltpu.HBM)] * len(weights...  3.79 us
    pallas_call x1, Pallas kernels, block_local(): pl.pallas_call(forward_kernel, in_specs=[whole(pltpu.SMEM)] + [whole()] *...  3.17 us
    ppermute x6, waiting for transfers between devices, swap_core(): return lax.ppermute(value, AXES, [(d, d ^ 1) for d in range(32)])  3.02 us
    ppermute x6, starting transfers between devices, swap_core(): return lax.ppermute(value, AXES, [(d, d ^ 1) for d in range(32)])  1.48 us
  transfers between devices with their start and end apart: 19, of which 9 were waited for; matrix products, arithmetic and copies ran while one was open for 1% of the time, Pallas kernels for 24%

profile of v4, /device:TPU:0, one launch (start us, length us, event | category | flops | bytes accessed | tf_op | source)
XLA Modules:
  0.0 51.1 jit_solution(9948472056493553490)
XLA Ops:
  0.6 0.9 %build_message.1 = bf16[8,4224]{1,0:T(8,128)(2,1)S(1)} custom-call(bf16[8,2048]{1,0:T(8,128)(2,1)} %bitcast.18, bf16[8,2048]{1,0:T(8,128)(2,1)} %bitcast.19, bf16[8,8]{1,0:T(8,128)(2,1)} %bitcast.20, s32[8,8]{1,0:T(8,128)} %bitcast.12), custom_call_target="tpu_custom_call" | custom-call | tf_op jit(solution)/shard_map/build_message/pallas_call | solution.py:385
  1.6 5.1 %collective-permute-start.2 = (bf16[8,4224]{1,0:T(8,128)(2,1)S(1)}, bf16[8,4224]{1,0:T(8,128)(2,1)S(1)}, u32[]{:S(2)}, u32[]{:S(2)}) collective-permute-start(bf16[8,4224]{1,0:T(8,128)(2,1)S(1)} %build_message.1), channel_id=1, source_target_pairs={{0,12},{1,19},{2,14},{3,17},{4,8},{5,23},{6,10},{7,21},{8,4},{9,27... | collective-permute-start | bytes 202760 | tf_op jit(solution)/shard_map/ppermute | solution.py:358
  6.7 0.0 collective-permute-start.1
  6.7 0.6 %collective-permute-start = (bf16[8,4224]{1,0:T(8,128)(2,1)S(1)}, bf16[8,4224]{1,0:T(8,128)(2,1)S(1)}, u32[]{:S(2)}, u32[]{:S(2)}) collective-permute-start(bf16[8,4224]{1,0:T(8,128)(2,1)S(1)} %build_message.1), channel_id=1, source_target_pairs={{0,4},{1,17},{2,6},{3,19},{4,0},{5,21},{6,2},{7,23},{8,12},{9,25},... | collective-permute-start | bytes 202760 | tf_op jit(solution)/shard_map/ppermute | solution.py:358
  7.3 3.8 %prefetch.1 = (bf16[768,2048]{1,0:T(8,128)(2,1)S(1)}, bf16[768,2048]{1,0:T(8,128)(2,1)S(1)}, bf16[768,2048]{1,0:T(8,128)(2,1)S(1)}) custom-call(bf16[768,2048]{1,0:T(8,128)(2,1)} %bitcast.14, bf16[768,2048]{1,0:T(8,128)(2,1)} %bitcast.15, bf16[768,2048]{1,0:T(8,128)(2,1)} %bitcast.16), custom_call_target="tpu_custom_call" | custom-call | tf_op jit(solution)/shard_map/prefetch/pallas_call | solution.py:183
  11.1 0.0 collective-permute-done.2
  11.2 0.7 %collective-permute-done.1 = bf16[8,4224]{1,0:T(8,128)(2,1)S(1)} collective-permute-done((bf16[8,4224]{1,0:T(8,128)(2,1)S(1)}, bf16[8,4224]{1,0:T(8,128)(2,1)S(1)}, u32[]{:S(2)}, u32[]{:S(2)}) %collective-permute-start.1) | collective-permute-done | bytes 67616 | tf_op jit(solution)/shard_map/ppermute | solution.py:358
  11.9 0.0 collective-permute-done
  12.0 1.6 %collective-permute-start.4 = (bf16[32,4224]{1,0:T(8,128)(2,1)S(1)}, bf16[32,4224]{1,0:T(8,128)(2,1)S(1)}, u32[]{:S(2)}, u32[]{:S(2)}) collective-permute-start(bf16[32,4224]{1,0:T(8,128)(2,1)S(1)} %constant_dynamic-update-slice_fusion), channel_id=1, source_target_pairs={{0,2},{1,9},{2,0},{3,11},{4,6},{5,13},{6,4},{7,15},{8,10},{9,1},{1... | collective-permute-start | bytes 811016 | tf_op jit(solution)/shard_map/ppermute | solution.py:358
  13.5 1.5 %collective-permute-start.3 = (bf16[32,4224]{1,0:T(8,128)(2,1)S(1)}, bf16[32,4224]{1,0:T(8,128)(2,1)S(1)}, u32[]{:S(2)}, u32[]{:S(2)}) collective-permute-start(bf16[32,4224]{1,0:T(8,128)(2,1)S(1)} %constant_dynamic-update-slice_fusion), channel_id=1, source_target_pairs={{0,16},{1,5},{2,18},{3,7},{4,20},{5,1},{6,22},{7,3},{8,24},{9,13},... | collective-permute-start | bytes 811016 | tf_op jit(solution)/shard_map/ppermute | solution.py:358
  15.0 0.5 %collective-permute-start.9 = (bf16[32,2176]{1,0:T(8,128)(2,1)S(1)}, bf16[32,2176]{1,0:T(8,128)(2,1)S(1)}, u32[]{:S(2)}, u32[]{:S(2)}) collective-permute-start(bf16[32,2176]{1,0:T(8,128)(2,1)S(1)} %slice.91), channel_id=1, source_target_pairs={{0,18},{1,13},{2,16},{3,15},{4,22},{5,9},{6,20},{7,11},{8,26},{9,5... | collective-permute-start | bytes 417800 | tf_op jit(solution)/shard_map/ppermute | solution.py:358
  15.6 0.1 collective-permute-start.6
  15.7 2.5 %collective-permute-start.5 = (bf16[32,2048]{1,0:T(8,128)(2,1)S(1)}, bf16[32,2048]{1,0:T(8,128)(2,1)S(1)}, u32[]{:S(2)}, u32[]{:S(2)}) collective-permute-start(bf16[32,2048]{1,0:T(8,128)(2,1)S(1)} %slice.82), channel_id=1, source_target_pairs={{0,18},{1,13},{2,16},{3,15},{4,22},{5,9},{6,20},{7,11},{8,26},{9,5... | collective-permute-start | bytes 393224 | tf_op jit(solution)/shard_map/ppermute | solution.py:358
  18.2 3.2 %collective-permute-done.9 = bf16[32,2176]{1,0:T(8,128)(2,1)S(1)} collective-permute-done((bf16[32,2176]{1,0:T(8,128)(2,1)S(1)}, bf16[32,2176]{1,0:T(8,128)(2,1)S(1)}, u32[]{:S(2)}, u32[]{:S(2)}) %collective-permute-start.9) | collective-permute-done | bytes 139296 | tf_op jit(solution)/shard_map/ppermute | solution.py:358
  21.4 0.0 collective-permute-start.10
  21.4 0.0 collective-permute-done.4
  21.5 0.6 %collective-permute-start.8 = (bf16[32,4224]{1,0:T(8,128)(2,1)S(1)}, bf16[32,4224]{1,0:T(8,128)(2,1)S(1)}, u32[]{:S(2)}, u32[]{:S(2)}) collective-permute-start(bf16[32,4224]{1,0:T(8,128)(2,1)S(1)} %collective-permute-done.4), channel_id=1, source_target_pairs={{0,1},{1,0},{2,3},{3,2},{4,5},{5,4},{6,7},{7,6},{8,9},{9,8},{10,11... | collective-permute-start | bytes 811016 | tf_op jit(solution)/shard_map/ppermute | solution.py:362
  22.0 0.0 collective-permute-done.3
  22.0 0.1 collective-permute-start.7
  22.2 0.0 collective-permute-done.6
  22.3 0.9 %collective-permute-done.8 = bf16[32,4224]{1,0:T(8,128)(2,1)S(1)} collective-permute-done((bf16[32,4224]{1,0:T(8,128)(2,1)S(1)}, bf16[32,4224]{1,0:T(8,128)(2,1)S(1)}, u32[]{:S(2)}, u32[]{:S(2)}) %collective-permute-start.8) | collective-permute-done | bytes 270368 | tf_op jit(solution)/shard_map/ppermute | solution.py:362
  23.2 0.4 collective-permute-done.7
  23.7 0.0 copy-start.1
  23.7 0.0 collective-permute-done.10
  23.8 0.0 collective-permute-done.5
  23.8 0.4 collective-permute-start.11
  24.2 0.2 copy-done.1
  24.4 3.2 %forward.1 = (bf16[128,2048]{1,0:T(8,128)(2,1)S(1)}, f32[128,768]{1,0:T(8,128)S(1)}, f32[128,768]{1,0:T(8,128)S(1)}, f32[128,768]{1,0:T(8,128)S(1)}, bf16[128,76...) custom-call(s32[2,16]{1,0:T(2,128)S(1)} %copy-done.1, bf16[128,2176]{1,0:T(8,128)(2,1)S(1)} %pad_maximum_fusion.1.near_ref, ...), custom_call_target="tpu_custom_call" | custom-call | flops 1 | bytes 1 | tf_op jit(solution)/shard_map/forward/pallas_call | solution.py:413
  27.6 0.0 collective-permute-done.11.last_ref
  27.6 4.1 %backward.1 = (bf16[128,2176]{1,0:T(8,128)(2,1)S(1)}, bf16[128,2176]{1,0:T(8,128)(2,1)S(1)}, bf16[128,2048]{1,0:T(8,128)(2,1)S(1)}, bf16[128,768]{1,0:T(8,128)(2,1)S(1)}, bf16[128,768]{1,0:T(8,128)(2,1)S(1)}) custom-call(s32[2,16]{1,0:T(2,128)S(1)} %copy-done.1, bf16[128,2048]{1,0:T(8,128)(2,1)S(1)} %pad_maximum_fusion.2.near_ref, ...), custom_call_target="tpu_custom_call" | custom-call | tf_op jit(solution)/shard_map/backward/pallas_call | solution.py:425
  31.7 0.4 collective-permute-start.12
  32.1 1.6 %collective-permute-done.12 = bf16[128,2176]{1,0:T(8,128)(2,1)S(1)} collective-permute-done((bf16[128,2176]{1,0:T(8,128)(2,1)S(1)}, bf16[128,2176]{1,0:T(8,128)(2,1)S(1)}, u32[]{:S(2)}, u32[]{:S(2)}) %collective-permute-start.12) | collective-permute-done | bytes 557088 | tf_op jit(solution)/shard_map/ppermute | solution.py:362
  33.7 0.1 add_convert_fusion
  33.9 2.5 %collective-permute-start.15 = (bf16[32,2176]{1,0:T(8,128)(2,1)S(1)}, bf16[32,2176]{1,0:T(8,128)(2,1)S(1)}, u32[]{:S(2)}, u32[]{:S(2)}) collective-permute-start(bf16[32,2176]{1,0:T(8,128)(2,1)S(1)} %get-tuple-element.81), channel_id=1, source_target_pairs={{0,18},{1,13},{2,16},{3,15},{4,22},{5,9},{6,20},{7,11},{8,26},{9,5... | collective-permute-start | bytes 417800 | tf_op jit(solution)/shard_map/ppermute | solution.py:358
  36.4 0.5 collective-permute-start.14
  36.9 0.5 %collective-permute-start.13 = (bf16[32,2176]{1,0:T(8,128)(2,1)S(1)}, bf16[32,2176]{1,0:T(8,128)(2,1)S(1)}, u32[]{:S(2)}, u32[]{:S(2)}) collective-permute-start(bf16[32,2176]{1,0:T(8,128)(2,1)S(1)} %get-tuple-element.83), channel_id=1, source_target_pairs={{0,16},{1,5},{2,18},{3,7},{4,20},{5,1},{6,22},{7,3},{8,24},{9,13},... | collective-permute-start | bytes 417800 | tf_op jit(solution)/shard_map/ppermute | solution.py:358
  37.4 3.2 %weight_grads.2 = (bf16[768,2048]{1,0:T(8,128)(2,1)}, bf16[768,2048]{1,0:T(8,128)(2,1)}) custom-call(bf16[128,768]{1,0:T(8,128)(2,1)S(1)} %get-tuple-element.61.refs_0_, bf16[128,2048]{1,0:T(8,128)(2,1)S(1)} %get-tuple-element.62.refs_1_.refs_3_, bf16[128,768]{1,0:T(8,128)(2,1)S(1)} %get-tuple-element.63.refs_2_, ...), custom_call_target="tpu_custom_call" | custom-call | tf_op jit(solution)/shard_map/weight_grads/pallas_call | solution.py:284
  40.6 0.0 collective-permute-done.15
  40.6 0.8 %collective-permute-done.14 = bf16[32,2176]{1,0:T(8,128)(2,1)S(1)} collective-permute-done((bf16[32,2176]{1,0:T(8,128)(2,1)S(1)}, bf16[32,2176]{1,0:T(8,128)(2,1)S(1)}, u32[]{:S(2)}, u32[]{:S(2)}) %collective-permute-start.14) | collective-permute-done | bytes 139296 | tf_op jit(solution)/shard_map/ppermute | solution.py:358
  41.5 0.5 collective-permute-done.13
  42.0 0.1 add_convert_fusion.1
  42.1 3.1 %collective-permute-start.18 = (bf16[8,2176]{1,0:T(8,128)(2,1)S(1)}, bf16[8,2176]{1,0:T(8,128)(2,1)S(1)}, u32[]{:S(2)}, u32[]{:S(2)}) collective-permute-start(bf16[8,2176]{1,0:T(8,128)(2,1)S(1)} %get-tuple-element.85), channel_id=1, source_target_pairs={{0,12},{1,19},{2,14},{3,17},{4,8},{5,23},{6,10},{7,21},{8,4},{9,27... | collective-permute-start | bytes 104456 | tf_op jit(solution)/shard_map/ppermute | solution.py:358
  45.2 1.0 %collective-permute-start.17 = (bf16[8,2176]{1,0:T(8,128)(2,1)S(1)}, bf16[8,2176]{1,0:T(8,128)(2,1)S(1)}, u32[]{:S(2)}, u32[]{:S(2)}) collective-permute-start(bf16[8,2176]{1,0:T(8,128)(2,1)S(1)} %get-tuple-element.86), channel_id=1, source_target_pairs={{0,8},{1,3},{2,10},{3,1},{4,12},{5,7},{6,14},{7,5},{8,0},{9,11},{1... | collective-permute-start | bytes 104456 | tf_op jit(solution)/shard_map/ppermute | solution.py:358
  46.2 0.5 collective-permute-start.16
  46.7 2.1 %weight_grads.3 = bf16[768,2048]{1,0:T(8,128)(2,1)} custom-call(bf16[128,768]{1,0:T(8,128)(2,1)S(1)} %get-tuple-element.70.refs_0_, bf16[128,2048]{1,0:T(8,128)(2,1)S(1)} %get-tuple-element.71.refs_1_), custom_call_target="tpu_custom_call" | custom-call | tf_op jit(solution)/shard_map/weight_grads/pallas_call | solution.py:284
  48.8 1.2 %collective-permute-done.17.c_ref = bf16[8,2176]{1,0:T(8,128)(2,1)S(1)} collective-permute-done((bf16[8,2176]{1,0:T(8,128)(2,1)S(1)}, bf16[8,2176]{1,0:T(8,128)(2,1)S(1)}, u32[]{:S(2)}, u32[]{:S(2)}) %collective-permute-start.17) | collective-permute-done | bytes 34848 | tf_op jit(solution)/shard_map/ppermute | solution.py:358
  50.0 0.4 collective-permute-done.16.b_ref
  50.4 0.8 %finish.1 = (bf16[8,2048]{1,0:T(8,128)(2,1)}, f32[8,8]{1,0:T(8,128)}) custom-call(bf16[8,2176]{1,0:T(8,128)(2,1)S(1)} %get-tuple-element.72.a_ref, bf16[8,2176]{1,0:T(8,128)(2,1)S(1)} %collective-permute-done.16.b_ref, bf16[8,2176]{1,0:T(8,128)(2,1)S(1)} %collective-permute-done.17.c_ref, bf16[8,2176]{1,0:T(8,128)(2,1)S(1)} %collective-permute-done.18.d_ref, ...), custom_call_target="tpu_custom_call" | custom-call | tf_op jit(solution)/shard_map/finish/pallas_call | solution.py:444
  (25 shorter events, 0.4 us)
Async XLA Ops:
  1.6 9.6 %collective-permute-start.2 = (bf16[8,4224]{1,0:T(8,128)(2,1)S(1)}, bf16[8,4224]{1,0:T(8,128)(2,1)S(1)}, u32[]{:S(2)}, u32[]{:S(2)}) collective-permute-start(bf16[8,4224]{1,0:T(8,128)(2,1)S(1)} %build_message.1), channel_id=1, source_target_pairs={{0,12},{1,19},{2,14},{3,17},{4,8},{5,23},{6,10},{7,21},{8,4},{9,27... | collective-permute-start | bytes 202760 | tf_op jit(solution)/shard_map/ppermute | solution.py:358
  6.7 5.2 %collective-permute-start.1 = (bf16[8,4224]{1,0:T(8,128)(2,1)S(1)}, bf16[8,4224]{1,0:T(8,128)(2,1)S(1)}, u32[]{:S(2)}, u32[]{:S(2)}) collective-permute-start(bf16[8,4224]{1,0:T(8,128)(2,1)S(1)} %build_message.1), channel_id=1, source_target_pairs={{0,8},{1,3},{2,10},{3,1},{4,12},{5,7},{6,14},{7,5},{8,0},{9,11},{1... | collective-permute-start | bytes 202760 | tf_op jit(solution)/shard_map/ppermute | solution.py:358
  6.7 5.2 %collective-permute-start = (bf16[8,4224]{1,0:T(8,128)(2,1)S(1)}, bf16[8,4224]{1,0:T(8,128)(2,1)S(1)}, u32[]{:S(2)}, u32[]{:S(2)}) collective-permute-start(bf16[8,4224]{1,0:T(8,128)(2,1)S(1)} %build_message.1), channel_id=1, source_target_pairs={{0,4},{1,17},{2,6},{3,19},{4,0},{5,21},{6,2},{7,23},{8,12},{9,25},... | collective-permute-start | bytes 202760 | tf_op jit(solution)/shard_map/ppermute | solution.py:358
  12.0 9.5 %collective-permute-start.4 = (bf16[32,4224]{1,0:T(8,128)(2,1)S(1)}, bf16[32,4224]{1,0:T(8,128)(2,1)S(1)}, u32[]{:S(2)}, u32[]{:S(2)}) collective-permute-start(bf16[32,4224]{1,0:T(8,128)(2,1)S(1)} %constant_dynamic-update-slice_fusion), channel_id=1, source_target_pairs={{0,2},{1,9},{2,0},{3,11},{4,6},{5,13},{6,4},{7,15},{8,10},{9,1},{1... | collective-permute-start | bytes 811016 | tf_op jit(solution)/shard_map/ppermute | solution.py:358
  13.5 8.5 %collective-permute-start.3 = (bf16[32,4224]{1,0:T(8,128)(2,1)S(1)}, bf16[32,4224]{1,0:T(8,128)(2,1)S(1)}, u32[]{:S(2)}, u32[]{:S(2)}) collective-permute-start(bf16[32,4224]{1,0:T(8,128)(2,1)S(1)} %constant_dynamic-update-slice_fusion), channel_id=1, source_target_pairs={{0,16},{1,5},{2,18},{3,7},{4,20},{5,1},{6,22},{7,3},{8,24},{9,13},... | collective-permute-start | bytes 811016 | tf_op jit(solution)/shard_map/ppermute | solution.py:358
  15.0 6.4 %collective-permute-start.9 = (bf16[32,2176]{1,0:T(8,128)(2,1)S(1)}, bf16[32,2176]{1,0:T(8,128)(2,1)S(1)}, u32[]{:S(2)}, u32[]{:S(2)}) collective-permute-start(bf16[32,2176]{1,0:T(8,128)(2,1)S(1)} %slice.91), channel_id=1, source_target_pairs={{0,18},{1,13},{2,16},{3,15},{4,22},{5,9},{6,20},{7,11},{8,26},{9,5... | collective-permute-start | bytes 417800 | tf_op jit(solution)/shard_map/ppermute | solution.py:358
  15.6 6.6 %collective-permute-start.6 = (bf16[32,4224]{1,0:T(8,128)(2,1)S(1)}, bf16[32,4224]{1,0:T(8,128)(2,1)S(1)}, u32[]{:S(2)}, u32[]{:S(2)}) collective-permute-start(bf16[32,4224]{1,0:T(8,128)(2,1)S(1)} %constant_dynamic-update-slice_fusion), channel_id=1, source_target_pairs={{0,1},{1,0},{2,3},{3,2},{4,5},{5,4},{6,7},{7,6},{8,9},{9,8},{10,11... | collective-permute-start | bytes 811016 | tf_op jit(solution)/shard_map/ppermute | solution.py:362
  15.7 8.1 %collective-permute-start.5 = (bf16[32,2048]{1,0:T(8,128)(2,1)S(1)}, bf16[32,2048]{1,0:T(8,128)(2,1)S(1)}, u32[]{:S(2)}, u32[]{:S(2)}) collective-permute-start(bf16[32,2048]{1,0:T(8,128)(2,1)S(1)} %slice.82), channel_id=1, source_target_pairs={{0,18},{1,13},{2,16},{3,15},{4,22},{5,9},{6,20},{7,11},{8,26},{9,5... | collective-permute-start | bytes 393224 | tf_op jit(solution)/shard_map/ppermute | solution.py:358
  21.4 2.3 %collective-permute-start.10 = (bf16[32,2176]{1,0:T(8,128)(2,1)S(1)}, bf16[32,2176]{1,0:T(8,128)(2,1)S(1)}, u32[]{:S(2)}, u32[]{:S(2)}) collective-permute-start(bf16[32,2176]{1,0:T(8,128)(2,1)S(1)} %collective-permute-done.9), channel_id=1, source_target_pairs={{0,1},{1,0},{2,3},{3,2},{4,5},{5,4},{6,7},{7,6},{8,9},{9,8},{10,11... | collective-permute-start | bytes 417800 | tf_op jit(solution)/shard_map/ppermute | solution.py:362
  21.5 1.7 %collective-permute-start.8 = (bf16[32,4224]{1,0:T(8,128)(2,1)S(1)}, bf16[32,4224]{1,0:T(8,128)(2,1)S(1)}, u32[]{:S(2)}, u32[]{:S(2)}) collective-permute-start(bf16[32,4224]{1,0:T(8,128)(2,1)S(1)} %collective-permute-done.4), channel_id=1, source_target_pairs={{0,1},{1,0},{2,3},{3,2},{4,5},{5,4},{6,7},{7,6},{8,9},{9,8},{10,11... | collective-permute-start | bytes 811016 | tf_op jit(solution)/shard_map/ppermute | solution.py:362
  22.0 1.6 %collective-permute-start.7 = (bf16[32,4224]{1,0:T(8,128)(2,1)S(1)}, bf16[32,4224]{1,0:T(8,128)(2,1)S(1)}, u32[]{:S(2)}, u32[]{:S(2)}) collective-permute-start(bf16[32,4224]{1,0:T(8,128)(2,1)S(1)} %collective-permute-done.3), channel_id=1, source_target_pairs={{0,1},{1,0},{2,3},{3,2},{4,5},{5,4},{6,7},{7,6},{8,9},{9,8},{10,11... | collective-permute-start | bytes 811016 | tf_op jit(solution)/shard_map/ppermute | solution.py:362
  23.7 0.7 %copy-start.1 = (s32[2,16]{1,0:T(2,128)S(1)}, s32[2,16]{1,0:T(2,128)}, u32[]{:S(2)}) copy-start(s32[2,16]{1,0:T(2,128)} %shard_ref.3) | copy-start | bytes 388
  23.8 3.8 %collective-permute-start.11 = (bf16[32,2048]{1,0:T(8,128)(2,1)S(1)}, bf16[32,2048]{1,0:T(8,128)(2,1)S(1)}, u32[]{:S(2)}, u32[]{:S(2)}) collective-permute-start(bf16[32,2048]{1,0:T(8,128)(2,1)S(1)} %collective-permute-done.5), channel_id=1, source_target_pairs={{0,1},{1,0},{2,3},{3,2},{4,5},{5,4},{6,7},{7,6},{8,9},{9,8},{10,11... | collective-permute-start | bytes 393224 | tf_op jit(solution)/shard_map/ppermute | solution.py:362
  31.7 2.0 %collective-permute-start.12 = (bf16[128,2176]{1,0:T(8,128)(2,1)S(1)}, bf16[128,2176]{1,0:T(8,128)(2,1)S(1)}, u32[]{:S(2)}, u32[]{:S(2)}) collective-permute-start(bf16[128,2176]{1,0:T(8,128)(2,1)S(1)} %get-tuple-element.60), channel_id=1, source_target_pairs={{0,1},{1,0},{2,3},{3,2},{4,5},{5,4},{6,7},{7,6},{8,9},{9,8},{10,11... | collective-permute-start | bytes 1671176 | tf_op jit(solution)/shard_map/ppermute | solution.py:362
  33.9 6.7 %collective-permute-start.15 = (bf16[32,2176]{1,0:T(8,128)(2,1)S(1)}, bf16[32,2176]{1,0:T(8,128)(2,1)S(1)}, u32[]{:S(2)}, u32[]{:S(2)}) collective-permute-start(bf16[32,2176]{1,0:T(8,128)(2,1)S(1)} %get-tuple-element.81), channel_id=1, source_target_pairs={{0,18},{1,13},{2,16},{3,15},{4,22},{5,9},{6,20},{7,11},{8,26},{9,5... | collective-permute-start | bytes 417800 | tf_op jit(solution)/shard_map/ppermute | solution.py:358
  36.4 5.1 %collective-permute-start.14 = (bf16[32,2176]{1,0:T(8,128)(2,1)S(1)}, bf16[32,2176]{1,0:T(8,128)(2,1)S(1)}, u32[]{:S(2)}, u32[]{:S(2)}) collective-permute-start(bf16[32,2176]{1,0:T(8,128)(2,1)S(1)} %get-tuple-element.82), channel_id=1, source_target_pairs={{0,2},{1,9},{2,0},{3,11},{4,6},{5,13},{6,4},{7,15},{8,10},{9,1},{1... | collective-permute-start | bytes 417800 | tf_op jit(solution)/shard_map/ppermute | solution.py:358
  36.9 5.1 %collective-permute-start.13 = (bf16[32,2176]{1,0:T(8,128)(2,1)S(1)}, bf16[32,2176]{1,0:T(8,128)(2,1)S(1)}, u32[]{:S(2)}, u32[]{:S(2)}) collective-permute-start(bf16[32,2176]{1,0:T(8,128)(2,1)S(1)} %get-tuple-element.83), channel_id=1, source_target_pairs={{0,16},{1,5},{2,18},{3,7},{4,20},{5,1},{6,22},{7,3},{8,24},{9,13},... | collective-permute-start | bytes 417800 | tf_op jit(solution)/shard_map/ppermute | solution.py:358
  42.1 6.8 %collective-permute-start.18 = (bf16[8,2176]{1,0:T(8,128)(2,1)S(1)}, bf16[8,2176]{1,0:T(8,128)(2,1)S(1)}, u32[]{:S(2)}, u32[]{:S(2)}) collective-permute-start(bf16[8,2176]{1,0:T(8,128)(2,1)S(1)} %get-tuple-element.85), channel_id=1, source_target_pairs={{0,12},{1,19},{2,14},{3,17},{4,8},{5,23},{6,10},{7,21},{8,4},{9,27... | collective-permute-start | bytes 104456 | tf_op jit(solution)/shard_map/ppermute | solution.py:358
  45.2 4.9 %collective-permute-start.17 = (bf16[8,2176]{1,0:T(8,128)(2,1)S(1)}, bf16[8,2176]{1,0:T(8,128)(2,1)S(1)}, u32[]{:S(2)}, u32[]{:S(2)}) collective-permute-start(bf16[8,2176]{1,0:T(8,128)(2,1)S(1)} %get-tuple-element.86), channel_id=1, source_target_pairs={{0,8},{1,3},{2,10},{3,1},{4,12},{5,7},{6,14},{7,5},{8,0},{9,11},{1... | collective-permute-start | bytes 104456 | tf_op jit(solution)/shard_map/ppermute | solution.py:358
  46.2 4.2 %collective-permute-start.16 = (bf16[8,2176]{1,0:T(8,128)(2,1)S(1)}, bf16[8,2176]{1,0:T(8,128)(2,1)S(1)}, u32[]{:S(2)}, u32[]{:S(2)}) collective-permute-start(bf16[8,2176]{1,0:T(8,128)(2,1)S(1)} %get-tuple-element.87), channel_id=1, source_target_pairs={{0,4},{1,17},{2,6},{3,19},{4,0},{5,21},{6,2},{7,23},{8,12},{9,25},... | collective-permute-start | bytes 104456 | tf_op jit(solution)/shard_map/ppermute | solution.py:358
  46.7 3.7 %copy-start = (s32[1,8,8]{2,1,0:T(8,128)S(1)}, s32[1,8,8]{2,1,0:T(8,128)}, u32[]{:S(2)}) copy-start(s32[1,8,8]{2,1,0:T(8,128)} %param.11) | copy-start | bytes 772
